TPU v7x, 256 devices: a whole 4x4x8 slice. The times are simulated.
256 devices in a mesh: docs: 8 (over x, core), seq: 32 (over z, y).
Axes of the slice: x: 4, y: 4, z: 8, core: 2. Of those that a mesh axis runs over, the one named last changes fastest.
Arguments:
- byte_input: bfloat16 [81920, 256], P(('docs', 'seq')), parts along dimension 0, may hold values from -6 to 6
- w_short: bfloat16 [1024, 1024], replicated, may hold values from -0.1875 to 0.1875
- w_attend: bfloat16 [1024, 3072], replicated, may hold values from -0.1875 to 0.1875
- w_expand: bfloat16 [1024, 1024], replicated, may hold values from -0.75 to 0.75
- out_grad: bfloat16 [81920, 256], P(('docs', 'seq')), parts along dimension 0, may hold values from -6 to 6
Outputs:
- byte_output: bfloat16 [81920, 256], P(('docs', 'seq')), parts along dimension 0
- input_grad: bfloat16 [81920, 256], P(('docs', 'seq')), parts along dimension 0
- grad_short: float32 [8192, 1024], P(('docs', 'seq')), parts along dimension 0
- grad_attend: float32 [8192, 3072], P(('docs', 'seq')), parts along dimension 0
- grad_expand: float32 [8192, 1024], P(('docs', 'seq')), parts along dimension 0
There are 8 independent parts, one for each index of `docs`. A program takes and returns all parts, laid end to end along the dimension named above; an argument that names none is the same for every part. Nothing has to cross between parts.
All inputs are finite; a program needn't handle non-finite values.
Results may differ from a plain program's by a relative error of at most 0.028.
Values may be sent and summed in bfloat16 or wider, within the bound.
No kernel may reach another device: no remote copies, remote signals or barrier semaphores. Data moves between devices by JAX's collectives and lax.ppermute only.
A program may use at most 128 MiB of HBM per device.

v0:
```python
import jax
import jax.numpy as jnp
from jax import lax
from jax.sharding import PartitionSpec as P

HEADS = 8


SCORE_BOUND = 16.0
EPSILON = 1e-06


def from_behind(value, axis, steps):
    count = lax.axis_size(axis)
    leading, last = (max(0, -steps), min(count, count - steps))
    return lax.ppermute(value, axis, [(source, source + steps) for source in range(leading, last)])


def rounded(value):
    return lax.optimization_barrier(value.astype(jnp.bfloat16))


def unit_heads(matrix):
    split = matrix.reshape(matrix.shape[0], HEADS, -1)
    scale = lax.rsqrt(jnp.mean(split * split, axis=2, keepdims=True) + EPSILON)
    return (split * scale, scale)


def norm_back(normed, scale, upstream):
    inner = jnp.mean(normed * upstream, axis=2, keepdims=True)
    return scale * (upstream - normed * inner)


def powers_of(query3, key3, query_pos, key_pos, factor):
    dots = jnp.einsum("thd,rhd->htr", query3, key3, preferred_element_type=jnp.float32)
    live = query_pos[:, None] >= key_pos[None, :]
    return jnp.where(live[None], jnp.exp(dots * factor), 0.0)


def local(byte_input, w_short, w_attend, w_expand, out_grad):
    shard_count = lax.axis_size("seq")
    own_index = lax.axis_index("seq")
    short_rows = byte_input.shape[0] // 4
    byte_width = byte_input.shape[1]
    attn_width = w_attend.shape[1] // 3
    head_size = attn_width // HEADS
    factor = SCORE_BOUND / head_size
    first_pos = own_index * short_rows
    query_pos = first_pos + jnp.arange(short_rows, dtype=jnp.int32)
    group_shards = min(8, shard_count)
    group_rows = group_shards * short_rows
    turns = own_index // group_shards + 1
    edge = from_behind(byte_input[-3:], "seq", 1)
    grouped = jnp.concatenate([edge, byte_input[:-3]], axis=0).reshape(short_rows, 4 * byte_width)
    hidden = jnp.dot(grouped, w_short, preferred_element_type=jnp.float32)
    hidden_scale = lax.rsqrt(jnp.mean(hidden * hidden, axis=1, keepdims=True) + EPSILON)
    normed = hidden * hidden_scale
    normed_b = normed.astype(jnp.bfloat16)
    projected = jnp.dot(normed_b, w_attend, preferred_element_type=jnp.float32)
    query_unit, query_scale = unit_heads(projected[:, :attn_width])
    key_unit, key_scale = unit_heads(projected[:, attn_width : 2 * attn_width])
    query3 = query_unit.astype(jnp.bfloat16)
    key_own = key_unit.astype(jnp.bfloat16).reshape(short_rows, attn_width)
    value_own = projected[:, 2 * attn_width :].astype(jnp.bfloat16)
    pair = jnp.concatenate([key_own, value_own], axis=1)

    def unpack(block):
        rows = block.shape[0]
        keys3 = block[:, :attn_width].reshape(rows, HEADS, head_size)
        values3 = block[:, attn_width:].reshape(rows, HEADS, head_size)
        return (keys3, values3)

    def absorb(totals, block, key_first):
        weighted, denom = totals
        keys3, values3 = unpack(block)
        key_pos = key_first + jnp.arange(block.shape[0], dtype=jnp.int32)
        powers = powers_of(query3, keys3, query_pos, key_pos, factor)
        weighted = weighted + jnp.einsum(
            "htr,rhd->thd", powers.astype(jnp.bfloat16), values3, preferred_element_type=jnp.float32
        )
        denom = denom + jnp.sum(powers, axis=2).T
        return (weighted, denom)

    zero_query = jnp.zeros((short_rows, HEADS, head_size), jnp.float32)
    zero_denom = jnp.zeros((short_rows, HEADS), jnp.float32)
    keep = lax.all_gather(pair, "seq", axis=0, tiled=True)

    def forward_step(block_no, totals):
        key_first = block_no * group_rows
        return absorb(totals, lax.dynamic_slice_in_dim(keep, key_first, group_rows, 0), key_first)

    weighted, denom = lax.fori_loop(0, turns, forward_step, (zero_query, zero_denom))
    attended = rounded((weighted / denom[:, :, None]).reshape(short_rows, attn_width))
    expanded = jnp.dot(attended, w_expand, preferred_element_type=jnp.float32)
    byte_output = (
        byte_input.astype(jnp.float32) + expanded.reshape(4 * short_rows, byte_width)
    ).astype(jnp.bfloat16)
    d_expand = out_grad.reshape(short_rows, 4 * byte_width)
    d_attended = rounded(jnp.dot(d_expand, w_expand.T, preferred_element_type=jnp.float32))
    d_attended = d_attended.astype(jnp.float32).reshape(short_rows, HEADS, head_size)
    inverse = 1.0 / denom
    grad3 = (d_attended * inverse[:, :, None]).astype(jnp.bfloat16)
    attended_f = attended.astype(jnp.float32).reshape(short_rows, HEADS, head_size)
    shifts = (jnp.sum(d_attended * attended_f, axis=2) * inverse).astype(jnp.bfloat16)
    shifts_cols = shifts.astype(jnp.float32).T[:, :, None]

    def score_grads(keys3, values3, key_first):
        key_pos = key_first + jnp.arange(keys3.shape[0], dtype=jnp.int32)
        powers = powers_of(query3, keys3, query_pos, key_pos, factor)
        grad_dot = jnp.einsum("thd,rhd->htr", grad3, values3, preferred_element_type=jnp.float32)
        d_score = (powers * (grad_dot - shifts_cols) * factor).astype(jnp.bfloat16)
        return (powers, d_score)

    def backward_step(block_no, totals):
        query_grad, term = totals
        key_first = block_no * group_rows
        keys3, values3 = unpack(lax.dynamic_slice_in_dim(keep, key_first, group_rows, 0))
        powers, d_score = score_grads(keys3, values3, key_first)
        query_grad = query_grad + jnp.einsum(
            "htr,rhd->thd", d_score, keys3, preferred_element_type=jnp.float32
        )
        key_part = jnp.einsum(
            "htr,thd->rhd", d_score, query3, preferred_element_type=jnp.float32
        ).reshape(group_rows, attn_width)
        value_part = jnp.einsum(
            "htr,thd->rhd", powers.astype(jnp.bfloat16), grad3, preferred_element_type=jnp.float32
        ).reshape(group_rows, attn_width)
        term = lax.dynamic_update_slice_in_dim(
            term, jnp.concatenate([key_part, value_part], axis=1), key_first, 0
        )
        return (query_grad, term)

    empty_term = jnp.zeros((shard_count * short_rows, 2 * attn_width), jnp.float32)
    query_grad, term = lax.fori_loop(0, turns, backward_step, (zero_query, empty_term))
    key_values = lax.psum_scatter(
        term.astype(jnp.bfloat16), "seq", scatter_dimension=0, tiled=True
    ).astype(jnp.float32)
    key_grad = key_values[:, :attn_width].reshape(short_rows, HEADS, head_size)
    value_grad = key_values[:, attn_width:].reshape(short_rows, HEADS, head_size)
    d_query = norm_back(query_unit, query_scale, query_grad).reshape(short_rows, attn_width)
    d_key = norm_back(key_unit, key_scale, key_grad).reshape(short_rows, attn_width)
    d_projected = jnp.concatenate(
        [d_query, d_key, value_grad.reshape(short_rows, attn_width)], axis=1
    ).astype(jnp.bfloat16)
    d_normed = jnp.dot(d_projected, w_attend.T, preferred_element_type=jnp.float32)
    d_hidden = (
        hidden_scale * (d_normed - normed * jnp.mean(normed * d_normed, axis=1, keepdims=True))
    ).astype(jnp.bfloat16)
    d_grouped = (
        jnp.dot(d_hidden, w_short.T, preferred_element_type=jnp.float32)
        .astype(jnp.bfloat16)
        .reshape(4 * short_rows, byte_width)
    )
    back_edge = from_behind(d_grouped[:3], "seq", -1)
    moved = jnp.concatenate([d_grouped[3:], back_edge], axis=0).astype(jnp.float32)
    input_grad = (out_grad.astype(jnp.float32) + moved).astype(jnp.bfloat16)

    def part(left, right):
        return jnp.dot(left.T, right, preferred_element_type=jnp.float32)

    grads = lax.psum_scatter(
        jnp.concatenate(
            [part(grouped, d_hidden), part(normed_b, d_projected), part(attended, d_expand)], axis=1
        ).astype(jnp.bfloat16),
        "seq",
        scatter_dimension=0,
        tiled=True,
    ).astype(jnp.float32)
    model_width = w_short.shape[1]
    grad_short = grads[:, :model_width]
    grad_attend = grads[:, model_width : model_width + 3 * attn_width]
    grad_expand = grads[:, model_width + 3 * attn_width :]
    return (byte_output, input_grad, grad_short, grad_attend, grad_expand)


def solution(mesh):
    in_specs = (P(("docs", "seq"), None), P(), P(), P(), P(("docs", "seq"), None))
    out_specs = (
        P(("docs", "seq"), None),
        P(("docs", "seq"), None),
        P(("docs", "seq"), None),
        P(("docs", "seq"), None),
        P(("docs", "seq"), None),
    )
    return jax.shard_map(local, mesh=mesh, in_specs=in_specs, out_specs=out_specs, check_vma=False)
```

profile of v0, /device:TPU:6, one launch (start us, length us, event | category | flops | bytes accessed | tf_op | source)
XLA Modules:
  0.0 731.3 jit_solution(5632253812423761780)
XLA Ops:
  7.2 0.8 slice.53
  8.1 3.5 collective-permute-start
  11.5 1.3 collective-permute-done
  12.8 1.0 pad_maximum_fusion.6
  13.9 0.6 multiply_reduce_fusion.6
  14.5 4.1 fusion.21
  18.6 0.7 slice.94
  19.3 0.3 copy-done.1
  19.7 0.7 copy-done.4
  20.4 0.2 multiply_reduce_fusion.5
  20.7 0.1 mul.135
  20.9 0.7 copy-done.2
  21.6 1.2 slice_bitcast_fusion.1
  22.8 0.7 pad_maximum_fusion.3
  23.7 1.0 reshape.175
  24.7 2.4 convolution_convert_fusion.4
  27.1 0.8 convert_bitcast_fusion.1
  27.9 0.8 copy.114
  28.7 0.2 multiply_reduce_fusion.4
  29.0 0.2 fusion.15
  29.1 108.0 %all-gather.2.cloned.1.call-done = bf16[2560,2048]{1,0:T(8,128)(2,1)} async-done(((bf16[80,2048]{1,0:T(8,128)(2,1)}), bf16[2560,2048]{1,0:T(8,128)(2,1)}) %all-gather.2.cloned.1.call-update) | async-done | bytes 10485776 | tf_op jit(solution)/shard_map/all_gather | solution.py:86
  137.1 13.8 %copy.81 = bf16[2560,2048]{0,1:T(8,128)(2,1)} copy(bf16[2560,2048]{1,0:T(8,128)(2,1)} %all-gather.2.cloned.1.call-done) | data formatting | bytes 20971520
  151.0 3.4 while.26
  151.0 2.0 constant_dynamic-slice_fusion.3
  153.1 0.6 fusion.81
  153.7 0.7 fusion.82
  154.4 0.2 copy_bitcast_fusion.1
  154.7 1.2 multiply_reduce_fusion.3
  156.0 0.2 fusion.13
  156.2 5.2 broadcast_in_dim.51.clone
  161.3 14.7 %while.27 = (s32[]{:T(128)}, f32[80,8,128]{2,0,1:T(8,128)S(1)}, bf16[2560,2048]{1,0:T(8,128)(2,1)}, s32[]{:T(128)}, bf16[2560,2048]{0,1:T(8,128)(2,1)}, /*index=...) while((s32[]{:T(128)}, f32[80,8,128]{2,0,1:T(8,128)S(1)}, ...), condition=%wide.region_8.9_spmd.clone, body=%wide.region_7.8_spmd.clone.sunk | while | flops 532531936 | bytes 36319576 | solution.py:134
  161.3 1.9 fusion.93
  163.4 0.5 bitcast_select_fusion.3
  163.9 0.4 fusion.94
  164.3 0.7 fusion.95
  165.0 0.6 fusion.96
  165.6 0.6 fusion.97
  166.1 1.8 pad_maximum_fusion.8
  167.9 4.5 copy.135
  172.4 3.6 constant_dynamic-update-slice_fusion.2
  176.1 0.2 reduce-scatter.5.cloned.1.call-start
  176.3 0.3 multiply_reduce_fusion.2
  176.7 0.9 copy_bitcast_fusion
  177.6 3.1 convolution_convert_fusion.1
  180.7 280.0 %reduce-scatter.3.cloned.1.call-done = bf16[80,2048]{1,0:T(8,128)(2,1)} async-done(((bf16[2560,2048]{1,0:T(8,128)(2,1)}), bf16[80,2048]{1,0:T(8,128)(2,1)}) %reduce-scatter.3.cloned.1.call-update) | async-done | bytes 327696 | tf_op jit(solution)/shard_map/reduce_scatter | solution.py:135
  460.7 1.0 convert_bitcast_fusion.2
  461.8 0.3 multiply_reduce_fusion.1
  462.2 0.1 mul.152
  462.4 1.2 fusion.12
  463.6 4.9 multiply_reduce_fusion
  468.5 4.5 convolution_convert_fusion
  473.1 2.1 convolution_convert_fusion.2
  475.2 3.9 copy.91
  479.1 9.7 %pad_maximum_fusion.1 = bf16[1024,5120]{1,0:T(8,128)(2,1)} fusion(bf16[1024,1024]{1,0:T(8,128)(2,1)} %convolution_convert_fusion.1, bf16[1024,3072]{1,0:T(8,128)(2,1)} %convolution_convert_fusion, bf16[1024,1024]{1,0:T(8,128)(2,1)} %copy.91), kind=kLoop, calls=%fused_computation.25 | loop fusion | flops 31457280 | bytes 20971520 | tf_op jit(solution)/shard_map/concatenate | solution.py:162
  488.9 0.9 copy-done.7
  489.8 2.1 fusion.26
  492.0 0.8 convolution_convert_fusion.3
  492.9 1.3 collective-permute-start.1
  494.2 0.7 add_convert_fusion.1
  495.0 3.4 collective-permute-done.1
  498.4 0.7 add_convert_fusion
  499.1 222.4 %reduce-scatter.5.cloned.1.call-done = bf16[32,5120]{1,0:T(8,128)(2,1)} async-done(((bf16[1024,5120]{1,0:T(8,128)(2,1)}), bf16[32,5120]{1,0:T(8,128)(2,1)}) %reduce-scatter.5.cloned.1.call-update) | async-done | bytes 327696 | tf_op jit(solution)/shard_map/reduce_scatter | solution.py:161
  721.5 1.6 fusion.24
  723.1 1.7 slice.78
  (68 shorter events, 1.7 us)
Async XLA Ops:
  7.2 6.7 copy-start
  7.2 130.0 %all-gather.2.cloned.1.call-start = ((), (), s32[]{:S(2)}) async-start(), calls=%async_computation.2 | async-start | bytes 10813440 | tf_op jit(solution)/shard_map/all_gather | solution.py:86
  8.1 4.8 collective-permute-start
  13.9 4.7 copy-start.8
  18.6 1.0 copy-start.1
  19.6 3.2 copy-start.14
  19.7 0.7 copy-start.4
  20.9 0.7 copy-start.2
  23.6 437.1 %reduce-scatter.3.cloned.1.call-start = ((), (), s32[]{:S(2)}) async-start(), calls=%async_computation.3 | async-start | bytes 10813440 | tf_op jit(solution)/shard_map/reduce_scatter | solution.py:135
  24.7 4.0 copy-start.10
  154.6 1.4 copy-start.6
  154.6 1.4 copy-start.12
  176.1 545.5 %reduce-scatter.5.cloned.1.call-start = ((), (), s32[]{:S(2)}) async-start(), calls=%async_computation.4 | async-start | bytes 10813440 | tf_op jit(solution)/shard_map/reduce_scatter | solution.py:161
  177.6 284.2 %copy-start.5 = (f32[10,8,8,128]{3,2,1,0:T(8,128)S(1)}, f32[10,8,8,128]{3,2,1,0:T(8,128)}, u32[]{:S(2)}) copy-start(f32[10,8,8,128]{3,2,1,0:T(8,128)} %copy-done.4) | copy-start | bytes 983044
  177.6 284.8 %copy-start.3 = (f32[80,8,128]{2,1,0:T(8,128)S(1)}, f32[80,8,128]{2,1,0:T(8,128)}, u32[]{:S(2)}) copy-start(f32[80,8,128]{2,1,0:T(8,128)} %copy-done.2) | copy-start | bytes 983044
  180.7 282.9 %copy-start.11 = (bf16[80,1024]{1,0:T(8,128)(2,1)S(1)}, bf16[80,1024]{1,0:T(8,128)(2,1)}, u32[]{:S(2)}) copy-start(bf16[80,1024]{1,0:T(8,128)(2,1)} %copy_bitcast_fusion) | copy-start | bytes 491524
  468.5 4.7 copy-start.9
  488.9 0.9 copy-start.7
  491.9 2.3 copy-start.13
  491.9 6.5 copy-start.15
  492.9 5.5 collective-permute-start.1
Sparse Core Ops, SparseCore 0:
  23.7 113.3 all-gather.1
  176.2 284.4 reduce-scatter.2
  489.0 232.4 reduce-scatter.4
where the time goes:
time: 733 us; the launch traced here: 731 us
  waiting for transfers between devices  615 us (84%)
  local copies, waits for them, and re-layouts  45.6 us (6%)
  matrix products  28.5 us (4%)
  other arithmetic  22.7 us (3%)
  between operations  14.2 us (2%)
    reduce_scatter x1, waiting for transfers between devices, local(): lax.psum_scatter(term.astype(jnp.bfloat16), 'seq', scatter_dimension=0, t...  280 us
    reduce_scatter x1, waiting for transfers between devices, local(): lax.psum_scatter(jnp.concatenate([part(grouped, d_hidden), part(normed_b,...  222 us
    all_gather x1, waiting for transfers between devices, local(): keep = lax.all_gather(pair, 'seq', axis=0, tiled=True)  108 us
    unnamed x39, local copies, waits for them, and re-layouts  17.5 us
  transfers between devices with their start and end apart: 5, of which 5 were waited for; matrix products, arithmetic and copies ran while one was open for 2% of the time, Pallas kernels for 0%

commit v1 on v0

v1 whole, which is shorter than its diff:
```python
import functools

import jax
import jax.numpy as jnp
from jax import lax
from jax.experimental import pallas as pl
from jax.experimental.pallas import tpu as pltpu
from jax.sharding import Mesh, PartitionSpec as P

HEADS = 8


SCORE_BOUND = 16.0
EPSILON = 1e-06

NT = (((1,), (1,)), ((), ()))
TN = (((0,), (0,)), ((), ()))


def mm(left, right, dims=(((1,), (0,)), ((), ()))):
    return lax.dot_general(left, right, dims, preferred_element_type=jnp.float32)


def unit(matrix):
    scale = lax.rsqrt(jnp.mean(matrix * matrix, axis=1, keepdims=True) + EPSILON)
    return (matrix * scale, scale)


def norm_back(normed, scale, upstream):
    inner = jnp.mean(normed * upstream, axis=1, keepdims=True)
    return scale * (upstream - normed * inner)


def chunks_of(rows, block, width=256):
    found = []
    for first in range(0, rows, width):
        found.append((first, min(width, rows - first), first // block * block))
    return found


def attention_body(block, shards, y_ref, qd_ref, *refs):
    kv_refs = refs[:shards]
    att_ref, dq_ref, own_ref = refs[shards : shards + 3]
    sent_refs = refs[shards + 3 : 2 * shards + 2]
    p_ref, kb_ref, acc_ref, dq_acc = refs[2 * shards + 2 :]
    rows, head_size = att_ref.shape
    factor = SCORE_BOUND / head_size
    chunks = chunks_of(rows, block)
    y = y_ref[0]
    query_unit, query_scale = unit(qd_ref[:, :head_size].astype(jnp.float32))
    qb = query_unit.astype(jnp.bfloat16)
    qpos = lax.broadcasted_iota(jnp.int32, (rows, 1), 0)
    start = jnp.zeros((rows, 1), jnp.int32)
    for edge in range(block, rows, block):
        start = start + jnp.where(qpos >= edge, block, 0)
    denom = jnp.zeros((rows, 1), jnp.float32)
    acc_ref[...] = jnp.zeros_like(acc_ref)
    for turn in range(shards):
        key_unit, _ = unit(kv_refs[turn][:, :head_size].astype(jnp.float32))
        kb_ref[turn] = key_unit.astype(jnp.bfloat16)
        limit = qpos + 1 if turn == 0 else start + jnp.where(y >= turn, block, 0)
        for number, (first, width, row) in enumerate(chunks):
            dots = mm(qb[row:], kb_ref[turn, first : first + width], NT)
            key_pos = first + lax.broadcasted_iota(jnp.int32, (rows - row, width), 1)
            powers = jnp.where(key_pos < limit[row:], jnp.exp(dots * factor), 0.0)
            p_ref[turn, number, row:, :width] = powers
            part = jnp.sum(powers, axis=1, keepdims=True)
            denom = denom + (part if row == 0 else jnp.concatenate([jnp.zeros((row, 1), jnp.float32), part], axis=0))
            acc_ref[row:] += mm(powers.astype(jnp.bfloat16), kv_refs[turn][first : first + width, head_size:])
    inverse = 1.0 / denom
    attended = (acc_ref[...] * inverse).astype(jnp.bfloat16)
    att_ref[...] = attended
    d_attended = qd_ref[:, head_size:].astype(jnp.float32)
    grad = (d_attended * inverse).astype(jnp.bfloat16)
    shift = jnp.sum(d_attended * attended.astype(jnp.float32), axis=1, keepdims=True) * inverse
    shift = shift.astype(jnp.bfloat16).astype(jnp.float32)
    dq_acc[...] = jnp.zeros_like(dq_acc)
    for turn in range(shards):
        out = own_ref if turn == 0 else sent_refs[turn - 1]
        for number, (first, width, row) in enumerate(chunks):
            powers = p_ref[turn, number, row:, :width]
            grad_dot = mm(grad[row:], kv_refs[turn][first : first + width, head_size:], NT)
            d_score = (powers * (grad_dot - shift[row:]) * factor).astype(jnp.bfloat16)
            dq_acc[row:] += mm(d_score, kb_ref[turn, first : first + width])
            out[first : first + width, :head_size] = mm(d_score, qb[row:], TN).astype(out.dtype)
            out[first : first + width, head_size:] = mm(powers.astype(jnp.bfloat16), grad[row:], TN).astype(out.dtype)
    dq_ref[...] = norm_back(query_unit, query_scale, dq_acc[...]).astype(jnp.bfloat16)


def attention(y, qd, kvs, block):
    rows, width = qd.shape
    head_size = width // 2
    shards = len(kvs)
    vmem = pl.BlockSpec(memory_space=pltpu.VMEM)
    shape = jax.ShapeDtypeStruct
    outs = [shape((rows, head_size), jnp.bfloat16)] * 2
    outs += [shape((rows, width), jnp.float32)] + [shape((rows, width), jnp.bfloat16)] * (shards - 1)
    return pl.pallas_call(
        functools.partial(attention_body, block, shards),
        out_shape=outs,
        in_specs=[pl.BlockSpec(memory_space=pltpu.SMEM)] + [vmem] * (shards + 1),
        out_specs=[vmem] * len(outs),
        scratch_shapes=[
            pltpu.VMEM((shards, len(chunks_of(rows, block)), rows, 256), jnp.float32),
            pltpu.VMEM((shards, rows, head_size), jnp.bfloat16),
            pltpu.VMEM((rows, head_size), jnp.float32),
            pltpu.VMEM((rows, head_size), jnp.float32),
        ],
        compiler_params=pltpu.CompilerParams(vmem_limit_bytes=40 * 1024 * 1024),
        name="attention",
    )(y, qd, *kvs)


def local(byte_input, w_short, w_attend, w_expand, out_grad):
    z_size, y_size = lax.axis_size("z"), lax.axis_size("y")
    count = z_size * y_size
    short_rows = byte_input.shape[0] // 4
    byte_width = byte_input.shape[1]
    attn_width = w_attend.shape[1] // 3
    model_width = w_short.shape[1]
    head_size = attn_width // HEADS
    both = ("z", "y")
    rows = z_size * short_rows

    def turn_y(value, steps):
        return lax.ppermute(value, "y", [(i, (i + steps) % y_size) for i in range(y_size)])

    def heads_of(*parts):
        stacked = jnp.stack([part.reshape(short_rows, HEADS, head_size) for part in parts], axis=2)
        return stacked.transpose(1, 0, 2, 3).reshape(HEADS, short_rows, len(parts) * head_size)

    def swap(value):
        return lax.all_to_all(value, "z", 0, 0)

    def back(value):
        parts = value.shape[2] // head_size
        split = value.reshape(HEADS, short_rows, parts, head_size).transpose(1, 2, 0, 3)
        return split.reshape(short_rows, parts, attn_width)

    d_expand = out_grad.reshape(short_rows, 4 * byte_width)
    d_expand_all = lax.all_gather(d_expand, "z", axis=0, tiled=True)
    edge = lax.ppermute(byte_input[-3:], both, [(i, i + 1) for i in range(count - 1)])
    d_attended = mm(d_expand, w_expand, NT).astype(jnp.bfloat16)
    grouped = jnp.concatenate([edge, byte_input[:-3]], axis=0).reshape(short_rows, 4 * byte_width)
    hidden = mm(grouped, w_short)
    normed, hidden_scale = unit(hidden)
    normed_b = normed.astype(jnp.bfloat16)
    projected = mm(normed_b, w_attend).astype(jnp.bfloat16)
    inputs_all = lax.all_gather(jnp.concatenate([grouped, normed_b], axis=1), "z", axis=0, tiled=True)
    query = projected[:, :attn_width]
    key = projected[:, attn_width : 2 * attn_width]
    value = projected[:, 2 * attn_width :]
    kv = swap(heads_of(key, value)).reshape(rows, 2 * head_size)
    kvs = [kv] + [turn_y(kv, step) for step in range(1, y_size)]
    qd = swap(heads_of(query, d_attended)).reshape(rows, 2 * head_size)
    y = lax.axis_index("y").astype(jnp.int32).reshape(1)
    attended, d_query, own, *sent = attention(y, qd, kvs, short_rows)

    grad_expand = lax.psum_scatter(
        mm(attended, d_expand_all, TN).astype(jnp.bfloat16), "y", scatter_dimension=0, tiled=True
    ).astype(jnp.float32)
    total = own
    for step in range(1, y_size):
        total = total + turn_y(sent[step - 1], -step).astype(jnp.float32)
    first_back = jnp.concatenate([attended, d_query], axis=1).reshape(HEADS, short_rows, 2 * head_size)
    first_back = back(swap(first_back))
    attended_own = first_back[:, 0]
    key_unit, key_scale = unit(kv[:, :head_size].astype(jnp.float32))
    d_kv = jnp.concatenate(
        [norm_back(key_unit, key_scale, total[:, :head_size]), total[:, head_size:]], axis=1
    ).astype(jnp.bfloat16)
    second_back = back(swap(d_kv.reshape(HEADS, short_rows, 2 * head_size)))
    d_projected = jnp.concatenate([first_back[:, 1], second_back[:, 0], second_back[:, 1]], axis=1)

    expanded = mm(attended_own, w_expand)
    byte_output = (
        byte_input.astype(jnp.float32) + expanded.reshape(4 * short_rows, byte_width)
    ).astype(jnp.bfloat16)

    d_normed = mm(d_projected, w_attend, NT)
    d_hidden = norm_back(normed, hidden_scale, d_normed).astype(jnp.bfloat16)
    d_hidden_cols = d_hidden.reshape(short_rows, z_size, model_width // z_size).transpose(1, 0, 2)
    d_hidden_cols = swap(d_hidden_cols).reshape(rows, model_width // z_size)
    d_grouped = mm(d_hidden, w_short, NT).astype(jnp.bfloat16).reshape(4 * short_rows, byte_width)
    back_edge = lax.ppermute(d_grouped[:3], both, [(i + 1, i) for i in range(count - 1)])
    moved = jnp.concatenate([d_grouped[3:], back_edge], axis=0).astype(jnp.float32)
    input_grad = (out_grad.astype(jnp.float32) + moved).astype(jnp.bfloat16)

    d_head = jnp.concatenate([d_query, d_kv], axis=1)
    part_attend = mm(inputs_all[:, model_width:], d_head, TN)
    part_short = mm(inputs_all[:, :model_width], d_hidden_cols, TN)
    parts = jnp.concatenate([part_attend, part_short], axis=1).astype(jnp.bfloat16)
    own_rows = model_width // count
    parts = lax.all_to_all(parts.reshape(count, own_rows, parts.shape[1]), both, 0, 0)
    parts = jnp.sum(parts.reshape(z_size, y_size, own_rows, 4, head_size).astype(jnp.float32), axis=1)
    parts = parts.transpose(1, 2, 0, 3).reshape(own_rows, 4 * attn_width)
    grad_attend = parts[:, : 3 * attn_width]
    grad_short = parts[:, 3 * attn_width :]
    return (byte_output, input_grad, grad_short, grad_attend, grad_expand)


def solution(mesh):
    docs, seq = mesh.devices.shape
    fine = Mesh(mesh.devices.reshape(docs, HEADS, seq // HEADS), ("docs", "z", "y"))
    split = P(("docs", "z", "y"), None)
    return jax.shard_map(
        local, mesh=fine, in_specs=(split, P(), P(), P(), split), out_specs=(split,) * 5, check_vma=False
    )
```

time: 733 us -> 201 us (0.27)
  waiting for transfers between devices: 615 us -> 73 us
  starting transfers between devices: 5.06 us -> 46.4 us
  local copies, waits for them, and re-layouts: 45.6 us -> 21 us
  other arithmetic: 22.7 us -> 13.7 us
  Pallas kernels: 0 us -> 8.18 us
    reduce_scatter x2 -> x1, waiting for transfers between devices: 502 us -> 15.5 us  [local(): lax.psum_scatter(mm(attended, d_expand_all, TN).astype(jnp.bfloat16), 'y'...]
    all_gather x1 -> x2, waiting for transfers between devices: 108 us -> 0.02 us  [the longest x1 0.02 us: local(): lax.all_gather(jnp.concatenate([grouped, normed_b], axis=1), 'z', axis=0,...]
    all_to_all x0 -> x6, waiting for transfers between devices: none -> 44 us  [the longest x5 44 us: swap(): return lax.all_to_all(value, 'z', 0, 0)]
    all_to_all x0 -> x6, starting transfers between devices: none -> 36.1 us  [the longest x5 32.2 us: swap(): return lax.all_to_all(value, 'z', 0, 0)]
    unnamed x39 -> x40, local copies, waits for them, and re-layouts: 17.5 us -> 4.62 us
    concatenate x3 -> x4, other arithmetic: 12.3 us -> 3.42 us  [the longest x1 1.12 us: local(): jnp.concatenate([part_attend, part_short], axis=1).astype(jnp.bfloat16)]
    pallas_call x0 -> x1, Pallas kernels: none -> 8.18 us  [attention(): pl.pallas_call(functools.partial(attention_body, block, shards), out_shap...]
    dynamic_update_slice x2 -> x0, local copies, waits for them, and re-layouts: 8.13 us -> none  [backward_step(): lax.dynamic_update_slice_in_dim(term, jnp.concatenate([key_part, value_pa...]
  transfers between devices with their start and end apart: 5 -> 17, of which waited for: 5 -> 10; matrix products, arithmetic and copies ran while one was open for 2% -> 22% of each run, Pallas kernels for 0% -> 4%
where the time goes in v1:
time: 201 us; the launch traced here: 199 us
  waiting for transfers between devices  73 us (36%)
  starting transfers between devices  46.4 us (23%)
  matrix products  22.9 us (11%)
  local copies, waits for them, and re-layouts  21 us (10%)
  between operations  14.2 us (7%)
  other arithmetic  13.7 us (7%)
  Pallas kernels  8.18 us (4%)
    all_to_all x5, waiting for transfers between devices, swap(): return lax.all_to_all(value, 'z', 0, 0)  44 us
    all_to_all x5, starting transfers between devices, swap(): return lax.all_to_all(value, 'z', 0, 0)  32.2 us
    dot_general x9, matrix products, mm(): lax.dot_general(left, right, dims, preferred_element_type=jnp.float32)  22.9 us
    reduce_scatter x1, waiting for transfers between devices, local(): lax.psum_scatter(mm(attended, d_expand_all, TN).astype(jnp.bfloat16), 'y'...  15.5 us
    ppermute x6, waiting for transfers between devices, turn_y(): lax.ppermute(value, 'y', [(i, (i + steps) % y_size) for i in range(y_size)])  9.05 us
    pallas_call x1, Pallas kernels, attention(): pl.pallas_call(functools.partial(attention_body, block, shards), out_shap...  8.18 us
    ppermute x6, starting transfers between devices, turn_y(): lax.ppermute(value, 'y', [(i, (i + steps) % y_size) for i in range(y_size)])  5.36 us
    dot_general x2, local copies, waits for them, and re-layouts, mm(): lax.dot_general(left, right, dims, preferred_element_type=jnp.float32)  4.99 us
  transfers between devices with their start and end apart: 17, of which 10 were waited for; matrix products, arithmetic and copies ran while one was open for 22% of the time, Pallas kernels for 4%

profile of v1, /device:TPU:6, one launch (start us, length us, event | category | flops | bytes accessed | tf_op | source)
XLA Modules:
  0.0 199.3 jit_solution(15038151976899703317)
XLA Ops:
  7.2 0.8 slice.54
  8.1 3.5 %collective-permute-start = (bf16[3,256]{1,0:T(4,128)(2,1)S(1)}, bf16[3,256]{1,0:T(4,128)(2,1)S(1)}, u32[]{:S(2)}, u32[]{:S(2)}) collective-permute-start(bf16[3,256]{1,0:T(4,128)(2,1)S(1)} %slice.54), channel_id=1, source_target_pairs={{0,1},{1,2},{2,3},{3,4},{4,5},{5,6},{6,7},{7,8},{8,9},{9,10},{10,1... | collective-permute-start | bytes 4616 | tf_op jit(solution)/shard_map/ppermute | solution.py:142
  11.5 1.3 collective-permute-done
  12.8 1.0 pad_maximum_fusion.4
  13.9 0.6 multiply_reduce_fusion.1
  14.5 0.7 copy-done.9
  15.3 0.8 pad_maximum_fusion.3
  16.1 4.0 %convolution_convert_fusion = bf16[80,3072]{1,0:T(8,128)(2,1)S(1)} fusion(bf16[80,1024]{1,0:T(8,128)(2,1)S(1)} %multiply_convert_fusion.1, bf16[1024,3072]{1,0:T(8,128)(2,1)} %param.7), kind=kOutput, calls=%fused_computation | convolution fusion | flops 503562240 | bytes 6946816 | tf_op jit(solution)/shard_map/dot_general | solution.py:21
  20.3 0.3 copy.31
  20.6 0.9 reshape.103
  21.6 12.5 %all-to-all-start.1 = ((bf16[8,80,256]{2,1,0:T(8,128)(2,1)}), bf16[8,80,256]{2,1,0:T(8,128)(2,1)S(1)}, u32[]{:S(2)}, u32[]{:S(2)}) async-start(bf16[8,80,256]{2,1,0:T(8,128)(2,1)} %reshape.103), calls=%async_computation.1 | async-start | bytes 655360 | tf_op jit(solution)/shard_map/all_to_all | solution.py:133
  34.2 2.4 %fusion.1 = bf16[10,8,8,128]{3,1,2,0:T(8,128)(2,1)S(1)} fusion(bf16[80,1024]{1,0:T(8,128)(2,1)S(1)} %reshape.100, bf16[1024,1024]{1,0:T(8,128)(2,1)} %param.8), kind=kOutput, calls=%fused_computation.8 | convolution fusion | flops 167854080 | bytes 2424832 | tf_op jit(solution)/shard_map/dot_general | solution.py:21
  36.7 0.3 copy.30
  37.1 0.9 reshape.101
  38.0 12.6 %all-to-all-done.1 = bf16[8,80,256]{2,1,0:T(8,128)(2,1)S(1)} async-done(((bf16[8,80,256]{2,1,0:T(8,128)(2,1)}), bf16[8,80,256]{2,1,0:T(8,128)(2,1)S(1)}, u32[]{:S(2)}, u32[]{:S(2)}) %all-to-all-start.1) | async-done | bytes 327712 | tf_op jit(solution)/shard_map/all_to_all | solution.py:133
  50.6 3.4 %all-to-all-start = ((bf16[8,80,256]{2,1,0:T(8,128)(2,1)}), bf16[8,80,256]{2,1,0:T(8,128)(2,1)S(1)}, u32[]{:S(2)}, u32[]{:S(2)}) async-start(bf16[8,80,256]{2,1,0:T(8,128)(2,1)} %reshape.101), calls=%async_computation | async-start | bytes 655360 | tf_op jit(solution)/shard_map/all_to_all | solution.py:133
  54.4 3.0 %collective-permute-start.3 = (bf16[640,256]{1,0:T(8,128)(2,1)S(1)}, bf16[640,256]{1,0:T(8,128)(2,1)}, u32[]{:S(2)}, u32[]{:S(2)}) collective-permute-start(bf16[640,256]{1,0:T(8,128)(2,1)S(1)} %bitcast.86), channel_id=1, source_target_pairs={{0,3},{1,0},{2,1},{3,2},{4,7},{5,4},{6,5},{7,6},{8,11},{9,8},{10,9... | collective-permute-start | bytes 983048 | tf_op jit(solution)/shard_map/ppermute | solution.py:126
  57.6 12.6 %all-to-all-done = bf16[8,80,256]{2,1,0:T(8,128)(2,1)S(1)} async-done(((bf16[8,80,256]{2,1,0:T(8,128)(2,1)}), bf16[8,80,256]{2,1,0:T(8,128)(2,1)S(1)}, u32[]{:S(2)}, u32[]{:S(2)}) %all-to-all-start) | async-done | bytes 327712 | tf_op jit(solution)/shard_map/all_to_all | solution.py:133
  70.2 0.7 copy-done.3
  70.9 0.7 copy-done.5
  71.6 1.0 copy-done.4
  72.6 1.0 copy-done.6
  73.6 8.2 %attention.1 = (bf16[640,128]{1,0:T(8,128)(2,1)S(1)}, bf16[640,128]{1,0:T(8,128)(2,1)S(1)}, f32[640,256]{1,0:T(8,128)S(1)}, bf16[640,256]{1,0:T(8,128)(2,1)}, bf...) custom-call(s32[1]{0:T(128)} %bitcast.y_ref, bf16[640,256]{1,0:T(8,128)(2,1)S(1)} %bitcast.91, ...), custom_call_target="tpu_custom_call" | custom-call | tf_op jit(solution)/shard_map/attention/pallas_call | solution.py:98
  81.7 1.1 collective-permute-start.4
  82.8 0.9 collective-permute-start.6
  83.8 0.8 pad_maximum_fusion.1
  84.6 6.8 %all-to-all-start.2 = ((bf16[8,80,256]{2,1,0:T(8,128)(2,1)}), bf16[8,80,256]{2,1,0:T(8,128)(2,1)S(1)}, u32[]{:S(2)}, u32[]{:S(2)}) async-start(bf16[8,80,256]{2,1,0:T(8,128)(2,1)} %bitcast.97), calls=%async_computation.2 | async-start | bytes 655360 | tf_op jit(solution)/shard_map/all_to_all | solution.py:133
  91.4 5.6 %collective-permute-done.4 = bf16[640,256]{1,0:T(8,128)(2,1)} collective-permute-done((bf16[640,256]{1,0:T(8,128)(2,1)}, bf16[640,256]{1,0:T(8,128)(2,1)}, u32[]{:S(2)}, u32[]{:S(2)}) %collective-permute-start.4) | collective-permute-done | bytes 327712 | tf_op jit(solution)/shard_map/ppermute | solution.py:126
  97.0 3.4 %collective-permute-done.6 = bf16[640,256]{1,0:T(8,128)(2,1)} collective-permute-done((bf16[640,256]{1,0:T(8,128)(2,1)}, bf16[640,256]{1,0:T(8,128)(2,1)}, u32[]{:S(2)}, u32[]{:S(2)}) %collective-permute-start.6) | collective-permute-done | bytes 327712 | tf_op jit(solution)/shard_map/ppermute | solution.py:126
  100.4 1.3 convert_add_fusion
  101.7 0.3 fusion.15
  102.0 0.2 fusion.18
  102.3 0.8 pad_maximum_fusion.2
  103.1 0.8 all-to-all-done.2
  103.9 5.9 %all-to-all-start.3 = ((bf16[8,80,256]{2,1,0:T(8,128)(2,1)}), bf16[8,80,256]{2,1,0:T(8,128)(2,1)S(1)}, u32[]{:S(2)}, u32[]{:S(2)}) async-start(bf16[8,80,256]{2,1,0:T(8,128)(2,1)} %pad_maximum_fusion.2), calls=%async_computation.3 | async-start | bytes 655360 | tf_op jit(solution)/shard_map/all_to_all | solution.py:133
  109.9 0.7 all-gather.5.cloned.1.call-update
  111.0 12.0 %all-to-all-done.3 = bf16[8,80,256]{2,1,0:T(8,128)(2,1)S(1)} async-done(((bf16[8,80,256]{2,1,0:T(8,128)(2,1)}), bf16[8,80,256]{2,1,0:T(8,128)(2,1)S(1)}, u32[]{:S(2)}, u32[]{:S(2)}) %all-to-all-start.3) | async-done | bytes 327712 | tf_op jit(solution)/shard_map/all_to_all | solution.py:133
  123.4 4.9 %multiply_reduce_fusion = (f32[80]{0:T(128)S(1)}, f32[80,1024]{1,0:T(8,128)S(1)}) fusion(f32[80,1024]{1,0:T(8,128)S(1)} %copy-done.10, f32[80]{0:T(128)S(1)} %add_rsqrt_fusion.1, bf16[1024,3072]{1,0:T(8,128)(2,1)} %param.7, bf16[80,1024]{1,0:T(8,128)(2,1)S(1)} %get-tuple-element.21, bf16[80,1024]{1,0:T(8,128)(2,1)S(1)} %get-tuple-element.20, ...), kind=kOutput, calls=%fused_computation.40 | convolution fusion | flops 505036736 | bytes 7438976 | tf_op jit(solution)/shard_map/dot_general | solution.py:21
  128.4 0.7 bitcast_bitcast_fusion
  129.1 3.6 %all-to-all-start.4 = ((bf16[8,80,128]{2,1,0:T(8,128)(2,1)}), bf16[8,80,128]{2,1,0:T(8,128)(2,1)S(1)}, u32[]{:S(2)}, u32[]{:S(2)}) async-start(bf16[8,80,128]{2,1,0:T(8,128)(2,1)} %bitcast_bitcast_fusion), calls=%async_computation.4 | async-start | bytes 327680 | tf_op jit(solution)/shard_map/all_to_all | solution.py:133
  132.8 2.5 %slice_bitcast_fusion = bf16[1024,640]{0,1:T(8,128)(2,1)} fusion(bf16[640,2048]{1,0:T(8,128)(2,1)} %all-gather.3.cloned.1.call-done), kind=kLoop, calls=%fused_computation.2 | loop fusion | bytes 2621440 | tf_op jit(solution)/shard_map/dot_general | solution.py:21
  135.3 2.5 %copy.34 = bf16[1024,640]{1,0:T(8,128)(2,1)} copy(bf16[1024,640]{0,1:T(8,128)(2,1)} %slice_bitcast_fusion) | data formatting | bytes 2621440 | tf_op jit(solution)/shard_map/dot_general | solution.py:21
  137.8 6.0 %all-to-all-done.4 = bf16[8,80,128]{2,1,0:T(8,128)(2,1)S(1)} async-done(((bf16[8,80,128]{2,1,0:T(8,128)(2,1)}), bf16[8,80,128]{2,1,0:T(8,128)(2,1)S(1)}, u32[]{:S(2)}, u32[]{:S(2)}) %all-to-all-start.4) | async-done | bytes 163872 | tf_op jit(solution)/shard_map/all_to_all | solution.py:133
  143.7 1.8 convolution_convert_fusion.3
  145.6 2.4 %convolution_convert_fusion.1 = bf16[1024,384]{1,0:T(8,128)(2,1)S(1)} fusion(bf16[640,2048]{1,0:T(8,128)(2,1)} %all-gather.3.cloned.1.call-done, bf16[640,128]{1,0:T(8,128)(2,1)} %copy-done.14, bf16[640,128]{1,0:T(8,128)(2,1)} %copy-done.15, bf16[640,128]{1,0:T(8,128)(2,1)S(1)} %copy-done.8), kind=kOutput, calls=%fused_computation.1 | convolution fusion | flops 505184256 | bytes 2588672 | tf_op jit(solution)/shard_map/dot_general | solution.py:21
  147.9 1.1 pad_maximum_fusion
  149.1 3.9 %all-to-all-start.5 = ((bf16[32,32,512]{2,1,0:T(8,128)(2,1)}), bf16[32,32,512]{2,1,0:T(8,128)(2,1)S(1)}, u32[]{:S(2)}, u32[]{:S(2)}) async-start(bf16[32,32,512]{2,1,0:T(8,128)(2,1)} %pad_maximum_fusion), calls=%async_computation.5 | async-start | bytes 2097152 | tf_op jit(solution)/shard_map/all_to_all | solution.py:194
  153.1 2.9 %fusion.20 = f32[80,1024]{1,0:T(8,128)} fusion(bf16[1024,1024]{1,0:T(8,128)(2,1)} %param.8, bf16[80,2,1024]{2,0,1:T(8,128)(2,1)} %copy-done.12), kind=kOutput, calls=%fused_computation.49 | convolution fusion | flops 167772160 | bytes 2588672 | tf_op jit(solution)/shard_map/dot_general | solution.py:21
  156.0 1.8 reshape.108
  157.8 2.4 %convolution_convert_fusion.2 = bf16[128,1024]{1,0:T(8,128)(2,1)} fusion(bf16[640,128]{1,0:T(8,128)(2,1)S(1)} %copy-done.2, bf16[640,1024]{1,0:T(8,128)(2,1)} %all-gather.5.cloned.1.call-done), kind=kOutput, calls=%fused_computation.4 | convolution fusion | flops 167903232 | bytes 1736704 | tf_op jit(solution)/shard_map/dot_general | solution.py:21
  160.2 1.4 convolution_convert_fusion.4
  161.7 1.0 reshape.111
  162.7 1.3 collective-permute-start.7
  164.0 1.7 add_convert_fusion.1
  165.7 2.5 %collective-permute-done.7 = bf16[3,256]{1,0:T(4,128)(2,1)S(1)} collective-permute-done((bf16[3,256]{1,0:T(4,128)(2,1)S(1)}, bf16[3,256]{1,0:T(4,128)(2,1)S(1)}, u32[]{:S(2)}, u32[]{:S(2)}) %collective-permute-start.7) | collective-permute-done | bytes 1568 | tf_op jit(solution)/shard_map/ppermute | solution.py:185
  168.2 1.6 add_convert_fusion
  169.8 15.5 %reduce-scatter.2.cloned.1.call-done = bf16[32,1024]{1,0:T(8,128)(2,1)} async-done(((bf16[128,1024]{1,0:T(8,128)(2,1)}), bf16[32,1024]{1,0:T(8,128)(2,1)}) %reduce-scatter.2.cloned.1.call-update) | async-done | bytes 65552 | tf_op jit(solution)/shard_map/reduce_scatter | solution.py:159
  185.3 1.5 convert_element_type.75
  186.8 1.7 reshape.115
  188.5 2.2 %reduce_sum.49 = f32[8,32,4,128]{3,2,1,0:T(4,128)S(1)} reduce(f32[8,4,32,4,128]{4,3,2,1,0:T(4,128)} %reshape.115, f32[]{:T(128)} %constant.6.clone.1), dimensions={1}, to_apply=%region_4.0 | reduce | flops 393216 | bytes 2621444 | tf_op jit(solution)/shard_map/reduce_sum | solution.py:195
  190.7 0.3 copy.36
  191.0 0.3 copy.45
  191.4 0.8 slice.87
  192.1 0.7 slice.86
  (70 shorter events, 2.2 us)
Async XLA Ops:
  7.2 6.7 %copy-start = (bf16[1024,1024]{1,0:T(8,128)(2,1)S(1)}, bf16[1024,1024]{1,0:T(8,128)(2,1)}, u32[]{:S(2)}) copy-start(bf16[1024,1024]{1,0:T(8,128)(2,1)} %param.6) | copy-start | bytes 6291460
  7.2 125.6 %all-gather.3.cloned.1.call-start = ((), (), s32[]{:S(2)}) async-start(), calls=%async_computation.7 | async-start | bytes 2949120 | tf_op jit(solution)/shard_map/all_gather | solution.py:149
  8.1 4.8 %collective-permute-start = (bf16[3,256]{1,0:T(4,128)(2,1)S(1)}, bf16[3,256]{1,0:T(4,128)(2,1)S(1)}, u32[]{:S(2)}, u32[]{:S(2)}) collective-permute-start(bf16[3,256]{1,0:T(4,128)(2,1)S(1)} %slice.54), channel_id=1, source_target_pairs={{0,1},{1,2},{2,3},{3,4},{4,5},{5,6},{6,7},{7,8},{8,9},{9,10},{10,1... | collective-permute-start | bytes 4616 | tf_op jit(solution)/shard_map/ppermute | solution.py:142
  14.5 0.8 copy-start.9
  20.1 13.9 %copy-start.16 = (bf16[320,256]{1,0:T(8,128)(2,1)S(1)}, bf16[320,256]{1,0:T(8,128)(2,1)}, u32[]{:S(2)}) copy-start(bf16[320,256]{1,0:T(8,128)(2,1)} %param.9) | copy-start | bytes 491524
  21.6 29.1 %all-to-all-start.1 = ((bf16[8,80,256]{2,1,0:T(8,128)(2,1)}), bf16[8,80,256]{2,1,0:T(8,128)(2,1)S(1)}, u32[]{:S(2)}, u32[]{:S(2)}) async-start(bf16[8,80,256]{2,1,0:T(8,128)(2,1)} %reshape.103), calls=%async_computation.1 | async-start | bytes 655360 | tf_op jit(solution)/shard_map/all_to_all | solution.py:133
  34.2 2.9 %copy-start.11 = (bf16[80,1024]{1,0:T(8,128)(2,1)}, bf16[80,1024]{1,0:T(8,128)(2,1)S(1)}, u32[]{:S(2)}) copy-start(bf16[80,1024]{1,0:T(8,128)(2,1)S(1)} %reshape.100) | copy-start | bytes 491524
  50.6 19.5 %all-to-all-start = ((bf16[8,80,256]{2,1,0:T(8,128)(2,1)}), bf16[8,80,256]{2,1,0:T(8,128)(2,1)S(1)}, u32[]{:S(2)}, u32[]{:S(2)}) async-start(bf16[8,80,256]{2,1,0:T(8,128)(2,1)} %reshape.101), calls=%async_computation | async-start | bytes 655360 | tf_op jit(solution)/shard_map/all_to_all | solution.py:133
  54.1 16.1 %collective-permute-start.1 = (bf16[640,256]{1,0:T(8,128)(2,1)S(1)}, bf16[640,256]{1,0:T(8,128)(2,1)S(1)}, u32[]{:S(2)}, u32[]{:S(2)}) collective-permute-start(bf16[640,256]{1,0:T(8,128)(2,1)S(1)} %bitcast.84), channel_id=1, source_target_pairs={{0,1},{1,2},{2,3},{3,0},{4,5},{5,6},{6,7},{7,4},{8,9},{9,10},{10,1... | collective-permute-start | bytes 983048 | tf_op jit(solution)/shard_map/ppermute | solution.py:126
  54.2 16.7 %collective-permute-start.2 = (bf16[640,256]{1,0:T(8,128)(2,1)S(1)}, bf16[640,256]{1,0:T(8,128)(2,1)S(1)}, u32[]{:S(2)}, u32[]{:S(2)}) collective-permute-start(bf16[640,256]{1,0:T(8,128)(2,1)S(1)} %bitcast.85), channel_id=1, source_target_pairs={{0,2},{1,3},{2,0},{3,1},{4,6},{5,7},{6,4},{7,5},{8,10},{9,11},{10,... | collective-permute-start | bytes 983048 | tf_op jit(solution)/shard_map/ppermute | solution.py:126
  54.4 17.2 %collective-permute-start.3 = (bf16[640,256]{1,0:T(8,128)(2,1)S(1)}, bf16[640,256]{1,0:T(8,128)(2,1)}, u32[]{:S(2)}, u32[]{:S(2)}) collective-permute-start(bf16[640,256]{1,0:T(8,128)(2,1)S(1)} %bitcast.86), channel_id=1, source_target_pairs={{0,3},{1,0},{2,1},{3,2},{4,7},{5,4},{6,5},{7,6},{8,11},{9,8},{10,9... | collective-permute-start | bytes 983048 | tf_op jit(solution)/shard_map/ppermute | solution.py:126
  70.2 0.7 copy-start.3
  70.9 0.7 copy-start.5
  71.6 1.0 copy-start.4
  72.6 1.0 copy-start.6
  81.7 2.1 %copy-start.1 = (bf16[640,128]{1,0:T(8,128)(2,1)}, bf16[640,128]{1,0:T(8,128)(2,1)S(1)}, u32[]{:S(2)}) copy-start(bf16[640,128]{1,0:T(8,128)(2,1)S(1)} %get-tuple-element.11) | copy-start | bytes 491524
  81.7 2.8 %copy-start.7 = (bf16[640,128]{1,0:T(8,128)(2,1)}, bf16[640,128]{1,0:T(8,128)(2,1)S(1)}, u32[]{:S(2)}) copy-start(bf16[640,128]{1,0:T(8,128)(2,1)S(1)} %get-tuple-element.12) | copy-start | bytes 491524
  81.7 15.2 %collective-permute-start.4 = (bf16[640,256]{1,0:T(8,128)(2,1)}, bf16[640,256]{1,0:T(8,128)(2,1)}, u32[]{:S(2)}, u32[]{:S(2)}) collective-permute-start(bf16[640,256]{1,0:T(8,128)(2,1)} %get-tuple-element.14), channel_id=1, source_target_pairs={{0,3},{1,0},{2,1},{3,2},{4,7},{5,4},{6,5},{7,6},{8,11},{9,8},{10,9... | collective-permute-start | bytes 983048 | tf_op jit(solution)/shard_map/ppermute | solution.py:126
  82.8 14.1 %collective-permute-start.5 = (bf16[640,256]{1,0:T(8,128)(2,1)}, bf16[640,256]{1,0:T(8,128)(2,1)}, u32[]{:S(2)}, u32[]{:S(2)}) collective-permute-start(bf16[640,256]{1,0:T(8,128)(2,1)} %get-tuple-element.15), channel_id=1, source_target_pairs={{0,2},{1,3},{2,0},{3,1},{4,6},{5,7},{6,4},{7,5},{8,10},{9,11},{10,... | collective-permute-start | bytes 983048 | tf_op jit(solution)/shard_map/ppermute | solution.py:126
  82.8 17.5 %collective-permute-start.6 = (bf16[640,256]{1,0:T(8,128)(2,1)}, bf16[640,256]{1,0:T(8,128)(2,1)}, u32[]{:S(2)}, u32[]{:S(2)}) collective-permute-start(bf16[640,256]{1,0:T(8,128)(2,1)} %get-tuple-element.16), channel_id=1, source_target_pairs={{0,1},{1,2},{2,3},{3,0},{4,5},{5,6},{6,7},{7,4},{8,9},{9,10},{10,1... | collective-permute-start | bytes 983048 | tf_op jit(solution)/shard_map/ppermute | solution.py:126
  84.6 19.3 %all-to-all-start.2 = ((bf16[8,80,256]{2,1,0:T(8,128)(2,1)}), bf16[8,80,256]{2,1,0:T(8,128)(2,1)S(1)}, u32[]{:S(2)}, u32[]{:S(2)}) async-start(bf16[8,80,256]{2,1,0:T(8,128)(2,1)} %bitcast.97), calls=%async_computation.2 | async-start | bytes 655360 | tf_op jit(solution)/shard_map/all_to_all | solution.py:133
  101.7 8.1 %copy-start.14 = (bf16[640,128]{1,0:T(8,128)(2,1)}, bf16[640,128]{1,0:T(8,128)(2,1)S(1)}, u32[]{:S(2)}) copy-start(bf16[640,128]{1,0:T(8,128)(2,1)S(1)} %slice.105) | copy-start | bytes 491524
  102.3 7.6 %copy-start.15 = (bf16[640,128]{1,0:T(8,128)(2,1)}, bf16[640,128]{1,0:T(8,128)(2,1)S(1)}, u32[]{:S(2)}) copy-start(bf16[640,128]{1,0:T(8,128)(2,1)S(1)} %fusion.18) | copy-start | bytes 491524
  103.9 19.0 %all-to-all-start.3 = ((bf16[8,80,256]{2,1,0:T(8,128)(2,1)}), bf16[8,80,256]{2,1,0:T(8,128)(2,1)S(1)}, u32[]{:S(2)}, u32[]{:S(2)}) async-start(bf16[8,80,256]{2,1,0:T(8,128)(2,1)} %pad_maximum_fusion.2), calls=%async_computation.3 | async-start | bytes 655360 | tf_op jit(solution)/shard_map/all_to_all | solution.py:133
  109.8 48.0 %all-gather.5.cloned.1.call-start = ((), (), s32[]{:S(2)}) async-start(), calls=%async_computation.8 | async-start | bytes 1474560 | tf_op jit(solution)/shard_map/all_gather | solution.py:141
  110.7 12.7 %copy-start.10 = (f32[80,1024]{1,0:T(8,128)S(1)}, f32[80,1024]{1,0:T(8,128)}, u32[]{:S(2)}) copy-start(f32[80,1024]{1,0:T(8,128)} %copy-done.9) | copy-start | bytes 983044
  111.0 12.4 %copy-start.12 = (bf16[80,2,1024]{2,0,1:T(8,128)(2,1)}, bf16[80,2,1024]{2,0,1:T(8,128)(2,1)S(1)}, u32[]{:S(2)}) copy-start(bf16[80,2,1024]{2,0,1:T(8,128)(2,1)S(1)} %reshape.107) | copy-start | bytes 983044
  129.1 14.6 %all-to-all-start.4 = ((bf16[8,80,128]{2,1,0:T(8,128)(2,1)}), bf16[8,80,128]{2,1,0:T(8,128)(2,1)S(1)}, u32[]{:S(2)}, u32[]{:S(2)}) async-start(bf16[8,80,128]{2,1,0:T(8,128)(2,1)} %bitcast_bitcast_fusion), calls=%async_computation.4 | async-start | bytes 327680 | tf_op jit(solution)/shard_map/all_to_all | solution.py:133
  135.3 10.3 %copy-start.8 = (bf16[640,128]{1,0:T(8,128)(2,1)S(1)}, bf16[640,128]{1,0:T(8,128)(2,1)}, u32[]{:S(2)}) copy-start(bf16[640,128]{1,0:T(8,128)(2,1)} %copy-done.7) | copy-start | bytes 491524
  149.1 37.8 %all-to-all-start.5 = ((bf16[32,32,512]{2,1,0:T(8,128)(2,1)}), bf16[32,32,512]{2,1,0:T(8,128)(2,1)S(1)}, u32[]{:S(2)}, u32[]{:S(2)}) async-start(bf16[32,32,512]{2,1,0:T(8,128)(2,1)} %pad_maximum_fusion), calls=%async_computation.5 | async-start | bytes 2097152 | tf_op jit(solution)/shard_map/all_to_all | solution.py:194
  153.0 4.8 %copy-start.2 = (bf16[640,128]{1,0:T(8,128)(2,1)S(1)}, bf16[640,128]{1,0:T(8,128)(2,1)}, u32[]{:S(2)}) copy-start(bf16[640,128]{1,0:T(8,128)(2,1)} %copy-done.1) | copy-start | bytes 491524
  153.0 32.3 %reduce-scatter.2.cloned.1.call-start = ((), (), s32[]{:S(2)}) async-start(), calls=%async_computation.9 | async-start | bytes 327680 | tf_op jit(solution)/shard_map/reduce_scatter | solution.py:159
  160.2 3.8 %copy-start.13 = (bf16[320,256]{1,0:T(8,128)(2,1)S(1)}, bf16[320,256]{1,0:T(8,128)(2,1)}, u32[]{:S(2)}) copy-start(bf16[320,256]{1,0:T(8,128)(2,1)} %param.5) | copy-start | bytes 491524
  162.7 5.5 %collective-permute-start.7 = (bf16[3,256]{1,0:T(4,128)(2,1)S(1)}, bf16[3,256]{1,0:T(4,128)(2,1)S(1)}, u32[]{:S(2)}, u32[]{:S(2)}) collective-permute-start(bf16[3,256]{1,0:T(4,128)(2,1)S(1)} %slice.83), channel_id=1, source_target_pairs={{1,0},{2,1},{3,2},{4,3},{5,4},{6,5},{7,6},{8,7},{9,8},{10,9},{11,1... | collective-permute-start | bytes 4616 | tf_op jit(solution)/shard_map/ppermute | solution.py:185
Sparse Core Ops, SparseCore 0:
  16.2 59.3 all-gather.2
  112.5 39.8 all-gather.4
  160.3 24.9 reduce-scatter.1

commit v2 on v1

--- a/solution.py
+++ b/solution.py
@@ -111,6 +111,171 @@
     )(y, qd, *kvs)
 
 
+def hidden_grad_body(y_ref, first_ref, second_ref, weight_ref, normed_ref, scale_ref, out_ref, *refs):
+    cols_refs, (joined_ref,) = refs[:-1], refs[-1:]
+    heads, rows, width = first_ref.shape
+    lanes = width // 2
+    attn_width = heads * lanes
+    for head in range(heads):
+        places = [part * attn_width + head * lanes for part in range(3)]
+        joined_ref[:, places[0] : places[0] + lanes] = first_ref[head, :, lanes:]
+        joined_ref[:, places[1] : places[1] + lanes] = second_ref[head, :, :lanes]
+        joined_ref[:, places[2] : places[2] + lanes] = second_ref[head, :, lanes:]
+    d_normed = mm(joined_ref[...], weight_ref[...], NT)
+    out_ref[...] = norm_back(normed_ref[...], scale_ref[...], d_normed).astype(jnp.bfloat16)
+    count = len(cols_refs)
+    y_cols = out_ref.shape[1] // count
+    for step, cols_ref in enumerate(cols_refs):
+        first = pl.multiple_of(lax.rem(y_ref[0] + step, count) * y_cols, y_cols)
+        cols_ref[...] = out_ref[:, pl.ds(first, y_cols)]
+
+
+def hidden_grad(y, first, second, weight, normed, scale, y_size):
+    rows, model_width = normed.shape
+    vmem = pl.BlockSpec(memory_space=pltpu.VMEM)
+    outs = [jax.ShapeDtypeStruct((rows, model_width), jnp.bfloat16)]
+    outs += [jax.ShapeDtypeStruct((rows, model_width // y_size), jnp.bfloat16)] * y_size
+    return pl.pallas_call(
+        hidden_grad_body,
+        out_shape=outs,
+        in_specs=[pl.BlockSpec(memory_space=pltpu.SMEM)] + [vmem] * 5,
+        out_specs=[vmem] * len(outs),
+        scratch_shapes=[pltpu.VMEM((rows, weight.shape[1]), jnp.bfloat16)],
+        compiler_params=pltpu.CompilerParams(vmem_limit_bytes=24 * 1024 * 1024),
+        name="hidden_grad",
+    )(y, first, second, weight, normed, scale)
+
+
+def head_grads_body(normed_ref, dq_ref, dkv_ref, attended_ref, expand_ref, out_ref):
+    shards, groups, own_rows, width = out_ref.shape
+    d_head = jnp.concatenate([dq_ref[...], dkv_ref[...]], axis=1)
+    attend = mm(normed_ref[...], d_head, TN).astype(out_ref.dtype)
+    expand = mm(attended_ref[...], expand_ref[...], TN).astype(out_ref.dtype)
+    head_width = d_head.shape[1]
+    lanes = width - head_width
+    for shard in range(shards):
+        for group in range(groups):
+            first = (group * shards + shard) * own_rows
+            out_ref[shard, group, :, :head_width] = attend[first : first + own_rows]
+            piece = expand[shard * own_rows : (shard + 1) * own_rows, group * lanes : (group + 1) * lanes]
+            out_ref[shard, group, :, head_width:] = piece
+
+
+def head_grads(normed, d_query, d_kv, attended, d_expand, groups, shards):
+    model_width = normed.shape[1]
+    width = 3 * d_query.shape[1] + d_expand.shape[1] // groups
+    vmem = pl.BlockSpec(memory_space=pltpu.VMEM)
+    return pl.pallas_call(
+        head_grads_body,
+        out_shape=jax.ShapeDtypeStruct((shards, groups, model_width // groups // shards, width), jnp.bfloat16),
+        in_specs=[vmem] * 5,
+        out_specs=vmem,
+        compiler_params=pltpu.CompilerParams(vmem_limit_bytes=24 * 1024 * 1024),
+        name="head_grads",
+    )(normed, d_query, d_kv, attended, d_expand)
+
+
+def split_parts_body(z_ref, parts_ref, expand_ref, *piece_refs):
+    groups, _, width = parts_ref.shape
+    head_width = piece_refs[0].shape[1]
+    lanes = width - head_width
+    for group in range(groups):
+        expand_ref[:, group * lanes : (group + 1) * lanes] = parts_ref[group, :, head_width:].astype(jnp.float32)
+    for step, piece_ref in enumerate(piece_refs):
+        piece_ref[...] = parts_ref[lax.rem(z_ref[0] + step, groups), :, :head_width]
+
+
+def split_parts(z, parts, head_width):
+    groups, own_rows, width = parts.shape
+    vmem = pl.BlockSpec(memory_space=pltpu.VMEM)
+    outs = [jax.ShapeDtypeStruct((own_rows, (width - head_width) * groups), jnp.float32)]
+    outs += [jax.ShapeDtypeStruct((own_rows, head_width), jnp.bfloat16)] * groups
+    return pl.pallas_call(
+        split_parts_body,
+        out_shape=outs,
+        in_specs=[pl.BlockSpec(memory_space=pltpu.SMEM), vmem],
+        out_specs=[vmem] * len(outs),
+        name="split_parts",
+    )(z, parts)
+
+
+def short_grads_body(shards, *refs):
+    grouped_refs, cols_refs, out_ref = refs[:shards], refs[shards : 2 * shards], refs[-1]
+    count, tall, lanes = out_ref.shape
+    grouped = jnp.concatenate([ref[...] for ref in grouped_refs], axis=0)
+    cols = jnp.concatenate([ref[...] for ref in cols_refs], axis=0)
+    short = mm(grouped, cols, TN).astype(jnp.bfloat16)
+    parts = short.shape[1] // lanes
+    own_rows = tall // parts
+    for part in range(parts):
+        piece = short[:, part * lanes : (part + 1) * lanes].reshape(count, own_rows, lanes)
+        out_ref[:, part * own_rows : (part + 1) * own_rows, :] = piece
+
+
+def short_grads(grouped, cols, count, lanes):
+    tall = grouped[0].shape[1] // count * (cols[0].shape[1] // lanes)
+    vmem = pl.BlockSpec(memory_space=pltpu.VMEM)
+    return pl.pallas_call(
+        functools.partial(short_grads_body, len(grouped)),
+        out_shape=jax.ShapeDtypeStruct((count, tall, lanes), jnp.bfloat16),
+        in_specs=[vmem] * (2 * len(grouped)),
+        out_specs=vmem,
+        name="short_grads",
+    )(*grouped, *cols)
+
+
+def assemble_attend_body(z_ref, *refs):
+    piece_refs, out_ref = refs[:-1], refs[-1]
+    groups = len(piece_refs)
+    lanes = piece_refs[0].shape[1] // 3
+    for step, piece_ref in enumerate(piece_refs):
+        head = lax.rem(z_ref[0] + (groups - step), groups)
+        for part in range(3):
+            first = pl.multiple_of((part * groups + head) * lanes, lanes)
+            piece = piece_ref[:, part * lanes : (part + 1) * lanes].astype(jnp.float32)
+            out_ref[:, pl.ds(first, lanes)] = piece
+
+
+def assemble_attend(z, pieces):
+    own_rows, width = pieces[0].shape
+    vmem = pl.BlockSpec(memory_space=pltpu.VMEM)
+    return pl.pallas_call(
+        assemble_attend_body,
+        out_shape=jax.ShapeDtypeStruct((own_rows, width * len(pieces)), jnp.float32),
+        in_specs=[pl.BlockSpec(memory_space=pltpu.SMEM)] + [vmem] * len(pieces),
+        out_specs=vmem,
+        name="assemble_attend",
+    )(z, *pieces)
+
+
+def assemble_short_body(shards, parts_ref, out_ref):
+    count, tall, lanes = parts_ref.shape
+    own_rows, model_width = out_ref.shape
+    parts = tall // own_rows
+    for shard in range(shards):
+        total = jnp.zeros((tall, lanes), jnp.float32)
+        for group in range(count // shards):
+            total = total + parts_ref[group * shards + shard].astype(jnp.float32)
+        for part in range(parts):
+            first = (shard * parts + part) * lanes
+            out_ref[:, first : first + lanes] = total[part * own_rows : (part + 1) * own_rows]
+
+
+def assemble_short(parts, own_rows, model_width, shards):
+    vmem = pl.BlockSpec(memory_space=pltpu.VMEM)
+    return pl.pallas_call(
+        functools.partial(assemble_short_body, shards),
+        out_shape=jax.ShapeDtypeStruct((own_rows, model_width), jnp.float32),
+        in_specs=[vmem],
+        out_specs=vmem,
+        name="assemble_short",
+    )(parts)
+
+
+def tie(*values):
+    return lax.optimization_barrier(values)
+
+
 def local(byte_input, w_short, w_attend, w_expand, out_grad):
     z_size, y_size = lax.axis_size("z"), lax.axis_size("y")
     count = z_size * y_size
@@ -132,13 +297,7 @@
     def swap(value):
         return lax.all_to_all(value, "z", 0, 0)
 
-    def back(value):
-        parts = value.shape[2] // head_size
-        split = value.reshape(HEADS, short_rows, parts, head_size).transpose(1, 2, 0, 3)
-        return split.reshape(short_rows, parts, attn_width)
-
     d_expand = out_grad.reshape(short_rows, 4 * byte_width)
-    d_expand_all = lax.all_gather(d_expand, "z", axis=0, tiled=True)
     edge = lax.ppermute(byte_input[-3:], both, [(i, i + 1) for i in range(count - 1)])
     d_attended = mm(d_expand, w_expand, NT).astype(jnp.bfloat16)
     grouped = jnp.concatenate([edge, byte_input[:-3]], axis=0).reshape(short_rows, 4 * byte_width)
@@ -146,56 +305,59 @@
     normed, hidden_scale = unit(hidden)
     normed_b = normed.astype(jnp.bfloat16)
     projected = mm(normed_b, w_attend).astype(jnp.bfloat16)
-    inputs_all = lax.all_gather(jnp.concatenate([grouped, normed_b], axis=1), "z", axis=0, tiled=True)
-    query = projected[:, :attn_width]
     key = projected[:, attn_width : 2 * attn_width]
     value = projected[:, 2 * attn_width :]
     kv = swap(heads_of(key, value)).reshape(rows, 2 * head_size)
+    qd = heads_of(projected[:, :attn_width], d_attended)
+    grouped_y = [grouped] + [turn_y(grouped, step) for step in range(1, y_size)]
+    kv, qd, gathered, *grouped_y = tie(kv, qd, jnp.concatenate([d_expand, normed_b], axis=1), *grouped_y)
+    gathered = lax.all_gather(gathered, "z", axis=0, tiled=True)
+    d_expand_all, normed_all = gathered[:, : 4 * byte_width], gathered[:, 4 * byte_width :]
     kvs = [kv] + [turn_y(kv, step) for step in range(1, y_size)]
-    qd = swap(heads_of(query, d_attended)).reshape(rows, 2 * head_size)
+    qd = swap(qd).reshape(rows, 2 * head_size)
     y = lax.axis_index("y").astype(jnp.int32).reshape(1)
     attended, d_query, own, *sent = attention(y, qd, kvs, short_rows)
 
-    grad_expand = lax.psum_scatter(
-        mm(attended, d_expand_all, TN).astype(jnp.bfloat16), "y", scatter_dimension=0, tiled=True
-    ).astype(jnp.float32)
+    own_rows = model_width // count
+    arrived = [turn_y(sent[step - 1], -step) for step in range(1, y_size)]
     total = own
-    for step in range(1, y_size):
-        total = total + turn_y(sent[step - 1], -step).astype(jnp.float32)
+    for part in arrived:
+        total = total + part.astype(jnp.float32)
     first_back = jnp.concatenate([attended, d_query], axis=1).reshape(HEADS, short_rows, 2 * head_size)
-    first_back = back(swap(first_back))
-    attended_own = first_back[:, 0]
+    first_back = swap(first_back)
     key_unit, key_scale = unit(kv[:, :head_size].astype(jnp.float32))
     d_kv = jnp.concatenate(
         [norm_back(key_unit, key_scale, total[:, :head_size]), total[:, head_size:]], axis=1
     ).astype(jnp.bfloat16)
-    second_back = back(swap(d_kv.reshape(HEADS, short_rows, 2 * head_size)))
-    d_projected = jnp.concatenate([first_back[:, 1], second_back[:, 0], second_back[:, 1]], axis=1)
-
+    first_back, d_kv = tie(first_back, d_kv)
+    second_back = swap(d_kv.reshape(HEADS, short_rows, 2 * head_size))
+    parts = head_grads(normed_all, d_query, d_kv, attended, d_expand_all, z_size, y_size)
+    second_back, parts = tie(second_back, parts)
+    parts = lax.psum_scatter(parts, "y", scatter_dimension=0)
+    d_hidden, *d_hidden_y = hidden_grad(y, first_back, second_back, w_attend, normed, hidden_scale, y_size)
+    d_hidden_y = d_hidden_y[:1] + [turn_y(d_hidden_y[step], step) for step in range(1, y_size)]
+    d_grouped = mm(d_hidden, w_short, NT).astype(jnp.bfloat16).reshape(4 * short_rows, byte_width)
+    *d_hidden_y, d_grouped = tie(*d_hidden_y, d_grouped)
+    short = short_grads(grouped_y, d_hidden_y, count, head_size)
+    short, first_back = tie(short, first_back)
+    short = lax.all_to_all(short, both, 0, 0)
+    z = lax.axis_index("z").astype(jnp.int32).reshape(1)
+    grad_expand, *pieces = split_parts(z, parts, 3 * head_size)
+    pieces = pieces[:1] + [
+        lax.ppermute(pieces[step], "z", [(i, (i + step) % z_size) for i in range(z_size)])
+        for step in range(1, z_size)
+    ]
+    grad_attend = assemble_attend(z, pieces)
+    attended_own = first_back[:, :, :head_size].transpose(1, 0, 2).reshape(short_rows, attn_width)
     expanded = mm(attended_own, w_expand)
     byte_output = (
         byte_input.astype(jnp.float32) + expanded.reshape(4 * short_rows, byte_width)
     ).astype(jnp.bfloat16)
-
-    d_normed = mm(d_projected, w_attend, NT)
-    d_hidden = norm_back(normed, hidden_scale, d_normed).astype(jnp.bfloat16)
-    d_hidden_cols = d_hidden.reshape(short_rows, z_size, model_width // z_size).transpose(1, 0, 2)
-    d_hidden_cols = swap(d_hidden_cols).reshape(rows, model_width // z_size)
-    d_grouped = mm(d_hidden, w_short, NT).astype(jnp.bfloat16).reshape(4 * short_rows, byte_width)
     back_edge = lax.ppermute(d_grouped[:3], both, [(i + 1, i) for i in range(count - 1)])
     moved = jnp.concatenate([d_grouped[3:], back_edge], axis=0).astype(jnp.float32)
     input_grad = (out_grad.astype(jnp.float32) + moved).astype(jnp.bfloat16)
-
-    d_head = jnp.concatenate([d_query, d_kv], axis=1)
-    part_attend = mm(inputs_all[:, model_width:], d_head, TN)
-    part_short = mm(inputs_all[:, :model_width], d_hidden_cols, TN)
-    parts = jnp.concatenate([part_attend, part_short], axis=1).astype(jnp.bfloat16)
-    own_rows = model_width // count
-    parts = lax.all_to_all(parts.reshape(count, own_rows, parts.shape[1]), both, 0, 0)
-    parts = jnp.sum(parts.reshape(z_size, y_size, own_rows, 4, head_size).astype(jnp.float32), axis=1)
-    parts = parts.transpose(1, 2, 0, 3).reshape(own_rows, 4 * attn_width)
-    grad_attend = parts[:, : 3 * attn_width]
-    grad_short = parts[:, 3 * attn_width :]
+    short, input_grad, byte_output, grad_attend = tie(short, input_grad, byte_output, grad_attend)
+    grad_short = assemble_short(short, own_rows, model_width, y_size)
     return (byte_output, input_grad, grad_short, grad_attend, grad_expand)
 
 

time: 201 us -> 182 us (0.905)
  waiting for transfers between devices: 73 us -> 35.6 us
  starting transfers between devices: 46.4 us -> 76.2 us
  matrix products: 22.9 us -> 9.77 us
  Pallas kernels: 8.18 us -> 21.2 us
  other arithmetic: 13.7 us -> 7.92 us
  local copies, waits for them, and re-layouts: 21 us -> 15.8 us
    all_to_all x5 -> x4, waiting for transfers between devices: 44 us -> 8.4 us  [swap(): return lax.all_to_all(value, 'z', 0, 0)]
    ppermute x0 -> x7, starting transfers between devices: none -> 20.2 us  [local(): lax.ppermute(pieces[step], 'z', [(i, (i + step) % z_size) for i in range(...]
    ppermute x6 -> x12, waiting for transfers between devices: 9.05 us -> 25.1 us  [turn_y(): lax.ppermute(value, 'y', [(i, (i + steps) % y_size) for i in range(y_size)])]
    reduce_scatter x1, waiting for transfers between devices: 15.5 us -> 0.02 us  [local(): parts = lax.psum_scatter(parts, 'y', scatter_dimension=0)]
    dot_general x9 -> x5, matrix products: 22.9 us -> 9.77 us  [mm(): lax.dot_general(left, right, dims, preferred_element_type=jnp.float32)]
    pallas_call x0 -> x6, Pallas kernels: none -> 12.9 us  [the longest x1 3.13 us: head_grads(): pl.pallas_call(head_grads_body, out_shape=jax.ShapeDtypeStruct((shards, g...]
    ppermute x6 -> x12, starting transfers between devices: 5.36 us -> 13.9 us  [turn_y(): lax.ppermute(value, 'y', [(i, (i + steps) % y_size) for i in range(y_size)])]
    dot_general x2 -> x0, local copies, waits for them, and re-layouts: 4.99 us -> none  [mm(): lax.dot_general(left, right, dims, preferred_element_type=jnp.float32)]
  transfers between devices with their start and end apart: 17 -> 28, of which waited for: 10 -> 12; matrix products, arithmetic and copies ran while one was open for 22% -> 10% of each run, Pallas kernels for 4% -> 11%
where the time goes in v2:
time: 182 us; the launch traced here: 181 us
  starting transfers between devices  76.2 us (42%)
  waiting for transfers between devices  35.6 us (20%)
  Pallas kernels  21.2 us (12%)
  local copies, waits for them, and re-layouts  15.8 us (9%)
  between operations  14.4 us (8%)
  matrix products  9.77 us (5%)
  other arithmetic  7.92 us (4%)
    all_to_all x4, starting transfers between devices, swap(): return lax.all_to_all(value, 'z', 0, 0)  32.6 us
    ppermute x12, waiting for transfers between devices, turn_y(): lax.ppermute(value, 'y', [(i, (i + steps) % y_size) for i in range(y_size)])  25.1 us
    ppermute x7, starting transfers between devices, local(): lax.ppermute(pieces[step], 'z', [(i, (i + step) % z_size) for i in range(...  20.2 us
    ppermute x12, starting transfers between devices, turn_y(): lax.ppermute(value, 'y', [(i, (i + steps) % y_size) for i in range(y_size)])  13.9 us
    dot_general x5, matrix products, mm(): lax.dot_general(left, right, dims, preferred_element_type=jnp.float32)  9.77 us
    all_to_all x4, waiting for transfers between devices, swap(): return lax.all_to_all(value, 'z', 0, 0)  8.4 us
    pallas_call x1, Pallas kernels, attention(): pl.pallas_call(functools.partial(attention_body, block, shards), out_shap...  8.31 us
    unnamed x41, local copies, waits for them, and re-layouts  7.3 us
  transfers between devices with their start and end apart: 28, of which 12 were waited for; matrix products, arithmetic and copies ran while one was open for 10% of the time, Pallas kernels for 11%

profile of v2, /device:TPU:6, one launch (start us, length us, event | category | flops | bytes accessed | tf_op | source)
XLA Modules:
  0.0 181.0 jit_solution(12805878722024301112)
XLA Ops:
  7.2 0.8 slice.40
  8.0 3.5 %collective-permute-start = (bf16[3,256]{1,0:T(4,128)(2,1)S(1)}, bf16[3,256]{1,0:T(4,128)(2,1)S(1)}, u32[]{:S(2)}, u32[]{:S(2)}) collective-permute-start(bf16[3,256]{1,0:T(4,128)(2,1)S(1)} %slice.40), channel_id=1, source_target_pairs={{0,1},{1,2},{2,3},{3,4},{4,5},{5,6},{6,7},{7,8},{8,9},{9,10},{10,1... | collective-permute-start | bytes 4616 | tf_op jit(solution)/shard_map/ppermute | solution.py:301
  11.5 1.0 reshape.85
  12.8 1.0 pad_maximum_fusion.3
  13.9 0.6 multiply_reduce_fusion
  14.6 4.0 %convolution_convert_fusion = bf16[80,3072]{1,0:T(8,128)(2,1)S(1)} fusion(bf16[80,1024]{1,0:T(8,128)(2,1)S(1)} %get-tuple-element.89, bf16[1024,3072]{1,0:T(8,128)(2,1)} %weight_ref.1), kind=kOutput, calls=%fused_computation | convolution fusion | flops 503562240 | bytes 6946816 | tf_op jit(solution)/shard_map/dot_general | solution.py:21
  19.1 0.9 reshape.83
  20.0 12.5 %all-to-all-start = ((bf16[8,80,256]{2,1,0:T(8,128)(2,1)}), bf16[8,80,256]{2,1,0:T(8,128)(2,1)S(1)}, u32[]{:S(2)}, u32[]{:S(2)}) async-start(bf16[8,80,256]{2,1,0:T(8,128)(2,1)} %reshape.83), calls=%async_computation | async-start | bytes 655360 | tf_op jit(solution)/shard_map/all_to_all | solution.py:298
  32.6 2.4 %fusion = bf16[10,8,8,128]{3,1,2,0:T(8,128)(2,1)S(1)} fusion(bf16[80,1024]{1,0:T(8,128)(2,1)S(1)} %reshape.85, bf16[1024,1024]{1,0:T(8,128)(2,1)} %param.8), kind=kOutput, calls=%fused_computation.3 | convolution fusion | flops 167854080 | bytes 2424832 | tf_op jit(solution)/shard_map/dot_general | solution.py:21
  35.0 1.1 collective-permute-start.2
  36.2 2.1 %collective-permute-start.3 = (bf16[80,1024]{1,0:T(8,128)(2,1)S(1)}, bf16[80,1024]{1,0:T(8,128)(2,1)}, u32[]{:S(2)}, u32[]{:S(2)}) collective-permute-start(bf16[80,1024]{1,0:T(8,128)(2,1)S(1)} %reshape.82.refs_0_), channel_id=1, source_target_pairs={{0,3},{1,0},{2,1},{3,2},{4,7},{5,4},{6,5},{7,6},{8,11},{9,8},{10,9... | collective-permute-start | bytes 491528 | tf_op jit(solution)/shard_map/ppermute | solution.py:291
  38.3 1.1 copy.14
  39.4 1.9 %reshape.86 = bf16[8,80,256]{2,1,0:T(8,128)(2,1)} reshape(bf16[8,80,2,128]{3,2,1,0:T(2,128)(2,1)} %copy.14) | data formatting | bytes 655360 | tf_op jit(solution)/shard_map/reshape | solution.py:295
  41.3 0.7 pad_maximum_fusion
  42.0 2.3 %collective-permute-done.1.refs_1_ = bf16[80,1024]{1,0:T(8,128)(2,1)} collective-permute-done((bf16[80,1024]{1,0:T(8,128)(2,1)S(1)}, bf16[80,1024]{1,0:T(8,128)(2,1)}, u32[]{:S(2)}, u32[]{:S(2)}) %collective-permute-start.1) | collective-permute-done | bytes 163872 | tf_op jit(solution)/shard_map/ppermute | solution.py:291
  44.4 0.6 collective-permute-done.3.refs_3_
  45.0 6.9 %all-to-all-start.1 = ((bf16[8,80,256]{2,1,0:T(8,128)(2,1)}), bf16[8,80,256]{2,1,0:T(8,128)(2,1)S(1)}, u32[]{:S(2)}, u32[]{:S(2)}) async-start(bf16[8,80,256]{2,1,0:T(8,128)(2,1)} %reshape.86), calls=%async_computation.1 | async-start | bytes 655360 | tf_op jit(solution)/shard_map/all_to_all | solution.py:298
  52.2 3.6 %collective-permute-start.5 = (bf16[640,256]{1,0:T(8,128)(2,1)S(1)}, bf16[640,256]{1,0:T(8,128)(2,1)}, u32[]{:S(2)}, u32[]{:S(2)}) collective-permute-start(bf16[640,256]{1,0:T(8,128)(2,1)S(1)} %bitcast.52), channel_id=1, source_target_pairs={{0,2},{1,3},{2,0},{3,1},{4,6},{5,7},{6,4},{7,5},{8,10},{9,11},{10,... | collective-permute-start | bytes 983048 | tf_op jit(solution)/shard_map/ppermute | solution.py:291
  55.9 7.9 %collective-permute-done.4.refs_1_ = bf16[640,256]{1,0:T(8,128)(2,1)S(1)} collective-permute-done((bf16[640,256]{1,0:T(8,128)(2,1)S(1)}, bf16[640,256]{1,0:T(8,128)(2,1)S(1)}, u32[]{:S(2)}, u32[]{:S(2)}) %collective-permute-start.4) | collective-permute-done | bytes 327712 | tf_op jit(solution)/shard_map/ppermute | solution.py:291
  63.8 0.7 copy-done.3
  64.5 2.9 %collective-permute-done.5.refs_2_ = bf16[640,256]{1,0:T(8,128)(2,1)} collective-permute-done((bf16[640,256]{1,0:T(8,128)(2,1)S(1)}, bf16[640,256]{1,0:T(8,128)(2,1)}, u32[]{:S(2)}, u32[]{:S(2)}) %collective-permute-start.5) | collective-permute-done | bytes 327712 | tf_op jit(solution)/shard_map/ppermute | solution.py:291
  67.4 1.0 copy-done.4
  68.4 8.3 %attention.1 = (bf16[640,128]{1,0:T(8,128)(2,1)S(1)}, bf16[640,128]{1,0:T(8,128)(2,1)S(1)}, f32[640,256]{1,0:T(8,128)S(1)}, bf16[640,256]{1,0:T(8,128)(2,1)}, bf...) custom-call(s32[1]{0:T(128)} %bitcast.3.y_ref, bf16[640,256]{1,0:T(8,128)(2,1)S(1)} %bitcast.58, ...), custom_call_target="tpu_custom_call" | custom-call | tf_op jit(solution)/shard_map/attention/pallas_call | solution.py:98
  76.7 0.8 copy-done.2
  77.6 2.4 %collective-permute-start.7 = (bf16[640,256]{1,0:T(8,128)(2,1)}, bf16[640,256]{1,0:T(8,128)(2,1)}, u32[]{:S(2)}, u32[]{:S(2)}) collective-permute-start(bf16[640,256]{1,0:T(8,128)(2,1)} %get-tuple-element.56), channel_id=1, source_target_pairs={{0,3},{1,0},{2,1},{3,2},{4,7},{5,4},{6,5},{7,6},{8,11},{9,8},{10,9... | collective-permute-start | bytes 983048 | tf_op jit(solution)/shard_map/ppermute | solution.py:291
  79.9 0.9 collective-permute-start.9
  80.8 0.8 pad_maximum_fusion.1
  81.6 6.9 %all-to-all-start.2 = ((bf16[8,80,256]{2,1,0:T(8,128)(2,1)}), bf16[8,80,256]{2,1,0:T(8,128)(2,1)S(1)}, u32[]{:S(2)}, u32[]{:S(2)}) async-start(bf16[8,80,256]{2,1,0:T(8,128)(2,1)} %bitcast.59), calls=%async_computation.2 | async-start | bytes 655360 | tf_op jit(solution)/shard_map/all_to_all | solution.py:298
  88.5 4.7 %collective-permute-done.7 = bf16[640,256]{1,0:T(8,128)(2,1)} collective-permute-done((bf16[640,256]{1,0:T(8,128)(2,1)}, bf16[640,256]{1,0:T(8,128)(2,1)}, u32[]{:S(2)}, u32[]{:S(2)}) %collective-permute-start.7) | collective-permute-done | bytes 327712 | tf_op jit(solution)/shard_map/ppermute | solution.py:291
  93.2 3.4 %collective-permute-done.9 = bf16[640,256]{1,0:T(8,128)(2,1)} collective-permute-done((bf16[640,256]{1,0:T(8,128)(2,1)}, bf16[640,256]{1,0:T(8,128)(2,1)}, u32[]{:S(2)}, u32[]{:S(2)}) %collective-permute-start.9) | collective-permute-done | bytes 327712 | tf_op jit(solution)/shard_map/ppermute | solution.py:291
  96.7 1.5 convert_add_fusion
  98.7 0.8 pad_maximum_fusion.2.dkv_ref
  99.5 0.4 all-to-all-done.2.first_ref
  99.9 6.2 %all-to-all-start.3 = ((bf16[8,80,256]{2,1,0:T(8,128)(2,1)}), bf16[8,80,256]{2,1,0:T(8,128)(2,1)S(1)}, u32[]{:S(2)}, u32[]{:S(2)}) async-start(bf16[8,80,256]{2,1,0:T(8,128)(2,1)} %bitcast.6), calls=%async_computation.3 | async-start | bytes 655360 | tf_op jit(solution)/shard_map/all_to_all | solution.py:298
  106.2 2.0 %fusion.13 = (bf16[640,1024]{1,0:T(8,128)(2,1)S(1)}, bf16[640,1024]{1,0:T(8,128)(2,1)S(1)}) fusion(bf16[640,2048]{1,0:T(8,128)(2,1)} %all-gather.2.cloned.1.call-done), kind=kLoop, calls=%fused_computation.37 | loop fusion | bytes 5242880 | tf_op jit(solution)/shard_map/slice | solution.py:315
  108.1 3.1 %head_grads.1 = bf16[4,8,32,512]{3,2,1,0:T(8,128)(2,1)} custom-call(bf16[640,1024]{1,0:T(8,128)(2,1)S(1)} %get-tuple-element.92.normed_ref, bf16[640,128]{1,0:T(8,128)(2,1)S(1)} %get-tuple-element.54.dq_ref, bf16[640,256]{1,0:T(8,128)(2,1)} %pad_maximum_fusion.2.dkv_ref, bf16[640,128]{1,0:T(8,128)(2,1)S(1)} %get-tuple-element.53.attended_ref, ...), custom_call_target="tpu_custom_call" | custom-call | tf_op jit(solution)/shard_map/head_grads/pallas_call | solution.py:168
  111.3 8.0 %all-to-all-done.3.second_ref = bf16[8,80,256]{2,1,0:T(8,128)(2,1)S(1)} async-done(((bf16[8,80,256]{2,1,0:T(8,128)(2,1)}), bf16[8,80,256]{2,1,0:T(8,128)(2,1)S(1)}, u32[]{:S(2)}, u32[]{:S(2)}) %all-to-all-start.3) | async-done | bytes 327712 | tf_op jit(solution)/shard_map/all_to_all | solution.py:298
  119.4 2.8 %copy-done.1 = bf16[1024,3072]{1,0:T(8,128)(2,1)S(1)} copy-done((bf16[1024,3072]{1,0:T(8,128)(2,1)S(1)}, bf16[1024,3072]{1,0:T(8,128)(2,1)}, u32[]{:S(2)}) %copy-start.1) | copy-done | bytes 6291480
  122.1 2.2 %hidden_grad.1 = (bf16[80,1024]{1,0:T(8,128)(2,1)S(1)}, bf16[80,256]{1,0:T(8,128)(2,1)S(1)}, bf16[80,256]{1,0:T(8,128)(2,1)S(1)}, bf16[80,256]{1,0:T(8,128)(2,1)S(1)}, bf16[80,256]{1,0:T(8,128)(2,1)S(1)}) custom-call(s32[1]{0:T(128)} %bitcast.3.y_ref, bf16[8,80,256]{2,1,0:T(8,128)(2,1)S(1)} %all-to-all-done.2.first_ref, ...), custom_call_target="tpu_custom_call" | custom-call | tf_op jit(solution)/shard_map/hidden_grad/pallas_call | solution.py:138
  124.4 0.6 copy-done.5
  125.0 1.0 collective-permute-start.11
  126.0 2.6 %collective-permute-start.12 = (bf16[80,256]{1,0:T(8,128)(2,1)S(1)}, bf16[80,256]{1,0:T(8,128)(2,1)S(1)}, u32[]{:S(2)}, u32[]{:S(2)}) collective-permute-start(bf16[80,256]{1,0:T(8,128)(2,1)S(1)} %get-tuple-element.66), channel_id=1, source_target_pairs={{0,3},{1,0},{2,1},{3,2},{4,7},{5,4},{6,5},{7,6},{8,11},{9,8},{10,9... | collective-permute-start | bytes 122888 | tf_op jit(solution)/shard_map/ppermute | solution.py:291
  128.5 0.8 convolution_convert_fusion.1
  129.4 2.0 %collective-permute-done.10.refs_5_ = bf16[80,256]{1,0:T(8,128)(2,1)S(1)} collective-permute-done((bf16[80,256]{1,0:T(8,128)(2,1)S(1)}, bf16[80,256]{1,0:T(8,128)(2,1)S(1)}, u32[]{:S(2)}, u32[]{:S(2)}) %collective-permute-start.10) | collective-permute-done | bytes 40992 | tf_op jit(solution)/shard_map/ppermute | solution.py:291
  131.5 1.1 collective-permute-done.12.refs_7_
  132.6 0.6 copy-done.10
  133.2 2.5 %short_grads.1 = bf16[32,64,128]{2,1,0:T(8,128)(2,1)} custom-call(bf16[80,1024]{1,0:T(8,128)(2,1)} %copy-done.6, bf16[80,1024]{1,0:T(8,128)(2,1)} %collective-permute-done.1.refs_1_, bf16[80,1024]{1,0:T(8,128)(2,1)} %collective-permute-done.2.refs_2_, bf16[80,1024]{1,0:T(8,128)(2,1)} %collective-permute-done.3.refs_3_, bf16[80,256]{1,0:T(8,128)(2,1)} %copy-done.5, ...), custom_call_target="tpu_custom_call" | custom-call | tf_op jit(solution)/shard_map/short_grads/pallas_call | solution.py:218
  135.7 4.8 %all-to-all-start.4 = ((bf16[32,64,128]{2,1,0:T(8,128)(2,1)}), bf16[32,64,128]{2,1,0:T(8,128)(2,1)}, u32[]{:S(2)}, u32[]{:S(2)}) async-start(bf16[32,64,128]{2,1,0:T(8,128)(2,1)} %short_grads.1), calls=%async_computation.4 | async-start | bytes 1048576 | tf_op jit(solution)/shard_map/all_to_all | solution.py:343
  140.5 2.1 %fusion.8 = f32[80,1024]{1,0:T(8,128)S(1)} fusion(bf16[1024,1024]{1,0:T(8,128)(2,1)} %param.8, bf16[8,80,256]{2,1,0:T(8,128)(2,1)S(1)} %all-to-all-done.2.first_ref), kind=kOutput, calls=%fused_computation.23 | convolution fusion | flops 167772160 | bytes 2588672 | tf_op jit(solution)/shard_map/dot_general | solution.py:21
  142.7 1.3 collective-permute-start.13
  144.0 1.7 split_parts.1
  145.7 4.9 %collective-permute-start.14 = (bf16[32,384]{1,0:T(8,128)(2,1)}, bf16[32,384]{1,0:T(8,128)(2,1)S(1)}, u32[]{:S(2)}, u32[]{:S(2)}) collective-permute-start(bf16[32,384]{1,0:T(8,128)(2,1)} %get-tuple-element.77), channel_id=1, source_target_pairs={{0,4},{4,8},{8,12},{12,16},{16,20},{20,24},{24,28},{28,0},{1,5},{5... | collective-permute-start | bytes 73736 | tf_op jit(solution)/shard_map/ppermute | solution.py:347
  150.6 2.4 %collective-permute-start.15 = (bf16[32,384]{1,0:T(8,128)(2,1)}, bf16[32,384]{1,0:T(8,128)(2,1)S(1)}, u32[]{:S(2)}, u32[]{:S(2)}) collective-permute-start(bf16[32,384]{1,0:T(8,128)(2,1)} %get-tuple-element.78), channel_id=1, source_target_pairs={{0,8},{4,12},{8,16},{12,20},{16,24},{20,28},{24,0},{28,4},{1,9},{5... | collective-permute-start | bytes 73736 | tf_op jit(solution)/shard_map/ppermute | solution.py:347
  153.0 0.7 add_convert_fusion
  153.7 3.7 %collective-permute-start.16 = (bf16[32,384]{1,0:T(8,128)(2,1)}, bf16[32,384]{1,0:T(8,128)(2,1)S(1)}, u32[]{:S(2)}, u32[]{:S(2)}) collective-permute-start(bf16[32,384]{1,0:T(8,128)(2,1)} %get-tuple-element.79), channel_id=1, source_target_pairs={{0,12},{4,16},{8,20},{12,24},{16,28},{20,0},{24,4},{28,8},{1,13},{... | collective-permute-start | bytes 73736 | tf_op jit(solution)/shard_map/ppermute | solution.py:347
  157.5 1.4 collective-permute-start.17
  158.8 3.7 %collective-permute-start.18 = (bf16[32,384]{1,0:T(8,128)(2,1)}, bf16[32,384]{1,0:T(8,128)(2,1)S(1)}, u32[]{:S(2)}, u32[]{:S(2)}) collective-permute-start(bf16[32,384]{1,0:T(8,128)(2,1)} %get-tuple-element.81), channel_id=1, source_target_pairs={{0,20},{4,24},{8,28},{12,0},{16,4},{20,8},{24,12},{28,16},{1,21},{... | collective-permute-start | bytes 73736 | tf_op jit(solution)/shard_map/ppermute | solution.py:347
  162.5 3.5 %collective-permute-start.19 = (bf16[32,384]{1,0:T(8,128)(2,1)}, bf16[32,384]{1,0:T(8,128)(2,1)S(1)}, u32[]{:S(2)}, u32[]{:S(2)}) collective-permute-start(bf16[32,384]{1,0:T(8,128)(2,1)} %get-tuple-element.82), channel_id=1, source_target_pairs={{0,24},{4,28},{8,0},{12,4},{16,8},{20,12},{24,16},{28,20},{1,25},{... | collective-permute-start | bytes 73736 | tf_op jit(solution)/shard_map/ppermute | solution.py:347
  166.1 0.5 collective-permute-start.20
  166.6 1.6 add_convert_fusion.1
  168.3 1.8 %collective-permute-done.20.refs_7_ = bf16[32,384]{1,0:T(8,128)(2,1)S(1)} collective-permute-done((bf16[32,384]{1,0:T(8,128)(2,1)}, bf16[32,384]{1,0:T(8,128)(2,1)S(1)}, u32[]{:S(2)}, u32[]{:S(2)}) %collective-permute-start.20) | collective-permute-done | bytes 24608 | tf_op jit(solution)/shard_map/ppermute | solution.py:347
  170.1 0.6 copy-done.17
  170.7 1.6 assemble_attend.1
  172.4 1.8 assemble_short.1
  (77 shorter events, 2.6 us)
Async XLA Ops:
  7.2 6.7 %copy-start = (bf16[1024,1024]{1,0:T(8,128)(2,1)S(1)}, bf16[1024,1024]{1,0:T(8,128)(2,1)}, u32[]{:S(2)}) copy-start(bf16[1024,1024]{1,0:T(8,128)(2,1)} %param.6) | copy-start | bytes 6291460
  8.0 4.8 %collective-permute-start = (bf16[3,256]{1,0:T(4,128)(2,1)S(1)}, bf16[3,256]{1,0:T(4,128)(2,1)S(1)}, u32[]{:S(2)}, u32[]{:S(2)}) collective-permute-start(bf16[3,256]{1,0:T(4,128)(2,1)S(1)} %slice.40), channel_id=1, source_target_pairs={{0,1},{1,2},{2,3},{3,4},{4,5},{5,6},{6,7},{7,8},{8,9},{9,10},{10,1... | collective-permute-start | bytes 4616 | tf_op jit(solution)/shard_map/ppermute | solution.py:301
  13.9 22.3 %copy-start.6 = (bf16[80,1024]{1,0:T(8,128)(2,1)}, bf16[80,1024]{1,0:T(8,128)(2,1)S(1)}, u32[]{:S(2)}) copy-start(bf16[80,1024]{1,0:T(8,128)(2,1)S(1)} %reshape.82.refs_0_) | copy-start | bytes 491524
  20.0 25.0 %all-to-all-start = ((bf16[8,80,256]{2,1,0:T(8,128)(2,1)}), bf16[8,80,256]{2,1,0:T(8,128)(2,1)S(1)}, u32[]{:S(2)}, u32[]{:S(2)}) async-start(bf16[8,80,256]{2,1,0:T(8,128)(2,1)} %reshape.83), calls=%async_computation | async-start | bytes 655360 | tf_op jit(solution)/shard_map/all_to_all | solution.py:298
  32.5 73.7 %all-gather.2.cloned.1.call-start = ((), (), s32[]{:S(2)}) async-start(), calls=%async_computation.6 | async-start | bytes 2949120 | tf_op jit(solution)/shard_map/all_gather | solution.py:314
  35.0 9.4 %collective-permute-start.1 = (bf16[80,1024]{1,0:T(8,128)(2,1)S(1)}, bf16[80,1024]{1,0:T(8,128)(2,1)}, u32[]{:S(2)}, u32[]{:S(2)}) collective-permute-start(bf16[80,1024]{1,0:T(8,128)(2,1)S(1)} %reshape.82.refs_0_), channel_id=1, source_target_pairs={{0,1},{1,2},{2,3},{3,0},{4,5},{5,6},{6,7},{7,4},{8,9},{9,10},{10,1... | collective-permute-start | bytes 491528 | tf_op jit(solution)/shard_map/ppermute | solution.py:291
  35.0 9.3 %collective-permute-start.2 = (bf16[80,1024]{1,0:T(8,128)(2,1)S(1)}, bf16[80,1024]{1,0:T(8,128)(2,1)}, u32[]{:S(2)}, u32[]{:S(2)}) collective-permute-start(bf16[80,1024]{1,0:T(8,128)(2,1)S(1)} %reshape.82.refs_0_), channel_id=1, source_target_pairs={{0,2},{1,3},{2,0},{3,1},{4,6},{5,7},{6,4},{7,5},{8,10},{9,11},{10,... | collective-permute-start | bytes 491528 | tf_op jit(solution)/shard_map/ppermute | solution.py:291
  36.2 8.8 %collective-permute-start.3 = (bf16[80,1024]{1,0:T(8,128)(2,1)S(1)}, bf16[80,1024]{1,0:T(8,128)(2,1)}, u32[]{:S(2)}, u32[]{:S(2)}) collective-permute-start(bf16[80,1024]{1,0:T(8,128)(2,1)S(1)} %reshape.82.refs_0_), channel_id=1, source_target_pairs={{0,3},{1,0},{2,1},{3,2},{4,7},{5,4},{6,5},{7,6},{8,11},{9,8},{10,9... | collective-permute-start | bytes 491528 | tf_op jit(solution)/shard_map/ppermute | solution.py:291
  45.0 22.4 %all-to-all-start.1 = ((bf16[8,80,256]{2,1,0:T(8,128)(2,1)}), bf16[8,80,256]{2,1,0:T(8,128)(2,1)S(1)}, u32[]{:S(2)}, u32[]{:S(2)}) async-start(bf16[8,80,256]{2,1,0:T(8,128)(2,1)} %reshape.86), calls=%async_computation.1 | async-start | bytes 655360 | tf_op jit(solution)/shard_map/all_to_all | solution.py:298
  52.0 11.8 %collective-permute-start.4 = (bf16[640,256]{1,0:T(8,128)(2,1)S(1)}, bf16[640,256]{1,0:T(8,128)(2,1)S(1)}, u32[]{:S(2)}, u32[]{:S(2)}) collective-permute-start(bf16[640,256]{1,0:T(8,128)(2,1)S(1)} %bitcast.51), channel_id=1, source_target_pairs={{0,1},{1,2},{2,3},{3,0},{4,5},{5,6},{6,7},{7,4},{8,9},{9,10},{10,1... | collective-permute-start | bytes 983048 | tf_op jit(solution)/shard_map/ppermute | solution.py:291
  52.2 15.3 %collective-permute-start.5 = (bf16[640,256]{1,0:T(8,128)(2,1)S(1)}, bf16[640,256]{1,0:T(8,128)(2,1)}, u32[]{:S(2)}, u32[]{:S(2)}) collective-permute-start(bf16[640,256]{1,0:T(8,128)(2,1)S(1)} %bitcast.52), channel_id=1, source_target_pairs={{0,2},{1,3},{2,0},{3,1},{4,6},{5,7},{6,4},{7,5},{8,10},{9,11},{10,... | collective-permute-start | bytes 983048 | tf_op jit(solution)/shard_map/ppermute | solution.py:291
  55.7 11.7 %collective-permute-start.6 = (bf16[640,256]{1,0:T(8,128)(2,1)S(1)}, bf16[640,256]{1,0:T(8,128)(2,1)}, u32[]{:S(2)}, u32[]{:S(2)}) collective-permute-start(bf16[640,256]{1,0:T(8,128)(2,1)S(1)} %bitcast.53), channel_id=1, source_target_pairs={{0,3},{1,0},{2,1},{3,2},{4,7},{5,4},{6,5},{7,6},{8,11},{9,8},{10,9... | collective-permute-start | bytes 983048 | tf_op jit(solution)/shard_map/ppermute | solution.py:291
  63.8 0.7 copy-start.3
  67.4 1.0 copy-start.4
  76.7 0.8 copy-start.2
  77.6 15.7 %collective-permute-start.7 = (bf16[640,256]{1,0:T(8,128)(2,1)}, bf16[640,256]{1,0:T(8,128)(2,1)}, u32[]{:S(2)}, u32[]{:S(2)}) collective-permute-start(bf16[640,256]{1,0:T(8,128)(2,1)} %get-tuple-element.56), channel_id=1, source_target_pairs={{0,3},{1,0},{2,1},{3,2},{4,7},{5,4},{6,5},{7,6},{8,11},{9,8},{10,9... | collective-permute-start | bytes 983048 | tf_op jit(solution)/shard_map/ppermute | solution.py:291
  79.9 13.3 %collective-permute-start.8 = (bf16[640,256]{1,0:T(8,128)(2,1)}, bf16[640,256]{1,0:T(8,128)(2,1)}, u32[]{:S(2)}, u32[]{:S(2)}) collective-permute-start(bf16[640,256]{1,0:T(8,128)(2,1)} %get-tuple-element.57), channel_id=1, source_target_pairs={{0,2},{1,3},{2,0},{3,1},{4,6},{5,7},{6,4},{7,5},{8,10},{9,11},{10,... | collective-permute-start | bytes 983048 | tf_op jit(solution)/shard_map/ppermute | solution.py:291
  79.9 16.7 %collective-permute-start.9 = (bf16[640,256]{1,0:T(8,128)(2,1)}, bf16[640,256]{1,0:T(8,128)(2,1)}, u32[]{:S(2)}, u32[]{:S(2)}) collective-permute-start(bf16[640,256]{1,0:T(8,128)(2,1)} %get-tuple-element.58), channel_id=1, source_target_pairs={{0,1},{1,2},{2,3},{3,0},{4,5},{5,6},{6,7},{7,4},{8,9},{9,10},{10,1... | collective-permute-start | bytes 983048 | tf_op jit(solution)/shard_map/ppermute | solution.py:291
  81.6 18.4 %all-to-all-start.2 = ((bf16[8,80,256]{2,1,0:T(8,128)(2,1)}), bf16[8,80,256]{2,1,0:T(8,128)(2,1)S(1)}, u32[]{:S(2)}, u32[]{:S(2)}) async-start(bf16[8,80,256]{2,1,0:T(8,128)(2,1)} %bitcast.59), calls=%async_computation.2 | async-start | bytes 655360 | tf_op jit(solution)/shard_map/all_to_all | solution.py:298
  99.9 19.3 %all-to-all-start.3 = ((bf16[8,80,256]{2,1,0:T(8,128)(2,1)}), bf16[8,80,256]{2,1,0:T(8,128)(2,1)S(1)}, u32[]{:S(2)}, u32[]{:S(2)}) async-start(bf16[8,80,256]{2,1,0:T(8,128)(2,1)} %bitcast.6), calls=%async_computation.3 | async-start | bytes 655360 | tf_op jit(solution)/shard_map/all_to_all | solution.py:298
  106.1 37.9 %reduce-scatter.2.cloned.1.call-start = ((), (), s32[]{:S(2)}) async-start(), calls=%async_computation.7 | async-start | bytes 1310720 | tf_op jit(solution)/shard_map/reduce_scatter | solution.py:336
  119.4 2.8 %copy-start.1 = (bf16[1024,3072]{1,0:T(8,128)(2,1)S(1)}, bf16[1024,3072]{1,0:T(8,128)(2,1)}, u32[]{:S(2)}) copy-start(bf16[1024,3072]{1,0:T(8,128)(2,1)} %weight_ref.1) | copy-start | bytes 18874372
  124.3 0.6 copy-start.5
  125.0 6.5 %collective-permute-start.10 = (bf16[80,256]{1,0:T(8,128)(2,1)S(1)}, bf16[80,256]{1,0:T(8,128)(2,1)S(1)}, u32[]{:S(2)}, u32[]{:S(2)}) collective-permute-start(bf16[80,256]{1,0:T(8,128)(2,1)S(1)} %get-tuple-element.64), channel_id=1, source_target_pairs={{0,1},{1,2},{2,3},{3,0},{4,5},{5,6},{6,7},{7,4},{8,9},{9,10},{10,1... | collective-permute-start | bytes 122888 | tf_op jit(solution)/shard_map/ppermute | solution.py:291
  125.0 6.5 %collective-permute-start.11 = (bf16[80,256]{1,0:T(8,128)(2,1)S(1)}, bf16[80,256]{1,0:T(8,128)(2,1)S(1)}, u32[]{:S(2)}, u32[]{:S(2)}) collective-permute-start(bf16[80,256]{1,0:T(8,128)(2,1)S(1)} %get-tuple-element.65), channel_id=1, source_target_pairs={{0,2},{1,3},{2,0},{3,1},{4,6},{5,7},{6,4},{7,5},{8,10},{9,11},{10,... | collective-permute-start | bytes 122888 | tf_op jit(solution)/shard_map/ppermute | solution.py:291
  126.0 6.6 %collective-permute-start.12 = (bf16[80,256]{1,0:T(8,128)(2,1)S(1)}, bf16[80,256]{1,0:T(8,128)(2,1)S(1)}, u32[]{:S(2)}, u32[]{:S(2)}) collective-permute-start(bf16[80,256]{1,0:T(8,128)(2,1)S(1)} %get-tuple-element.66), channel_id=1, source_target_pairs={{0,3},{1,0},{2,1},{3,2},{4,7},{5,4},{6,5},{7,6},{8,11},{9,8},{10,9... | collective-permute-start | bytes 122888 | tf_op jit(solution)/shard_map/ppermute | solution.py:291
  131.5 1.1 copy-start.8
  131.5 1.1 copy-start.9
  132.6 0.6 copy-start.10
  135.7 17.3 %copy-start.7 = (bf16[320,256]{1,0:T(8,128)(2,1)S(1)}, bf16[320,256]{1,0:T(8,128)(2,1)}, u32[]{:S(2)}) copy-start(bf16[320,256]{1,0:T(8,128)(2,1)} %param.5) | copy-start | bytes 491524
  135.7 36.7 %all-to-all-start.4 = ((bf16[32,64,128]{2,1,0:T(8,128)(2,1)}), bf16[32,64,128]{2,1,0:T(8,128)(2,1)}, u32[]{:S(2)}, u32[]{:S(2)}) async-start(bf16[32,64,128]{2,1,0:T(8,128)(2,1)} %short_grads.1), calls=%async_computation.4 | async-start | bytes 1048576 | tf_op jit(solution)/shard_map/all_to_all | solution.py:343
  142.7 16.2 %collective-permute-start.13 = (bf16[3,256]{1,0:T(4,128)(2,1)S(1)}, bf16[3,256]{1,0:T(4,128)(2,1)S(1)}, u32[]{:S(2)}, u32[]{:S(2)}) collective-permute-start(bf16[3,256]{1,0:T(4,128)(2,1)S(1)} %slice.51), channel_id=1, source_target_pairs={{1,0},{2,1},{3,2},{4,3},{5,4},{6,5},{7,6},{8,7},{9,8},{10,9},{11,1... | collective-permute-start | bytes 4616 | tf_op jit(solution)/shard_map/ppermute | solution.py:356
  145.7 16.9 %collective-permute-start.14 = (bf16[32,384]{1,0:T(8,128)(2,1)}, bf16[32,384]{1,0:T(8,128)(2,1)S(1)}, u32[]{:S(2)}, u32[]{:S(2)}) collective-permute-start(bf16[32,384]{1,0:T(8,128)(2,1)} %get-tuple-element.77), channel_id=1, source_target_pairs={{0,4},{4,8},{8,12},{12,16},{16,20},{20,24},{24,28},{28,0},{1,5},{5... | collective-permute-start | bytes 73736 | tf_op jit(solution)/shard_map/ppermute | solution.py:347
  150.6 15.5 %collective-permute-start.15 = (bf16[32,384]{1,0:T(8,128)(2,1)}, bf16[32,384]{1,0:T(8,128)(2,1)S(1)}, u32[]{:S(2)}, u32[]{:S(2)}) collective-permute-start(bf16[32,384]{1,0:T(8,128)(2,1)} %get-tuple-element.78), channel_id=1, source_target_pairs={{0,8},{4,12},{8,16},{12,20},{16,24},{20,28},{24,0},{28,4},{1,9},{5... | collective-permute-start | bytes 73736 | tf_op jit(solution)/shard_map/ppermute | solution.py:347
  153.7 14.5 %collective-permute-start.16 = (bf16[32,384]{1,0:T(8,128)(2,1)}, bf16[32,384]{1,0:T(8,128)(2,1)S(1)}, u32[]{:S(2)}, u32[]{:S(2)}) collective-permute-start(bf16[32,384]{1,0:T(8,128)(2,1)} %get-tuple-element.79), channel_id=1, source_target_pairs={{0,12},{4,16},{8,20},{12,24},{16,28},{20,0},{24,4},{28,8},{1,13},{... | collective-permute-start | bytes 73736 | tf_op jit(solution)/shard_map/ppermute | solution.py:347
  157.5 10.8 %collective-permute-start.17 = (bf16[32,384]{1,0:T(8,128)(2,1)}, bf16[32,384]{1,0:T(8,128)(2,1)S(1)}, u32[]{:S(2)}, u32[]{:S(2)}) collective-permute-start(bf16[32,384]{1,0:T(8,128)(2,1)} %get-tuple-element.80), channel_id=1, source_target_pairs={{0,16},{4,20},{8,24},{12,28},{16,0},{20,4},{24,8},{28,12},{1,17},{... | collective-permute-start | bytes 73736 | tf_op jit(solution)/shard_map/ppermute | solution.py:347
  158.8 9.4 %collective-permute-start.18 = (bf16[32,384]{1,0:T(8,128)(2,1)}, bf16[32,384]{1,0:T(8,128)(2,1)S(1)}, u32[]{:S(2)}, u32[]{:S(2)}) collective-permute-start(bf16[32,384]{1,0:T(8,128)(2,1)} %get-tuple-element.81), channel_id=1, source_target_pairs={{0,20},{4,24},{8,28},{12,0},{16,4},{20,8},{24,12},{28,16},{1,21},{... | collective-permute-start | bytes 73736 | tf_op jit(solution)/shard_map/ppermute | solution.py:347
  162.5 7.6 %copy-start.11 = (bf16[32,384]{1,0:T(8,128)(2,1)}, bf16[32,384]{1,0:T(8,128)(2,1)S(1)}, u32[]{:S(2)}) copy-start(bf16[32,384]{1,0:T(8,128)(2,1)S(1)} %collective-permute-done.14.refs_1_) | copy-start | bytes 73732
  162.5 5.7 %collective-permute-start.19 = (bf16[32,384]{1,0:T(8,128)(2,1)}, bf16[32,384]{1,0:T(8,128)(2,1)S(1)}, u32[]{:S(2)}, u32[]{:S(2)}) collective-permute-start(bf16[32,384]{1,0:T(8,128)(2,1)} %get-tuple-element.82), channel_id=1, source_target_pairs={{0,24},{4,28},{8,0},{12,4},{16,8},{20,12},{24,16},{28,20},{1,25},{... | collective-permute-start | bytes 73736 | tf_op jit(solution)/shard_map/ppermute | solution.py:347
  166.1 4.0 %copy-start.12 = (bf16[32,384]{1,0:T(8,128)(2,1)}, bf16[32,384]{1,0:T(8,128)(2,1)S(1)}, u32[]{:S(2)}) copy-start(bf16[32,384]{1,0:T(8,128)(2,1)S(1)} %collective-permute-done.15.refs_2_) | copy-start | bytes 73732
  166.1 4.0 %collective-permute-start.20 = (bf16[32,384]{1,0:T(8,128)(2,1)}, bf16[32,384]{1,0:T(8,128)(2,1)S(1)}, u32[]{:S(2)}, u32[]{:S(2)}) collective-permute-start(bf16[32,384]{1,0:T(8,128)(2,1)} %get-tuple-element.83), channel_id=1, source_target_pairs={{0,28},{4,0},{8,4},{12,8},{16,12},{20,16},{24,20},{28,24},{1,29},{... | collective-permute-start | bytes 73736 | tf_op jit(solution)/shard_map/ppermute | solution.py:347
  168.2 1.9 %copy-start.13 = (bf16[32,384]{1,0:T(8,128)(2,1)}, bf16[32,384]{1,0:T(8,128)(2,1)S(1)}, u32[]{:S(2)}) copy-start(bf16[32,384]{1,0:T(8,128)(2,1)S(1)} %collective-permute-done.16.refs_3_) | copy-start | bytes 73732
  168.2 1.9 %copy-start.14 = (bf16[32,384]{1,0:T(8,128)(2,1)}, bf16[32,384]{1,0:T(8,128)(2,1)S(1)}, u32[]{:S(2)}) copy-start(bf16[32,384]{1,0:T(8,128)(2,1)S(1)} %collective-permute-done.17.refs_4_) | copy-start | bytes 73732
  168.3 1.9 %copy-start.15 = (bf16[32,384]{1,0:T(8,128)(2,1)}, bf16[32,384]{1,0:T(8,128)(2,1)S(1)}, u32[]{:S(2)}) copy-start(bf16[32,384]{1,0:T(8,128)(2,1)S(1)} %collective-permute-done.18.refs_5_) | copy-start | bytes 73732
  168.3 1.9 %copy-start.16 = (bf16[32,384]{1,0:T(8,128)(2,1)}, bf16[32,384]{1,0:T(8,128)(2,1)S(1)}, u32[]{:S(2)}) copy-start(bf16[32,384]{1,0:T(8,128)(2,1)S(1)} %collective-permute-done.19.refs_6_) | copy-start | bytes 73732
  170.1 0.6 copy-start.17
Sparse Core Ops, SparseCore 0:
  45.1 43.6 all-gather.1
  119.4 20.8 reduce-scatter.1

commit v3 on v2

--- a/solution.py
+++ b/solution.py
@@ -146,11 +146,12 @@
     )(y, first, second, weight, normed, scale)
 
 
-def head_grads_body(normed_ref, dq_ref, dkv_ref, attended_ref, expand_ref, out_ref):
+def head_grads_body(gathered_ref, dq_ref, dkv_ref, attended_ref, out_ref):
     shards, groups, own_rows, width = out_ref.shape
+    model_width = groups * shards * own_rows
     d_head = jnp.concatenate([dq_ref[...], dkv_ref[...]], axis=1)
-    attend = mm(normed_ref[...], d_head, TN).astype(out_ref.dtype)
-    expand = mm(attended_ref[...], expand_ref[...], TN).astype(out_ref.dtype)
+    attend = mm(gathered_ref[:, gathered_ref.shape[1] - model_width :], d_head, TN).astype(out_ref.dtype)
+    expand = mm(attended_ref[...], gathered_ref[:, : gathered_ref.shape[1] - model_width], TN).astype(out_ref.dtype)
     head_width = d_head.shape[1]
     lanes = width - head_width
     for shard in range(shards):
@@ -161,18 +162,17 @@
             out_ref[shard, group, :, head_width:] = piece
 
 
-def head_grads(normed, d_query, d_kv, attended, d_expand, groups, shards):
-    model_width = normed.shape[1]
-    width = 3 * d_query.shape[1] + d_expand.shape[1] // groups
+def head_grads(gathered, d_query, d_kv, attended, model_width, groups, shards):
+    width = 3 * d_query.shape[1] + (gathered.shape[1] - model_width) // groups
     vmem = pl.BlockSpec(memory_space=pltpu.VMEM)
     return pl.pallas_call(
         head_grads_body,
         out_shape=jax.ShapeDtypeStruct((shards, groups, model_width // groups // shards, width), jnp.bfloat16),
-        in_specs=[vmem] * 5,
+        in_specs=[vmem] * 4,
         out_specs=vmem,
         compiler_params=pltpu.CompilerParams(vmem_limit_bytes=24 * 1024 * 1024),
         name="head_grads",
-    )(normed, d_query, d_kv, attended, d_expand)
+    )(gathered, d_query, d_kv, attended)
 
 
 def split_parts_body(z_ref, parts_ref, expand_ref, *piece_refs):
@@ -312,7 +312,6 @@
     grouped_y = [grouped] + [turn_y(grouped, step) for step in range(1, y_size)]
     kv, qd, gathered, *grouped_y = tie(kv, qd, jnp.concatenate([d_expand, normed_b], axis=1), *grouped_y)
     gathered = lax.all_gather(gathered, "z", axis=0, tiled=True)
-    d_expand_all, normed_all = gathered[:, : 4 * byte_width], gathered[:, 4 * byte_width :]
     kvs = [kv] + [turn_y(kv, step) for step in range(1, y_size)]
     qd = swap(qd).reshape(rows, 2 * head_size)
     y = lax.axis_index("y").astype(jnp.int32).reshape(1)
@@ -330,9 +329,9 @@
         [norm_back(key_unit, key_scale, total[:, :head_size]), total[:, head_size:]], axis=1
     ).astype(jnp.bfloat16)
     first_back, d_kv = tie(first_back, d_kv)
+    parts = head_grads(gathered, d_query, d_kv, attended, model_width, z_size, y_size)
+    parts, d_kv = tie(parts, d_kv)
     second_back = swap(d_kv.reshape(HEADS, short_rows, 2 * head_size))
-    parts = head_grads(normed_all, d_query, d_kv, attended, d_expand_all, z_size, y_size)
-    second_back, parts = tie(second_back, parts)
     parts = lax.psum_scatter(parts, "y", scatter_dimension=0)
     d_hidden, *d_hidden_y = hidden_grad(y, first_back, second_back, w_attend, normed, hidden_scale, y_size)
     d_hidden_y = d_hidden_y[:1] + [turn_y(d_hidden_y[step], step) for step in range(1, y_size)]

time: 182 us -> 186 us (1.022)
  waiting for transfers between devices: 35.6 us -> 39.3 us
    all_to_all x4, waiting for transfers between devices: 8.4 us -> 14.3 us  [swap(): return lax.all_to_all(value, 'z', 0, 0)]
    ppermute x12, waiting for transfers between devices: 25.1 us -> 22.9 us  [turn_y(): lax.ppermute(value, 'y', [(i, (i + steps) % y_size) for i in range(y_size)])]
    ppermute x12, starting transfers between devices: 13.9 us -> 16 us  [turn_y(): lax.ppermute(value, 'y', [(i, (i + steps) % y_size) for i in range(y_size)])]
    all_to_all x4, starting transfers between devices: 32.6 us -> 30.5 us  [swap(): return lax.all_to_all(value, 'z', 0, 0)]
    slice x1 -> x0, local copies, waits for them, and re-layouts: 1.95 us -> none  [local(): gathered[:, :4 * byte_width]]
    unnamed x41 -> x43, local copies, waits for them, and re-layouts: 7.3 us -> 9.11 us
  transfers between devices with their start and end apart: 28 -> 28, of which waited for: 12 -> 12; matrix products, arithmetic and copies ran while one was open for 10% -> 9% of each run, Pallas kernels for 11% -> 9%
where the time goes in v3:
time: 186 us; the launch traced here: 185 us
  starting transfers between devices  76.3 us (41%)
  waiting for transfers between devices  39.3 us (21%)
  Pallas kernels  21.2 us (11%)
  local copies, waits for them, and re-layouts  15.7 us (8%)
  between operations  14.4 us (8%)
  matrix products  9.77 us (5%)
  other arithmetic  7.92 us (4%)
    all_to_all x4, starting transfers between devices, swap(): return lax.all_to_all(value, 'z', 0, 0)  30.5 us
    ppermute x12, waiting for transfers between devices, turn_y(): lax.ppermute(value, 'y', [(i, (i + steps) % y_size) for i in range(y_size)])  22.9 us
    ppermute x7, starting transfers between devices, local(): lax.ppermute(pieces[step], 'z', [(i, (i + step) % z_size) for i in range(...  20.2 us
    ppermute x12, starting transfers between devices, turn_y(): lax.ppermute(value, 'y', [(i, (i + steps) % y_size) for i in range(y_size)])  16 us
    all_to_all x4, waiting for transfers between devices, swap(): return lax.all_to_all(value, 'z', 0, 0)  14.3 us
    dot_general x5, matrix products, mm(): lax.dot_general(left, right, dims, preferred_element_type=jnp.float32)  9.77 us
    unnamed x43, local copies, waits for them, and re-layouts  9.11 us
    pallas_call x1, Pallas kernels, attention(): pl.pallas_call(functools.partial(attention_body, block, shards), out_shap...  8.31 us
  transfers between devices with their start and end apart: 28, of which 12 were waited for; matrix products, arithmetic and copies ran while one was open for 9% of the time, Pallas kernels for 9%

profile of v3, /device:TPU:6, one launch (start us, length us, event | category | flops | bytes accessed | tf_op | source)
XLA Modules:
  0.0 184.6 jit_solution(14820824122949175912)
XLA Ops:
  7.2 0.8 slice.34
  8.0 3.5 %collective-permute-start = (bf16[3,256]{1,0:T(4,128)(2,1)S(1)}, bf16[3,256]{1,0:T(4,128)(2,1)S(1)}, u32[]{:S(2)}, u32[]{:S(2)}) collective-permute-start(bf16[3,256]{1,0:T(4,128)(2,1)S(1)} %slice.34), channel_id=1, source_target_pairs={{0,1},{1,2},{2,3},{3,4},{4,5},{5,6},{6,7},{7,8},{8,9},{9,10},{10,1... | collective-permute-start | bytes 4616 | tf_op jit(solution)/shard_map/ppermute | solution.py:301
  11.5 1.0 reshape.85
  12.8 1.0 pad_maximum_fusion.3
  13.9 0.6 multiply_reduce_fusion
  14.6 4.0 %convolution_convert_fusion = bf16[80,3072]{1,0:T(8,128)(2,1)S(1)} fusion(bf16[80,1024]{1,0:T(8,128)(2,1)S(1)} %get-tuple-element.89, bf16[1024,3072]{1,0:T(8,128)(2,1)} %weight_ref.1), kind=kOutput, calls=%fused_computation | convolution fusion | flops 503562240 | bytes 6946816 | tf_op jit(solution)/shard_map/dot_general | solution.py:21
  18.7 0.3 copy.13
  19.1 0.9 reshape.83
  20.0 12.5 %all-to-all-start = ((bf16[8,80,256]{2,1,0:T(8,128)(2,1)}), bf16[8,80,256]{2,1,0:T(8,128)(2,1)S(1)}, u32[]{:S(2)}, u32[]{:S(2)}) async-start(bf16[8,80,256]{2,1,0:T(8,128)(2,1)} %reshape.83), calls=%async_computation | async-start | bytes 655360 | tf_op jit(solution)/shard_map/all_to_all | solution.py:298
  32.6 2.4 %fusion = bf16[10,8,8,128]{3,1,2,0:T(8,128)(2,1)S(1)} fusion(bf16[80,1024]{1,0:T(8,128)(2,1)S(1)} %reshape.85, bf16[1024,1024]{1,0:T(8,128)(2,1)} %param.8), kind=kOutput, calls=%fused_computation.3 | convolution fusion | flops 167854080 | bytes 2424832 | tf_op jit(solution)/shard_map/dot_general | solution.py:21
  35.0 1.1 collective-permute-start.2
  36.2 2.1 %collective-permute-start.3 = (bf16[80,1024]{1,0:T(8,128)(2,1)S(1)}, bf16[80,1024]{1,0:T(8,128)(2,1)}, u32[]{:S(2)}, u32[]{:S(2)}) collective-permute-start(bf16[80,1024]{1,0:T(8,128)(2,1)S(1)} %reshape.82.refs_0_), channel_id=1, source_target_pairs={{0,3},{1,0},{2,1},{3,2},{4,7},{5,4},{6,5},{7,6},{8,11},{9,8},{10,9... | collective-permute-start | bytes 491528 | tf_op jit(solution)/shard_map/ppermute | solution.py:291
  38.3 1.1 copy.14
  39.4 1.9 %reshape.86 = bf16[8,80,256]{2,1,0:T(8,128)(2,1)} reshape(bf16[8,80,2,128]{3,2,1,0:T(2,128)(2,1)} %copy.14) | data formatting | bytes 655360 | tf_op jit(solution)/shard_map/reshape | solution.py:295
  41.3 0.7 pad_maximum_fusion
  42.0 2.3 %collective-permute-done.1.refs_1_ = bf16[80,1024]{1,0:T(8,128)(2,1)} collective-permute-done((bf16[80,1024]{1,0:T(8,128)(2,1)S(1)}, bf16[80,1024]{1,0:T(8,128)(2,1)}, u32[]{:S(2)}, u32[]{:S(2)}) %collective-permute-start.1) | collective-permute-done | bytes 163872 | tf_op jit(solution)/shard_map/ppermute | solution.py:291
  44.4 0.6 collective-permute-done.3.refs_3_
  45.0 6.9 %all-to-all-start.1 = ((bf16[8,80,256]{2,1,0:T(8,128)(2,1)}), bf16[8,80,256]{2,1,0:T(8,128)(2,1)S(1)}, u32[]{:S(2)}, u32[]{:S(2)}) async-start(bf16[8,80,256]{2,1,0:T(8,128)(2,1)} %reshape.86), calls=%async_computation.1 | async-start | bytes 655360 | tf_op jit(solution)/shard_map/all_to_all | solution.py:298
  52.2 3.6 %collective-permute-start.5 = (bf16[640,256]{1,0:T(8,128)(2,1)S(1)}, bf16[640,256]{1,0:T(8,128)(2,1)}, u32[]{:S(2)}, u32[]{:S(2)}) collective-permute-start(bf16[640,256]{1,0:T(8,128)(2,1)S(1)} %bitcast.52), channel_id=1, source_target_pairs={{0,2},{1,3},{2,0},{3,1},{4,6},{5,7},{6,4},{7,5},{8,10},{9,11},{10,... | collective-permute-start | bytes 983048 | tf_op jit(solution)/shard_map/ppermute | solution.py:291
  55.9 7.9 %collective-permute-done.4.refs_1_ = bf16[640,256]{1,0:T(8,128)(2,1)S(1)} collective-permute-done((bf16[640,256]{1,0:T(8,128)(2,1)S(1)}, bf16[640,256]{1,0:T(8,128)(2,1)S(1)}, u32[]{:S(2)}, u32[]{:S(2)}) %collective-permute-start.4) | collective-permute-done | bytes 327712 | tf_op jit(solution)/shard_map/ppermute | solution.py:291
  63.8 0.7 copy-done.4
  64.5 2.9 %collective-permute-done.5.refs_2_ = bf16[640,256]{1,0:T(8,128)(2,1)} collective-permute-done((bf16[640,256]{1,0:T(8,128)(2,1)S(1)}, bf16[640,256]{1,0:T(8,128)(2,1)}, u32[]{:S(2)}, u32[]{:S(2)}) %collective-permute-start.5) | collective-permute-done | bytes 327712 | tf_op jit(solution)/shard_map/ppermute | solution.py:291
  67.4 1.0 copy-done.5
  68.4 8.3 %attention.1 = (bf16[640,128]{1,0:T(8,128)(2,1)S(1)}, bf16[640,128]{1,0:T(8,128)(2,1)S(1)}, f32[640,256]{1,0:T(8,128)S(1)}, bf16[640,256]{1,0:T(8,128)(2,1)}, bf...) custom-call(s32[1]{0:T(128)} %bitcast.3.y_ref, bf16[640,256]{1,0:T(8,128)(2,1)S(1)} %bitcast.58, ...), custom_call_target="tpu_custom_call" | custom-call | tf_op jit(solution)/shard_map/attention/pallas_call | solution.py:98
  76.7 0.8 copy-done.3
  77.6 3.8 %collective-permute-start.8 = (bf16[640,256]{1,0:T(8,128)(2,1)}, bf16[640,256]{1,0:T(8,128)(2,1)}, u32[]{:S(2)}, u32[]{:S(2)}) collective-permute-start(bf16[640,256]{1,0:T(8,128)(2,1)} %get-tuple-element.57), channel_id=1, source_target_pairs={{0,2},{1,3},{2,0},{3,1},{4,6},{5,7},{6,4},{7,5},{8,10},{9,11},{10,... | collective-permute-start | bytes 983048 | tf_op jit(solution)/shard_map/ppermute | solution.py:291
  81.4 0.8 pad_maximum_fusion.1
  82.2 6.9 %all-to-all-start.2 = ((bf16[8,80,256]{2,1,0:T(8,128)(2,1)}), bf16[8,80,256]{2,1,0:T(8,128)(2,1)S(1)}, u32[]{:S(2)}, u32[]{:S(2)}) async-start(bf16[8,80,256]{2,1,0:T(8,128)(2,1)} %bitcast.59), calls=%async_computation.2 | async-start | bytes 655360 | tf_op jit(solution)/shard_map/all_to_all | solution.py:298
  89.2 6.0 %collective-permute-done.8 = bf16[640,256]{1,0:T(8,128)(2,1)} collective-permute-done((bf16[640,256]{1,0:T(8,128)(2,1)}, bf16[640,256]{1,0:T(8,128)(2,1)}, u32[]{:S(2)}, u32[]{:S(2)}) %collective-permute-start.8) | collective-permute-done | bytes 327712 | tf_op jit(solution)/shard_map/ppermute | solution.py:291
  95.2 1.5 convert_add_fusion
  96.7 0.3 fusion.3
  97.2 0.8 pad_maximum_fusion.2.dkv_ref
  98.0 2.5 %all-to-all-done.2.first_ref = bf16[8,80,256]{2,1,0:T(8,128)(2,1)S(1)} async-done(((bf16[8,80,256]{2,1,0:T(8,128)(2,1)}), bf16[8,80,256]{2,1,0:T(8,128)(2,1)S(1)}, u32[]{:S(2)}, u32[]{:S(2)}) %all-to-all-start.2) | async-done | bytes 327712 | tf_op jit(solution)/shard_map/all_to_all | solution.py:298
  100.5 1.7 copy-done.2
  102.3 3.1 %head_grads.1 = bf16[4,8,32,512]{3,2,1,0:T(8,128)(2,1)} custom-call(bf16[640,2048]{1,0:T(8,128)(2,1)S(1)} %copy-done.2, bf16[640,128]{1,0:T(8,128)(2,1)S(1)} %get-tuple-element.54.dq_ref, bf16[640,256]{1,0:T(8,128)(2,1)} %pad_maximum_fusion.2.dkv_ref, bf16[640,128]{1,0:T(8,128)(2,1)S(1)} %get-tuple-element.53.attended_ref), custom_call_target="tpu_custom_call" | custom-call | tf_op jit(solution)/shard_map/head_grads/pallas_call | solution.py:168
  105.4 4.1 %all-to-all-start.3 = ((bf16[8,80,256]{2,1,0:T(8,128)(2,1)}), bf16[8,80,256]{2,1,0:T(8,128)(2,1)S(1)}, u32[]{:S(2)}, u32[]{:S(2)}) async-start(bf16[8,80,256]{2,1,0:T(8,128)(2,1)} %bitcast.6), calls=%async_computation.3 | async-start | bytes 655360 | tf_op jit(solution)/shard_map/all_to_all | solution.py:298
  109.6 11.7 %all-to-all-done.3.second_ref = bf16[8,80,256]{2,1,0:T(8,128)(2,1)S(1)} async-done(((bf16[8,80,256]{2,1,0:T(8,128)(2,1)}), bf16[8,80,256]{2,1,0:T(8,128)(2,1)S(1)}, u32[]{:S(2)}, u32[]{:S(2)}) %all-to-all-start.3) | async-done | bytes 327712 | tf_op jit(solution)/shard_map/all_to_all | solution.py:298
  121.4 2.9 %copy-done.1 = bf16[1024,3072]{1,0:T(8,128)(2,1)S(1)} copy-done((bf16[1024,3072]{1,0:T(8,128)(2,1)S(1)}, bf16[1024,3072]{1,0:T(8,128)(2,1)}, u32[]{:S(2)}) %copy-start.1) | copy-done | bytes 6291480
  124.2 2.2 %hidden_grad.1 = (bf16[80,1024]{1,0:T(8,128)(2,1)S(1)}, bf16[80,256]{1,0:T(8,128)(2,1)S(1)}, bf16[80,256]{1,0:T(8,128)(2,1)S(1)}, bf16[80,256]{1,0:T(8,128)(2,1)S(1)}, bf16[80,256]{1,0:T(8,128)(2,1)S(1)}) custom-call(s32[1]{0:T(128)} %bitcast.3.y_ref, bf16[8,80,256]{2,1,0:T(8,128)(2,1)S(1)} %all-to-all-done.2.first_ref, ...), custom_call_target="tpu_custom_call" | custom-call | tf_op jit(solution)/shard_map/hidden_grad/pallas_call | solution.py:138
  126.4 0.6 copy-done.6
  127.0 0.7 collective-permute-start.10
  127.8 4.4 %collective-permute-start.11 = (bf16[80,256]{1,0:T(8,128)(2,1)S(1)}, bf16[80,256]{1,0:T(8,128)(2,1)S(1)}, u32[]{:S(2)}, u32[]{:S(2)}) collective-permute-start(bf16[80,256]{1,0:T(8,128)(2,1)S(1)} %get-tuple-element.65), channel_id=1, source_target_pairs={{0,2},{1,3},{2,0},{3,1},{4,6},{5,7},{6,4},{7,5},{8,10},{9,11},{10,... | collective-permute-start | bytes 122888 | tf_op jit(solution)/shard_map/ppermute | solution.py:291
  132.2 0.8 convolution_convert_fusion.1
  133.1 1.5 collective-permute-done.11.refs_6_
  134.6 1.6 collective-permute-done.12.refs_7_
  136.2 0.6 copy-done.11
  136.8 2.5 %short_grads.1 = bf16[32,64,128]{2,1,0:T(8,128)(2,1)} custom-call(bf16[80,1024]{1,0:T(8,128)(2,1)} %copy-done.7, bf16[80,1024]{1,0:T(8,128)(2,1)} %collective-permute-done.1.refs_1_, bf16[80,1024]{1,0:T(8,128)(2,1)} %collective-permute-done.2.refs_2_, bf16[80,1024]{1,0:T(8,128)(2,1)} %collective-permute-done.3.refs_3_, bf16[80,256]{1,0:T(8,128)(2,1)} %copy-done.6, ...), custom_call_target="tpu_custom_call" | custom-call | tf_op jit(solution)/shard_map/short_grads/pallas_call | solution.py:218
  139.3 4.7 %all-to-all-start.4 = ((bf16[32,64,128]{2,1,0:T(8,128)(2,1)}), bf16[32,64,128]{2,1,0:T(8,128)(2,1)}, u32[]{:S(2)}, u32[]{:S(2)}) async-start(bf16[32,64,128]{2,1,0:T(8,128)(2,1)} %short_grads.1), calls=%async_computation.4 | async-start | bytes 1048576 | tf_op jit(solution)/shard_map/all_to_all | solution.py:342
  144.1 1.3 collective-permute-start.13
  145.4 2.1 %fusion.8 = f32[80,1024]{1,0:T(8,128)S(1)} fusion(bf16[1024,1024]{1,0:T(8,128)(2,1)} %param.8, bf16[8,80,256]{2,1,0:T(8,128)(2,1)S(1)} %all-to-all-done.2.first_ref), kind=kOutput, calls=%fused_computation.23 | convolution fusion | flops 167772160 | bytes 2588672 | tf_op jit(solution)/shard_map/dot_general | solution.py:21
  147.6 1.7 split_parts.1
  149.3 4.9 %collective-permute-start.14 = (bf16[32,384]{1,0:T(8,128)(2,1)}, bf16[32,384]{1,0:T(8,128)(2,1)S(1)}, u32[]{:S(2)}, u32[]{:S(2)}) collective-permute-start(bf16[32,384]{1,0:T(8,128)(2,1)} %get-tuple-element.77), channel_id=1, source_target_pairs={{0,4},{4,8},{8,12},{12,16},{16,20},{20,24},{24,28},{28,0},{1,5},{5... | collective-permute-start | bytes 73736 | tf_op jit(solution)/shard_map/ppermute | solution.py:346
  154.2 2.4 %collective-permute-start.15 = (bf16[32,384]{1,0:T(8,128)(2,1)}, bf16[32,384]{1,0:T(8,128)(2,1)S(1)}, u32[]{:S(2)}, u32[]{:S(2)}) collective-permute-start(bf16[32,384]{1,0:T(8,128)(2,1)} %get-tuple-element.78), channel_id=1, source_target_pairs={{0,8},{4,12},{8,16},{12,20},{16,24},{20,28},{24,0},{28,4},{1,9},{5... | collective-permute-start | bytes 73736 | tf_op jit(solution)/shard_map/ppermute | solution.py:346
  156.6 0.7 add_convert_fusion
  157.3 3.7 %collective-permute-start.16 = (bf16[32,384]{1,0:T(8,128)(2,1)}, bf16[32,384]{1,0:T(8,128)(2,1)S(1)}, u32[]{:S(2)}, u32[]{:S(2)}) collective-permute-start(bf16[32,384]{1,0:T(8,128)(2,1)} %get-tuple-element.79), channel_id=1, source_target_pairs={{0,12},{4,16},{8,20},{12,24},{16,28},{20,0},{24,4},{28,8},{1,13},{... | collective-permute-start | bytes 73736 | tf_op jit(solution)/shard_map/ppermute | solution.py:346
  161.1 1.4 collective-permute-start.17
  162.4 3.7 %collective-permute-start.18 = (bf16[32,384]{1,0:T(8,128)(2,1)}, bf16[32,384]{1,0:T(8,128)(2,1)S(1)}, u32[]{:S(2)}, u32[]{:S(2)}) collective-permute-start(bf16[32,384]{1,0:T(8,128)(2,1)} %get-tuple-element.81), channel_id=1, source_target_pairs={{0,20},{4,24},{8,28},{12,0},{16,4},{20,8},{24,12},{28,16},{1,21},{... | collective-permute-start | bytes 73736 | tf_op jit(solution)/shard_map/ppermute | solution.py:346
  166.1 3.5 %collective-permute-start.19 = (bf16[32,384]{1,0:T(8,128)(2,1)}, bf16[32,384]{1,0:T(8,128)(2,1)S(1)}, u32[]{:S(2)}, u32[]{:S(2)}) collective-permute-start(bf16[32,384]{1,0:T(8,128)(2,1)} %get-tuple-element.82), channel_id=1, source_target_pairs={{0,24},{4,28},{8,0},{12,4},{16,8},{20,12},{24,16},{28,20},{1,25},{... | collective-permute-start | bytes 73736 | tf_op jit(solution)/shard_map/ppermute | solution.py:346
  169.7 0.5 collective-permute-start.20
  170.2 1.6 add_convert_fusion.1
  171.9 1.8 collective-permute-done.20.refs_7_
  173.7 0.6 copy-done.18
  174.3 1.6 assemble_attend.1
  176.0 1.8 assemble_short.1
  (78 shorter events, 2.1 us)
Async XLA Ops:
  7.2 6.7 %copy-start = (bf16[1024,1024]{1,0:T(8,128)(2,1)S(1)}, bf16[1024,1024]{1,0:T(8,128)(2,1)}, u32[]{:S(2)}) copy-start(bf16[1024,1024]{1,0:T(8,128)(2,1)} %param.6) | copy-start | bytes 6291460
  8.0 4.8 %collective-permute-start = (bf16[3,256]{1,0:T(4,128)(2,1)S(1)}, bf16[3,256]{1,0:T(4,128)(2,1)S(1)}, u32[]{:S(2)}, u32[]{:S(2)}) collective-permute-start(bf16[3,256]{1,0:T(4,128)(2,1)S(1)} %slice.34), channel_id=1, source_target_pairs={{0,1},{1,2},{2,3},{3,4},{4,5},{5,6},{6,7},{7,8},{8,9},{9,10},{10,1... | collective-permute-start | bytes 4616 | tf_op jit(solution)/shard_map/ppermute | solution.py:301
  13.9 22.3 %copy-start.7 = (bf16[80,1024]{1,0:T(8,128)(2,1)}, bf16[80,1024]{1,0:T(8,128)(2,1)S(1)}, u32[]{:S(2)}) copy-start(bf16[80,1024]{1,0:T(8,128)(2,1)S(1)} %reshape.82.refs_0_) | copy-start | bytes 491524
  20.0 25.0 %all-to-all-start = ((bf16[8,80,256]{2,1,0:T(8,128)(2,1)}), bf16[8,80,256]{2,1,0:T(8,128)(2,1)S(1)}, u32[]{:S(2)}, u32[]{:S(2)}) async-start(bf16[8,80,256]{2,1,0:T(8,128)(2,1)} %reshape.83), calls=%async_computation | async-start | bytes 655360 | tf_op jit(solution)/shard_map/all_to_all | solution.py:298
  32.5 68.0 %all-gather.2.cloned.1.call-start = ((), (), s32[]{:S(2)}) async-start(), calls=%async_computation.6 | async-start | bytes 2949120 | tf_op jit(solution)/shard_map/all_gather | solution.py:314
  35.0 9.4 %collective-permute-start.1 = (bf16[80,1024]{1,0:T(8,128)(2,1)S(1)}, bf16[80,1024]{1,0:T(8,128)(2,1)}, u32[]{:S(2)}, u32[]{:S(2)}) collective-permute-start(bf16[80,1024]{1,0:T(8,128)(2,1)S(1)} %reshape.82.refs_0_), channel_id=1, source_target_pairs={{0,1},{1,2},{2,3},{3,0},{4,5},{5,6},{6,7},{7,4},{8,9},{9,10},{10,1... | collective-permute-start | bytes 491528 | tf_op jit(solution)/shard_map/ppermute | solution.py:291
  35.0 9.3 %collective-permute-start.2 = (bf16[80,1024]{1,0:T(8,128)(2,1)S(1)}, bf16[80,1024]{1,0:T(8,128)(2,1)}, u32[]{:S(2)}, u32[]{:S(2)}) collective-permute-start(bf16[80,1024]{1,0:T(8,128)(2,1)S(1)} %reshape.82.refs_0_), channel_id=1, source_target_pairs={{0,2},{1,3},{2,0},{3,1},{4,6},{5,7},{6,4},{7,5},{8,10},{9,11},{10,... | collective-permute-start | bytes 491528 | tf_op jit(solution)/shard_map/ppermute | solution.py:291
  36.2 8.8 %collective-permute-start.3 = (bf16[80,1024]{1,0:T(8,128)(2,1)S(1)}, bf16[80,1024]{1,0:T(8,128)(2,1)}, u32[]{:S(2)}, u32[]{:S(2)}) collective-permute-start(bf16[80,1024]{1,0:T(8,128)(2,1)S(1)} %reshape.82.refs_0_), channel_id=1, source_target_pairs={{0,3},{1,0},{2,1},{3,2},{4,7},{5,4},{6,5},{7,6},{8,11},{9,8},{10,9... | collective-permute-start | bytes 491528 | tf_op jit(solution)/shard_map/ppermute | solution.py:291
  45.0 22.4 %all-to-all-start.1 = ((bf16[8,80,256]{2,1,0:T(8,128)(2,1)}), bf16[8,80,256]{2,1,0:T(8,128)(2,1)S(1)}, u32[]{:S(2)}, u32[]{:S(2)}) async-start(bf16[8,80,256]{2,1,0:T(8,128)(2,1)} %reshape.86), calls=%async_computation.1 | async-start | bytes 655360 | tf_op jit(solution)/shard_map/all_to_all | solution.py:298
  52.0 11.8 %collective-permute-start.4 = (bf16[640,256]{1,0:T(8,128)(2,1)S(1)}, bf16[640,256]{1,0:T(8,128)(2,1)S(1)}, u32[]{:S(2)}, u32[]{:S(2)}) collective-permute-start(bf16[640,256]{1,0:T(8,128)(2,1)S(1)} %bitcast.51), channel_id=1, source_target_pairs={{0,1},{1,2},{2,3},{3,0},{4,5},{5,6},{6,7},{7,4},{8,9},{9,10},{10,1... | collective-permute-start | bytes 983048 | tf_op jit(solution)/shard_map/ppermute | solution.py:291
  52.2 15.3 %collective-permute-start.5 = (bf16[640,256]{1,0:T(8,128)(2,1)S(1)}, bf16[640,256]{1,0:T(8,128)(2,1)}, u32[]{:S(2)}, u32[]{:S(2)}) collective-permute-start(bf16[640,256]{1,0:T(8,128)(2,1)S(1)} %bitcast.52), channel_id=1, source_target_pairs={{0,2},{1,3},{2,0},{3,1},{4,6},{5,7},{6,4},{7,5},{8,10},{9,11},{10,... | collective-permute-start | bytes 983048 | tf_op jit(solution)/shard_map/ppermute | solution.py:291
  55.7 11.7 %collective-permute-start.6 = (bf16[640,256]{1,0:T(8,128)(2,1)S(1)}, bf16[640,256]{1,0:T(8,128)(2,1)}, u32[]{:S(2)}, u32[]{:S(2)}) collective-permute-start(bf16[640,256]{1,0:T(8,128)(2,1)S(1)} %bitcast.53), channel_id=1, source_target_pairs={{0,3},{1,0},{2,1},{3,2},{4,7},{5,4},{6,5},{7,6},{8,11},{9,8},{10,9... | collective-permute-start | bytes 983048 | tf_op jit(solution)/shard_map/ppermute | solution.py:291
  63.8 0.7 copy-start.4
  67.4 1.0 copy-start.5
  76.7 0.8 copy-start.3
  77.6 11.6 %collective-permute-start.9 = (bf16[640,256]{1,0:T(8,128)(2,1)}, bf16[640,256]{1,0:T(8,128)(2,1)}, u32[]{:S(2)}, u32[]{:S(2)}) collective-permute-start(bf16[640,256]{1,0:T(8,128)(2,1)} %get-tuple-element.58), channel_id=1, source_target_pairs={{0,1},{1,2},{2,3},{3,0},{4,5},{5,6},{6,7},{7,4},{8,9},{9,10},{10,1... | collective-permute-start | bytes 983048 | tf_op jit(solution)/shard_map/ppermute | solution.py:291
  77.6 17.6 %collective-permute-start.8 = (bf16[640,256]{1,0:T(8,128)(2,1)}, bf16[640,256]{1,0:T(8,128)(2,1)}, u32[]{:S(2)}, u32[]{:S(2)}) collective-permute-start(bf16[640,256]{1,0:T(8,128)(2,1)} %get-tuple-element.57), channel_id=1, source_target_pairs={{0,2},{1,3},{2,0},{3,1},{4,6},{5,7},{6,4},{7,5},{8,10},{9,11},{10,... | collective-permute-start | bytes 983048 | tf_op jit(solution)/shard_map/ppermute | solution.py:291
  81.4 13.8 %collective-permute-start.7 = (bf16[640,256]{1,0:T(8,128)(2,1)}, bf16[640,256]{1,0:T(8,128)(2,1)}, u32[]{:S(2)}, u32[]{:S(2)}) collective-permute-start(bf16[640,256]{1,0:T(8,128)(2,1)} %get-tuple-element.56), channel_id=1, source_target_pairs={{0,3},{1,0},{2,1},{3,2},{4,7},{5,4},{6,5},{7,6},{8,11},{9,8},{10,9... | collective-permute-start | bytes 983048 | tf_op jit(solution)/shard_map/ppermute | solution.py:291
  82.2 18.4 %all-to-all-start.2 = ((bf16[8,80,256]{2,1,0:T(8,128)(2,1)}), bf16[8,80,256]{2,1,0:T(8,128)(2,1)S(1)}, u32[]{:S(2)}, u32[]{:S(2)}) async-start(bf16[8,80,256]{2,1,0:T(8,128)(2,1)} %bitcast.59), calls=%async_computation.2 | async-start | bytes 655360 | tf_op jit(solution)/shard_map/all_to_all | solution.py:298
  89.1 58.5 %reduce-scatter.2.cloned.1.call-start = ((), (), s32[]{:S(2)}) async-start(), calls=%async_computation.7 | async-start | bytes 1310720 | tf_op jit(solution)/shard_map/reduce_scatter | solution.py:335
  100.5 1.7 copy-start.2
  105.4 16.0 %all-to-all-start.3 = ((bf16[8,80,256]{2,1,0:T(8,128)(2,1)}), bf16[8,80,256]{2,1,0:T(8,128)(2,1)S(1)}, u32[]{:S(2)}, u32[]{:S(2)}) async-start(bf16[8,80,256]{2,1,0:T(8,128)(2,1)} %bitcast.6), calls=%async_computation.3 | async-start | bytes 655360 | tf_op jit(solution)/shard_map/all_to_all | solution.py:298
  121.4 2.9 %copy-start.1 = (bf16[1024,3072]{1,0:T(8,128)(2,1)S(1)}, bf16[1024,3072]{1,0:T(8,128)(2,1)}, u32[]{:S(2)}) copy-start(bf16[1024,3072]{1,0:T(8,128)(2,1)} %weight_ref.1) | copy-start | bytes 18874372
  126.4 0.6 copy-start.6
  127.0 6.1 %collective-permute-start.10 = (bf16[80,256]{1,0:T(8,128)(2,1)S(1)}, bf16[80,256]{1,0:T(8,128)(2,1)S(1)}, u32[]{:S(2)}, u32[]{:S(2)}) collective-permute-start(bf16[80,256]{1,0:T(8,128)(2,1)S(1)} %get-tuple-element.64), channel_id=1, source_target_pairs={{0,1},{1,2},{2,3},{3,0},{4,5},{5,6},{6,7},{7,4},{8,9},{9,10},{10,1... | collective-permute-start | bytes 122888 | tf_op jit(solution)/shard_map/ppermute | solution.py:291
  127.8 6.8 %collective-permute-start.11 = (bf16[80,256]{1,0:T(8,128)(2,1)S(1)}, bf16[80,256]{1,0:T(8,128)(2,1)S(1)}, u32[]{:S(2)}, u32[]{:S(2)}) collective-permute-start(bf16[80,256]{1,0:T(8,128)(2,1)S(1)} %get-tuple-element.65), channel_id=1, source_target_pairs={{0,2},{1,3},{2,0},{3,1},{4,6},{5,7},{6,4},{7,5},{8,10},{9,11},{10,... | collective-permute-start | bytes 122888 | tf_op jit(solution)/shard_map/ppermute | solution.py:291
  132.2 4.0 %collective-permute-start.12 = (bf16[80,256]{1,0:T(8,128)(2,1)S(1)}, bf16[80,256]{1,0:T(8,128)(2,1)S(1)}, u32[]{:S(2)}, u32[]{:S(2)}) collective-permute-start(bf16[80,256]{1,0:T(8,128)(2,1)S(1)} %get-tuple-element.66), channel_id=1, source_target_pairs={{0,3},{1,0},{2,1},{3,2},{4,7},{5,4},{6,5},{7,6},{8,11},{9,8},{10,9... | collective-permute-start | bytes 122888 | tf_op jit(solution)/shard_map/ppermute | solution.py:291
  133.1 3.1 %copy-start.9 = (bf16[80,256]{1,0:T(8,128)(2,1)}, bf16[80,256]{1,0:T(8,128)(2,1)S(1)}, u32[]{:S(2)}) copy-start(bf16[80,256]{1,0:T(8,128)(2,1)S(1)} %collective-permute-done.10.refs_5_) | copy-start | bytes 122884
  134.6 1.6 copy-start.10
  136.2 0.6 copy-start.11
  139.3 17.3 %copy-start.8 = (bf16[320,256]{1,0:T(8,128)(2,1)S(1)}, bf16[320,256]{1,0:T(8,128)(2,1)}, u32[]{:S(2)}) copy-start(bf16[320,256]{1,0:T(8,128)(2,1)} %param.5) | copy-start | bytes 491524
  139.3 36.7 %all-to-all-start.4 = ((bf16[32,64,128]{2,1,0:T(8,128)(2,1)}), bf16[32,64,128]{2,1,0:T(8,128)(2,1)}, u32[]{:S(2)}, u32[]{:S(2)}) async-start(bf16[32,64,128]{2,1,0:T(8,128)(2,1)} %short_grads.1), calls=%async_computation.4 | async-start | bytes 1048576 | tf_op jit(solution)/shard_map/all_to_all | solution.py:342
  144.1 18.4 %collective-permute-start.13 = (bf16[3,256]{1,0:T(4,128)(2,1)S(1)}, bf16[3,256]{1,0:T(4,128)(2,1)S(1)}, u32[]{:S(2)}, u32[]{:S(2)}) collective-permute-start(bf16[3,256]{1,0:T(4,128)(2,1)S(1)} %slice.43), channel_id=1, source_target_pairs={{1,0},{2,1},{3,2},{4,3},{5,4},{6,5},{7,6},{8,7},{9,8},{10,9},{11,1... | collective-permute-start | bytes 4616 | tf_op jit(solution)/shard_map/ppermute | solution.py:355
  149.3 16.9 %collective-permute-start.14 = (bf16[32,384]{1,0:T(8,128)(2,1)}, bf16[32,384]{1,0:T(8,128)(2,1)S(1)}, u32[]{:S(2)}, u32[]{:S(2)}) collective-permute-start(bf16[32,384]{1,0:T(8,128)(2,1)} %get-tuple-element.77), channel_id=1, source_target_pairs={{0,4},{4,8},{8,12},{12,16},{16,20},{20,24},{24,28},{28,0},{1,5},{5... | collective-permute-start | bytes 73736 | tf_op jit(solution)/shard_map/ppermute | solution.py:346
  154.2 15.5 %collective-permute-start.15 = (bf16[32,384]{1,0:T(8,128)(2,1)}, bf16[32,384]{1,0:T(8,128)(2,1)S(1)}, u32[]{:S(2)}, u32[]{:S(2)}) collective-permute-start(bf16[32,384]{1,0:T(8,128)(2,1)} %get-tuple-element.78), channel_id=1, source_target_pairs={{0,8},{4,12},{8,16},{12,20},{16,24},{20,28},{24,0},{28,4},{1,9},{5... | collective-permute-start | bytes 73736 | tf_op jit(solution)/shard_map/ppermute | solution.py:346
  157.3 14.5 %collective-permute-start.16 = (bf16[32,384]{1,0:T(8,128)(2,1)}, bf16[32,384]{1,0:T(8,128)(2,1)S(1)}, u32[]{:S(2)}, u32[]{:S(2)}) collective-permute-start(bf16[32,384]{1,0:T(8,128)(2,1)} %get-tuple-element.79), channel_id=1, source_target_pairs={{0,12},{4,16},{8,20},{12,24},{16,28},{20,0},{24,4},{28,8},{1,13},{... | collective-permute-start | bytes 73736 | tf_op jit(solution)/shard_map/ppermute | solution.py:346
  161.1 10.8 %collective-permute-start.17 = (bf16[32,384]{1,0:T(8,128)(2,1)}, bf16[32,384]{1,0:T(8,128)(2,1)S(1)}, u32[]{:S(2)}, u32[]{:S(2)}) collective-permute-start(bf16[32,384]{1,0:T(8,128)(2,1)} %get-tuple-element.80), channel_id=1, source_target_pairs={{0,16},{4,20},{8,24},{12,28},{16,0},{20,4},{24,8},{28,12},{1,17},{... | collective-permute-start | bytes 73736 | tf_op jit(solution)/shard_map/ppermute | solution.py:346
  162.4 9.4 %collective-permute-start.18 = (bf16[32,384]{1,0:T(8,128)(2,1)}, bf16[32,384]{1,0:T(8,128)(2,1)S(1)}, u32[]{:S(2)}, u32[]{:S(2)}) collective-permute-start(bf16[32,384]{1,0:T(8,128)(2,1)} %get-tuple-element.81), channel_id=1, source_target_pairs={{0,20},{4,24},{8,28},{12,0},{16,4},{20,8},{24,12},{28,16},{1,21},{... | collective-permute-start | bytes 73736 | tf_op jit(solution)/shard_map/ppermute | solution.py:346
  166.1 7.6 %copy-start.12 = (bf16[32,384]{1,0:T(8,128)(2,1)}, bf16[32,384]{1,0:T(8,128)(2,1)S(1)}, u32[]{:S(2)}) copy-start(bf16[32,384]{1,0:T(8,128)(2,1)S(1)} %collective-permute-done.14.refs_1_) | copy-start | bytes 73732
  166.1 5.7 %collective-permute-start.19 = (bf16[32,384]{1,0:T(8,128)(2,1)}, bf16[32,384]{1,0:T(8,128)(2,1)S(1)}, u32[]{:S(2)}, u32[]{:S(2)}) collective-permute-start(bf16[32,384]{1,0:T(8,128)(2,1)} %get-tuple-element.82), channel_id=1, source_target_pairs={{0,24},{4,28},{8,0},{12,4},{16,8},{20,12},{24,16},{28,20},{1,25},{... | collective-permute-start | bytes 73736 | tf_op jit(solution)/shard_map/ppermute | solution.py:346
  169.7 4.0 %copy-start.13 = (bf16[32,384]{1,0:T(8,128)(2,1)}, bf16[32,384]{1,0:T(8,128)(2,1)S(1)}, u32[]{:S(2)}) copy-start(bf16[32,384]{1,0:T(8,128)(2,1)S(1)} %collective-permute-done.15.refs_2_) | copy-start | bytes 73732
  169.7 4.0 %collective-permute-start.20 = (bf16[32,384]{1,0:T(8,128)(2,1)}, bf16[32,384]{1,0:T(8,128)(2,1)S(1)}, u32[]{:S(2)}, u32[]{:S(2)}) collective-permute-start(bf16[32,384]{1,0:T(8,128)(2,1)} %get-tuple-element.83), channel_id=1, source_target_pairs={{0,28},{4,0},{8,4},{12,8},{16,12},{20,16},{24,20},{28,24},{1,29},{... | collective-permute-start | bytes 73736 | tf_op jit(solution)/shard_map/ppermute | solution.py:346
  171.8 1.9 %copy-start.14 = (bf16[32,384]{1,0:T(8,128)(2,1)}, bf16[32,384]{1,0:T(8,128)(2,1)S(1)}, u32[]{:S(2)}) copy-start(bf16[32,384]{1,0:T(8,128)(2,1)S(1)} %collective-permute-done.16.refs_3_) | copy-start | bytes 73732
  171.8 1.9 %copy-start.15 = (bf16[32,384]{1,0:T(8,128)(2,1)}, bf16[32,384]{1,0:T(8,128)(2,1)S(1)}, u32[]{:S(2)}) copy-start(bf16[32,384]{1,0:T(8,128)(2,1)S(1)} %collective-permute-done.17.refs_4_) | copy-start | bytes 73732
  171.9 1.9 %copy-start.16 = (bf16[32,384]{1,0:T(8,128)(2,1)}, bf16[32,384]{1,0:T(8,128)(2,1)S(1)}, u32[]{:S(2)}) copy-start(bf16[32,384]{1,0:T(8,128)(2,1)S(1)} %collective-permute-done.18.refs_5_) | copy-start | bytes 73732
  171.9 1.9 %copy-start.17 = (bf16[32,384]{1,0:T(8,128)(2,1)}, bf16[32,384]{1,0:T(8,128)(2,1)S(1)}, u32[]{:S(2)}) copy-start(bf16[32,384]{1,0:T(8,128)(2,1)S(1)} %collective-permute-done.19.refs_6_) | copy-start | bytes 73732
  173.7 0.6 copy-start.18
Sparse Core Ops, SparseCore 0:
  45.1 43.6 all-gather.1
  105.5 23.5 reduce-scatter.1

commit v4 on v3

--- a/solution.py
+++ b/solution.py
@@ -175,30 +175,6 @@
     )(gathered, d_query, d_kv, attended)
 
 
-def split_parts_body(z_ref, parts_ref, expand_ref, *piece_refs):
-    groups, _, width = parts_ref.shape
-    head_width = piece_refs[0].shape[1]
-    lanes = width - head_width
-    for group in range(groups):
-        expand_ref[:, group * lanes : (group + 1) * lanes] = parts_ref[group, :, head_width:].astype(jnp.float32)
-    for step, piece_ref in enumerate(piece_refs):
-        piece_ref[...] = parts_ref[lax.rem(z_ref[0] + step, groups), :, :head_width]
-
-
-def split_parts(z, parts, head_width):
-    groups, own_rows, width = parts.shape
-    vmem = pl.BlockSpec(memory_space=pltpu.VMEM)
-    outs = [jax.ShapeDtypeStruct((own_rows, (width - head_width) * groups), jnp.float32)]
-    outs += [jax.ShapeDtypeStruct((own_rows, head_width), jnp.bfloat16)] * groups
-    return pl.pallas_call(
-        split_parts_body,
-        out_shape=outs,
-        in_specs=[pl.BlockSpec(memory_space=pltpu.SMEM), vmem],
-        out_specs=[vmem] * len(outs),
-        name="split_parts",
-    )(z, parts)
-
-
 def short_grads_body(shards, *refs):
     grouped_refs, cols_refs, out_ref = refs[:shards], refs[shards : 2 * shards], refs[-1]
     count, tall, lanes = out_ref.shape
@@ -224,28 +200,31 @@
     )(*grouped, *cols)
 
 
-def assemble_attend_body(z_ref, *refs):
-    piece_refs, out_ref = refs[:-1], refs[-1]
-    groups = len(piece_refs)
-    lanes = piece_refs[0].shape[1] // 3
-    for step, piece_ref in enumerate(piece_refs):
-        head = lax.rem(z_ref[0] + (groups - step), groups)
+def assemble_heads_body(parts_ref, came_ref, expand_ref, attend_ref):
+    heads, _, width = parts_ref.shape
+    lanes = expand_ref.shape[1] // heads
+    head_lanes = attend_ref.shape[1] // 3 // heads
+    for head in range(heads):
+        expand_ref[:, head * lanes : (head + 1) * lanes] = parts_ref[head, :, width - lanes :].astype(jnp.float32)
         for part in range(3):
-            first = pl.multiple_of((part * groups + head) * lanes, lanes)
-            piece = piece_ref[:, part * lanes : (part + 1) * lanes].astype(jnp.float32)
-            out_ref[:, pl.ds(first, lanes)] = piece
-
-
-def assemble_attend(z, pieces):
-    own_rows, width = pieces[0].shape
-    vmem = pl.BlockSpec(memory_space=pltpu.VMEM)
-    return pl.pallas_call(
-        assemble_attend_body,
-        out_shape=jax.ShapeDtypeStruct((own_rows, width * len(pieces)), jnp.float32),
-        in_specs=[pl.BlockSpec(memory_space=pltpu.SMEM)] + [vmem] * len(pieces),
-        out_specs=vmem,
-        name="assemble_attend",
-    )(z, *pieces)
+            first = (part * heads + head) * head_lanes
+            piece = came_ref[head, :, part * head_lanes : (part + 1) * head_lanes]
+            attend_ref[:, first : first + head_lanes] = piece.astype(jnp.float32)
+
+
+def assemble_heads(parts, came, expand_width, qkv_width):
+    own_rows = parts.shape[1]
+    vmem = pl.BlockSpec(memory_space=pltpu.VMEM)
+    return pl.pallas_call(
+        assemble_heads_body,
+        out_shape=[
+            jax.ShapeDtypeStruct((own_rows, expand_width), jnp.float32),
+            jax.ShapeDtypeStruct((own_rows, qkv_width), jnp.float32),
+        ],
+        in_specs=[vmem] * 2,
+        out_specs=[vmem] * 2,
+        name="assemble_heads",
+    )(parts, came)
 
 
 def assemble_short_body(shards, parts_ref, out_ref):
@@ -335,18 +314,14 @@
     parts = lax.psum_scatter(parts, "y", scatter_dimension=0)
     d_hidden, *d_hidden_y = hidden_grad(y, first_back, second_back, w_attend, normed, hidden_scale, y_size)
     d_hidden_y = d_hidden_y[:1] + [turn_y(d_hidden_y[step], step) for step in range(1, y_size)]
+    parts, d_hidden = tie(parts, d_hidden)
     d_grouped = mm(d_hidden, w_short, NT).astype(jnp.bfloat16).reshape(4 * short_rows, byte_width)
     *d_hidden_y, d_grouped = tie(*d_hidden_y, d_grouped)
     short = short_grads(grouped_y, d_hidden_y, count, head_size)
-    short, first_back = tie(short, first_back)
+    came = swap(parts)
+    short, first_back, parts, came = tie(short, first_back, parts, came)
     short = lax.all_to_all(short, both, 0, 0)
-    z = lax.axis_index("z").astype(jnp.int32).reshape(1)
-    grad_expand, *pieces = split_parts(z, parts, 3 * head_size)
-    pieces = pieces[:1] + [
-        lax.ppermute(pieces[step], "z", [(i, (i + step) % z_size) for i in range(z_size)])
-        for step in range(1, z_size)
-    ]
-    grad_attend = assemble_attend(z, pieces)
+    grad_expand, grad_attend = assemble_heads(parts, came, 4 * byte_width, 3 * attn_width)
     attended_own = first_back[:, :, :head_size].transpose(1, 0, 2).reshape(short_rows, attn_width)
     expanded = mm(attended_own, w_expand)
     byte_output = (

time: 186 us -> 185 us (level)
  starting transfers between devices: 76.3 us -> 66.1 us
  waiting for transfers between devices: 39.3 us -> 46.2 us
  local copies, waits for them, and re-layouts: 15.7 us -> 18.3 us
    ppermute x7 -> x0, starting transfers between devices: 20.2 us -> none  [local(): lax.ppermute(pieces[step], 'z', [(i, (i + step) % z_size) for i in range(...]
    all_to_all x4 -> x5, starting transfers between devices: 30.5 us -> 37.4 us  [swap(): return lax.all_to_all(value, 'z', 0, 0)]
    all_to_all x1, starting transfers between devices: 4.75 us -> 8.9 us  [local(): short = lax.all_to_all(short, both, 0, 0)]
    ppermute x1, waiting for transfers between devices: 0.01 us -> 4.13 us  [local(): lax.ppermute(d_grouped[:3], both, [(i + 1, i) for i in range(count - 1)])]
    all_to_all x1, waiting for transfers between devices: 0.01 us -> 3.19 us  [local(): short = lax.all_to_all(short, both, 0, 0)]
    reduce_scatter x1, waiting for transfers between devices: 0.02 us -> 2.07 us  [local(): parts = lax.psum_scatter(parts, 'y', scatter_dimension=0)]
    all_to_all x4 -> x5, waiting for transfers between devices: 14.3 us -> 15.2 us  [swap(): return lax.all_to_all(value, 'z', 0, 0)]
    unnamed x43 -> x33, local copies, waits for them, and re-layouts: 9.11 us -> 10 us
  transfers between devices with their start and end apart: 28 -> 22, of which waited for: 12 -> 15; matrix products, arithmetic and copies ran while one was open for 9% -> 9% of each run, Pallas kernels for 9% -> 8%
where the time goes in v4:
time: 185 us; the launch traced here: 182 us
  starting transfers between devices  66.1 us (36%)
  waiting for transfers between devices  46.2 us (25%)
  Pallas kernels  19.7 us (11%)
  local copies, waits for them, and re-layouts  18.3 us (10%)
  between operations  14.3 us (8%)
  matrix products  9.77 us (5%)
  other arithmetic  7.95 us (4%)
    all_to_all x5, starting transfers between devices, swap(): return lax.all_to_all(value, 'z', 0, 0)  37.4 us
    ppermute x12, waiting for transfers between devices, turn_y(): lax.ppermute(value, 'y', [(i, (i + steps) % y_size) for i in range(y_size)])  21.3 us
    all_to_all x5, waiting for transfers between devices, swap(): return lax.all_to_all(value, 'z', 0, 0)  15.2 us
    ppermute x12, starting transfers between devices, turn_y(): lax.ppermute(value, 'y', [(i, (i + steps) % y_size) for i in range(y_size)])  15 us
    unnamed x33, local copies, waits for them, and re-layouts  10 us
    dot_general x5, matrix products, mm(): lax.dot_general(left, right, dims, preferred_element_type=jnp.float32)  9.77 us
    all_to_all x1, starting transfers between devices, local(): short = lax.all_to_all(short, both, 0, 0)  8.9 us
    pallas_call x1, Pallas kernels, attention(): pl.pallas_call(functools.partial(attention_body, block, shards), out_shap...  8.29 us
  transfers between devices with their start and end apart: 22, of which 15 were waited for; matrix products, arithmetic and copies ran while one was open for 9% of the time, Pallas kernels for 8%

profile of v4, /device:TPU:6, one launch (start us, length us, event | category | flops | bytes accessed | tf_op | source)
XLA Modules:
  0.0 182.3 jit_solution(15982086702541011973)
XLA Ops:
  7.2 0.8 slice.34
  8.0 3.5 %collective-permute-start = (bf16[3,256]{1,0:T(4,128)(2,1)S(1)}, bf16[3,256]{1,0:T(4,128)(2,1)S(1)}, u32[]{:S(2)}, u32[]{:S(2)}) collective-permute-start(bf16[3,256]{1,0:T(4,128)(2,1)S(1)} %slice.34), channel_id=1, source_target_pairs={{0,1},{1,2},{2,3},{3,4},{4,5},{5,6},{6,7},{7,8},{8,9},{9,10},{10,1... | collective-permute-start | bytes 4616 | tf_op jit(solution)/shard_map/ppermute | solution.py:280
  11.5 1.0 reshape.82
  12.5 0.3 collective-permute-done
  12.8 1.0 pad_maximum_fusion.3
  13.9 0.6 multiply_reduce_fusion
  14.6 4.0 %convolution_convert_fusion = bf16[80,3072]{1,0:T(8,128)(2,1)S(1)} fusion(bf16[80,1024]{1,0:T(8,128)(2,1)S(1)} %get-tuple-element.83, bf16[1024,3072]{1,0:T(8,128)(2,1)} %weight_ref.1), kind=kOutput, calls=%fused_computation | convolution fusion | flops 503562240 | bytes 6946816 | tf_op jit(solution)/shard_map/dot_general | solution.py:21
  18.7 1.1 copy.13
  19.8 1.9 %reshape.80 = bf16[8,80,256]{2,1,0:T(8,128)(2,1)} reshape(bf16[8,80,2,128]{3,2,1,0:T(2,128)(2,1)} %copy.13) | data formatting | bytes 655360 | tf_op jit(solution)/shard_map/reshape | solution.py:274
  21.7 12.5 %all-to-all-start = ((bf16[8,80,256]{2,1,0:T(8,128)(2,1)}), bf16[8,80,256]{2,1,0:T(8,128)(2,1)S(1)}, u32[]{:S(2)}, u32[]{:S(2)}) async-start(bf16[8,80,256]{2,1,0:T(8,128)(2,1)} %reshape.80), calls=%async_computation | async-start | bytes 655360 | tf_op jit(solution)/shard_map/all_to_all | solution.py:277
  34.2 2.4 %fusion = bf16[10,8,8,128]{3,1,2,0:T(8,128)(2,1)S(1)} fusion(bf16[80,1024]{1,0:T(8,128)(2,1)S(1)} %reshape.82, bf16[1024,1024]{1,0:T(8,128)(2,1)} %param.8), kind=kOutput, calls=%fused_computation.3 | convolution fusion | flops 167854080 | bytes 2424832 | tf_op jit(solution)/shard_map/dot_general | solution.py:21
  36.7 1.1 collective-permute-start.2
  37.9 2.1 %collective-permute-start.3 = (bf16[80,1024]{1,0:T(8,128)(2,1)S(1)}, bf16[80,1024]{1,0:T(8,128)(2,1)}, u32[]{:S(2)}, u32[]{:S(2)}) collective-permute-start(bf16[80,1024]{1,0:T(8,128)(2,1)S(1)} %reshape.79.refs_0_), channel_id=1, source_target_pairs={{0,3},{1,0},{2,1},{3,2},{4,7},{5,4},{6,5},{7,6},{8,11},{9,8},{10,9... | collective-permute-start | bytes 491528 | tf_op jit(solution)/shard_map/ppermute | solution.py:270
  40.0 1.1 copy.14
  41.1 1.9 %reshape.83 = bf16[8,80,256]{2,1,0:T(8,128)(2,1)} reshape(bf16[8,80,2,128]{3,2,1,0:T(2,128)(2,1)} %copy.14) | data formatting | bytes 655360 | tf_op jit(solution)/shard_map/reshape | solution.py:274
  43.0 0.7 pad_maximum_fusion
  43.7 2.3 %collective-permute-done.1.refs_1_ = bf16[80,1024]{1,0:T(8,128)(2,1)} collective-permute-done((bf16[80,1024]{1,0:T(8,128)(2,1)S(1)}, bf16[80,1024]{1,0:T(8,128)(2,1)}, u32[]{:S(2)}, u32[]{:S(2)}) %collective-permute-start.1) | collective-permute-done | bytes 163872 | tf_op jit(solution)/shard_map/ppermute | solution.py:270
  46.0 0.7 collective-permute-done.3.refs_3_
  46.7 6.9 %all-to-all-start.1 = ((bf16[8,80,256]{2,1,0:T(8,128)(2,1)}), bf16[8,80,256]{2,1,0:T(8,128)(2,1)S(1)}, u32[]{:S(2)}, u32[]{:S(2)}) async-start(bf16[8,80,256]{2,1,0:T(8,128)(2,1)} %reshape.83), calls=%async_computation.1 | async-start | bytes 655360 | tf_op jit(solution)/shard_map/all_to_all | solution.py:277
  53.8 3.6 %collective-permute-start.5 = (bf16[640,256]{1,0:T(8,128)(2,1)S(1)}, bf16[640,256]{1,0:T(8,128)(2,1)}, u32[]{:S(2)}, u32[]{:S(2)}) collective-permute-start(bf16[640,256]{1,0:T(8,128)(2,1)S(1)} %bitcast.51), channel_id=1, source_target_pairs={{0,2},{1,3},{2,0},{3,1},{4,6},{5,7},{6,4},{7,5},{8,10},{9,11},{10,... | collective-permute-start | bytes 983048 | tf_op jit(solution)/shard_map/ppermute | solution.py:270
  57.6 7.9 %collective-permute-done.4.refs_1_ = bf16[640,256]{1,0:T(8,128)(2,1)S(1)} collective-permute-done((bf16[640,256]{1,0:T(8,128)(2,1)S(1)}, bf16[640,256]{1,0:T(8,128)(2,1)S(1)}, u32[]{:S(2)}, u32[]{:S(2)}) %collective-permute-start.4) | collective-permute-done | bytes 327712 | tf_op jit(solution)/shard_map/ppermute | solution.py:270
  65.4 0.7 copy-done.4
  66.2 2.9 %collective-permute-done.5.refs_2_ = bf16[640,256]{1,0:T(8,128)(2,1)} collective-permute-done((bf16[640,256]{1,0:T(8,128)(2,1)S(1)}, bf16[640,256]{1,0:T(8,128)(2,1)}, u32[]{:S(2)}, u32[]{:S(2)}) %collective-permute-start.5) | collective-permute-done | bytes 327712 | tf_op jit(solution)/shard_map/ppermute | solution.py:270
  69.1 1.0 copy-done.5
  70.1 8.3 %attention.1 = (bf16[640,128]{1,0:T(8,128)(2,1)S(1)}, bf16[640,128]{1,0:T(8,128)(2,1)S(1)}, f32[640,256]{1,0:T(8,128)S(1)}, bf16[640,256]{1,0:T(8,128)(2,1)}, bf...) custom-call(s32[1]{0:T(128)} %bitcast.3.y_ref, bf16[640,256]{1,0:T(8,128)(2,1)S(1)} %bitcast.57, ...), custom_call_target="tpu_custom_call" | custom-call | tf_op jit(solution)/shard_map/attention/pallas_call | solution.py:98
  78.4 0.8 copy-done.3
  79.2 3.8 %collective-permute-start.8 = (bf16[640,256]{1,0:T(8,128)(2,1)}, bf16[640,256]{1,0:T(8,128)(2,1)}, u32[]{:S(2)}, u32[]{:S(2)}) collective-permute-start(bf16[640,256]{1,0:T(8,128)(2,1)} %get-tuple-element.54), channel_id=1, source_target_pairs={{0,2},{1,3},{2,0},{3,1},{4,6},{5,7},{6,4},{7,5},{8,10},{9,11},{10,... | collective-permute-start | bytes 983048 | tf_op jit(solution)/shard_map/ppermute | solution.py:270
  83.0 0.8 pad_maximum_fusion.1
  83.8 6.9 %all-to-all-start.2 = ((bf16[8,80,256]{2,1,0:T(8,128)(2,1)}), bf16[8,80,256]{2,1,0:T(8,128)(2,1)S(1)}, u32[]{:S(2)}, u32[]{:S(2)}) async-start(bf16[8,80,256]{2,1,0:T(8,128)(2,1)} %bitcast.58), calls=%async_computation.2 | async-start | bytes 655360 | tf_op jit(solution)/shard_map/all_to_all | solution.py:277
  90.8 6.0 %collective-permute-done.8 = bf16[640,256]{1,0:T(8,128)(2,1)} collective-permute-done((bf16[640,256]{1,0:T(8,128)(2,1)}, bf16[640,256]{1,0:T(8,128)(2,1)}, u32[]{:S(2)}, u32[]{:S(2)}) %collective-permute-start.8) | collective-permute-done | bytes 327712 | tf_op jit(solution)/shard_map/ppermute | solution.py:270
  96.8 1.5 convert_add_fusion
  98.3 0.3 fusion.3
  98.6 0.2 fusion.6
  98.9 0.8 pad_maximum_fusion.2.dkv_ref
  99.6 2.6 %all-to-all-done.2.first_ref = bf16[8,80,256]{2,1,0:T(8,128)(2,1)S(1)} async-done(((bf16[8,80,256]{2,1,0:T(8,128)(2,1)}), bf16[8,80,256]{2,1,0:T(8,128)(2,1)S(1)}, u32[]{:S(2)}, u32[]{:S(2)}) %all-to-all-start.2) | async-done | bytes 327712 | tf_op jit(solution)/shard_map/all_to_all | solution.py:277
  102.2 1.7 copy-done.2
  103.9 3.1 %head_grads.1 = bf16[4,8,32,512]{3,2,1,0:T(8,128)(2,1)} custom-call(bf16[640,2048]{1,0:T(8,128)(2,1)S(1)} %copy-done.2, bf16[640,128]{1,0:T(8,128)(2,1)S(1)} %get-tuple-element.51.dq_ref, bf16[640,256]{1,0:T(8,128)(2,1)} %pad_maximum_fusion.2.dkv_ref, bf16[640,128]{1,0:T(8,128)(2,1)S(1)} %get-tuple-element.50.attended_ref), custom_call_target="tpu_custom_call" | custom-call | tf_op jit(solution)/shard_map/head_grads/pallas_call | solution.py:168
  107.1 4.1 %all-to-all-start.3 = ((bf16[8,80,256]{2,1,0:T(8,128)(2,1)}), bf16[8,80,256]{2,1,0:T(8,128)(2,1)S(1)}, u32[]{:S(2)}, u32[]{:S(2)}) async-start(bf16[8,80,256]{2,1,0:T(8,128)(2,1)} %bitcast.6), calls=%async_computation.3 | async-start | bytes 655360 | tf_op jit(solution)/shard_map/all_to_all | solution.py:277
  111.3 11.7 %all-to-all-done.3.second_ref = bf16[8,80,256]{2,1,0:T(8,128)(2,1)S(1)} async-done(((bf16[8,80,256]{2,1,0:T(8,128)(2,1)}), bf16[8,80,256]{2,1,0:T(8,128)(2,1)S(1)}, u32[]{:S(2)}, u32[]{:S(2)}) %all-to-all-start.3) | async-done | bytes 327712 | tf_op jit(solution)/shard_map/all_to_all | solution.py:277
  123.0 2.9 %copy-done.1 = bf16[1024,3072]{1,0:T(8,128)(2,1)S(1)} copy-done((bf16[1024,3072]{1,0:T(8,128)(2,1)S(1)}, bf16[1024,3072]{1,0:T(8,128)(2,1)}, u32[]{:S(2)}) %copy-start.1) | copy-done | bytes 6291480
  125.9 2.2 %hidden_grad.1 = (bf16[80,1024]{1,0:T(8,128)(2,1)S(1)}, bf16[80,256]{1,0:T(8,128)(2,1)S(1)}, bf16[80,256]{1,0:T(8,128)(2,1)S(1)}, bf16[80,256]{1,0:T(8,128)(2,1)S(1)}, bf16[80,256]{1,0:T(8,128)(2,1)S(1)}) custom-call(s32[1]{0:T(128)} %bitcast.3.y_ref, bf16[8,80,256]{2,1,0:T(8,128)(2,1)S(1)} %all-to-all-done.2.first_ref, ...), custom_call_target="tpu_custom_call" | custom-call | tf_op jit(solution)/shard_map/hidden_grad/pallas_call | solution.py:138
  128.1 0.6 copy-done.6
  128.7 2.1 %reduce-scatter.2.cloned.1.call-done = bf16[1,8,32,512]{3,2,1,0:T(8,128)(2,1)} async-done(((bf16[4,8,32,512]{3,2,1,0:T(8,128)(2,1)}), bf16[1,8,32,512]{3,2,1,0:T(8,128)(2,1)}) %reduce-scatter.2.cloned.1.call-update) | async-done | bytes 262160 | tf_op jit(solution)/shard_map/reduce_scatter | solution.py:314
  130.8 7.0 %all-to-all-start.4 = ((bf16[8,32,512]{2,1,0:T(8,128)(2,1)}), bf16[8,32,512]{2,1,0:T(8,128)(2,1)S(1)}, u32[]{:S(2)}, u32[]{:S(2)}) async-start(bf16[8,32,512]{2,1,0:T(8,128)(2,1)} %bitcast.59), calls=%async_computation.5 | async-start | bytes 524288 | tf_op jit(solution)/shard_map/all_to_all | solution.py:277
  137.8 2.2 %collective-permute-start.11 = (bf16[80,256]{1,0:T(8,128)(2,1)S(1)}, bf16[80,256]{1,0:T(8,128)(2,1)S(1)}, u32[]{:S(2)}, u32[]{:S(2)}) collective-permute-start(bf16[80,256]{1,0:T(8,128)(2,1)S(1)} %get-tuple-element.62), channel_id=1, source_target_pairs={{0,2},{1,3},{2,0},{3,1},{4,6},{5,7},{6,4},{7,5},{8,10},{9,11},{10,... | collective-permute-start | bytes 122888 | tf_op jit(solution)/shard_map/ppermute | solution.py:270
  139.9 1.9 %collective-permute-start.12 = (bf16[80,256]{1,0:T(8,128)(2,1)S(1)}, bf16[80,256]{1,0:T(8,128)(2,1)S(1)}, u32[]{:S(2)}, u32[]{:S(2)}) collective-permute-start(bf16[80,256]{1,0:T(8,128)(2,1)S(1)} %get-tuple-element.63), channel_id=1, source_target_pairs={{0,3},{1,0},{2,1},{3,2},{4,7},{5,4},{6,5},{7,6},{8,11},{9,8},{10,9... | collective-permute-start | bytes 122888 | tf_op jit(solution)/shard_map/ppermute | solution.py:270
  141.8 0.8 convolution_convert_fusion.1
  142.7 0.3 collective-permute-done.10.refs_5_
  143.0 0.4 collective-permute-done.11.refs_6_
  143.4 0.9 collective-permute-done.12.refs_7_
  144.3 0.6 copy-done.13
  144.9 2.4 %short_grads.1 = bf16[32,64,128]{2,1,0:T(8,128)(2,1)} custom-call(bf16[80,1024]{1,0:T(8,128)(2,1)} %copy-done.8, bf16[80,1024]{1,0:T(8,128)(2,1)} %collective-permute-done.1.refs_1_, bf16[80,1024]{1,0:T(8,128)(2,1)} %collective-permute-done.2.refs_2_, bf16[80,1024]{1,0:T(8,128)(2,1)} %collective-permute-done.3.refs_3_, bf16[80,256]{1,0:T(8,128)(2,1)} %copy-done.6, ...), custom_call_target="tpu_custom_call" | custom-call | tf_op jit(solution)/shard_map/short_grads/pallas_call | solution.py:194
  147.3 0.9 all-to-all-done.4.came_ref
  148.2 0.7 copy-done.9
  149.0 8.9 %all-to-all-start.5 = ((bf16[32,64,128]{2,1,0:T(8,128)(2,1)}), bf16[32,64,128]{2,1,0:T(8,128)(2,1)S(1)}, u32[]{:S(2)}, u32[]{:S(2)}) async-start(bf16[32,64,128]{2,1,0:T(8,128)(2,1)} %short_grads.1), calls=%async_computation.6 | async-start | bytes 1048576 | tf_op jit(solution)/shard_map/all_to_all | solution.py:323
  157.9 1.3 collective-permute-start.13
  159.2 4.1 %collective-permute-done.13 = bf16[3,256]{1,0:T(4,128)(2,1)S(1)} collective-permute-done((bf16[3,256]{1,0:T(4,128)(2,1)S(1)}, bf16[3,256]{1,0:T(4,128)(2,1)S(1)}, u32[]{:S(2)}, u32[]{:S(2)}) %collective-permute-start.13) | collective-permute-done | bytes 1568 | tf_op jit(solution)/shard_map/ppermute | solution.py:330
  163.4 0.7 add_convert_fusion.1
  164.1 2.1 %fusion.8 = f32[80,1024]{1,0:T(8,128)S(1)} fusion(bf16[1024,1024]{1,0:T(8,128)(2,1)} %param.8, bf16[8,80,256]{2,1,0:T(8,128)(2,1)S(1)} %all-to-all-done.2.first_ref), kind=kOutput, calls=%fused_computation.23 | convolution fusion | flops 167772160 | bytes 2588672 | tf_op jit(solution)/shard_map/dot_general | solution.py:21
  166.3 1.9 %assemble_heads.1 = (f32[32,1024]{1,0:T(8,128)}, f32[32,3072]{1,0:T(8,128)}) custom-call(bf16[8,32,512]{2,1,0:T(8,128)(2,1)} %bitcast.60, bf16[8,32,512]{2,1,0:T(8,128)(2,1)} %copy-done.9), custom_call_target="tpu_custom_call" | custom-call | tf_op jit(solution)/shard_map/assemble_heads/pallas_call | solution.py:218
  168.1 1.6 add_convert_fusion
  169.7 3.2 %all-to-all-done.5.parts_ref = bf16[32,64,128]{2,1,0:T(8,128)(2,1)S(1)} async-done(((bf16[32,64,128]{2,1,0:T(8,128)(2,1)}), bf16[32,64,128]{2,1,0:T(8,128)(2,1)S(1)}, u32[]{:S(2)}, u32[]{:S(2)}) %all-to-all-start.5) | async-done | bytes 524320 | tf_op jit(solution)/shard_map/all_to_all | solution.py:323
  172.9 0.8 copy-done.7
  173.7 1.8 assemble_short.1
  (55 shorter events, 1.5 us)
Async XLA Ops:
  7.2 6.7 %copy-start = (bf16[1024,1024]{1,0:T(8,128)(2,1)S(1)}, bf16[1024,1024]{1,0:T(8,128)(2,1)}, u32[]{:S(2)}) copy-start(bf16[1024,1024]{1,0:T(8,128)(2,1)} %param.6) | copy-start | bytes 6291460
  8.0 4.8 %collective-permute-start = (bf16[3,256]{1,0:T(4,128)(2,1)S(1)}, bf16[3,256]{1,0:T(4,128)(2,1)S(1)}, u32[]{:S(2)}, u32[]{:S(2)}) collective-permute-start(bf16[3,256]{1,0:T(4,128)(2,1)S(1)} %slice.34), channel_id=1, source_target_pairs={{0,1},{1,2},{2,3},{3,4},{4,5},{5,6},{6,7},{7,8},{8,9},{9,10},{10,1... | collective-permute-start | bytes 4616 | tf_op jit(solution)/shard_map/ppermute | solution.py:280
  13.9 24.0 %copy-start.8 = (bf16[80,1024]{1,0:T(8,128)(2,1)}, bf16[80,1024]{1,0:T(8,128)(2,1)S(1)}, u32[]{:S(2)}) copy-start(bf16[80,1024]{1,0:T(8,128)(2,1)S(1)} %reshape.79.refs_0_) | copy-start | bytes 491524
  21.7 25.0 %all-to-all-start = ((bf16[8,80,256]{2,1,0:T(8,128)(2,1)}), bf16[8,80,256]{2,1,0:T(8,128)(2,1)S(1)}, u32[]{:S(2)}, u32[]{:S(2)}) async-start(bf16[8,80,256]{2,1,0:T(8,128)(2,1)} %reshape.80), calls=%async_computation | async-start | bytes 655360 | tf_op jit(solution)/shard_map/all_to_all | solution.py:277
  34.2 68.0 %all-gather.2.cloned.1.call-start = ((), (), s32[]{:S(2)}) async-start(), calls=%async_computation.7 | async-start | bytes 2949120 | tf_op jit(solution)/shard_map/all_gather | solution.py:293
  36.6 9.4 %collective-permute-start.1 = (bf16[80,1024]{1,0:T(8,128)(2,1)S(1)}, bf16[80,1024]{1,0:T(8,128)(2,1)}, u32[]{:S(2)}, u32[]{:S(2)}) collective-permute-start(bf16[80,1024]{1,0:T(8,128)(2,1)S(1)} %reshape.79.refs_0_), channel_id=1, source_target_pairs={{0,1},{1,2},{2,3},{3,0},{4,5},{5,6},{6,7},{7,4},{8,9},{9,10},{10,1... | collective-permute-start | bytes 491528 | tf_op jit(solution)/shard_map/ppermute | solution.py:270
  36.7 9.3 %collective-permute-start.2 = (bf16[80,1024]{1,0:T(8,128)(2,1)S(1)}, bf16[80,1024]{1,0:T(8,128)(2,1)}, u32[]{:S(2)}, u32[]{:S(2)}) collective-permute-start(bf16[80,1024]{1,0:T(8,128)(2,1)S(1)} %reshape.79.refs_0_), channel_id=1, source_target_pairs={{0,2},{1,3},{2,0},{3,1},{4,6},{5,7},{6,4},{7,5},{8,10},{9,11},{10,... | collective-permute-start | bytes 491528 | tf_op jit(solution)/shard_map/ppermute | solution.py:270
  37.9 8.8 %collective-permute-start.3 = (bf16[80,1024]{1,0:T(8,128)(2,1)S(1)}, bf16[80,1024]{1,0:T(8,128)(2,1)}, u32[]{:S(2)}, u32[]{:S(2)}) collective-permute-start(bf16[80,1024]{1,0:T(8,128)(2,1)S(1)} %reshape.79.refs_0_), channel_id=1, source_target_pairs={{0,3},{1,0},{2,1},{3,2},{4,7},{5,4},{6,5},{7,6},{8,11},{9,8},{10,9... | collective-permute-start | bytes 491528 | tf_op jit(solution)/shard_map/ppermute | solution.py:270
  46.7 22.4 %all-to-all-start.1 = ((bf16[8,80,256]{2,1,0:T(8,128)(2,1)}), bf16[8,80,256]{2,1,0:T(8,128)(2,1)S(1)}, u32[]{:S(2)}, u32[]{:S(2)}) async-start(bf16[8,80,256]{2,1,0:T(8,128)(2,1)} %reshape.83), calls=%async_computation.1 | async-start | bytes 655360 | tf_op jit(solution)/shard_map/all_to_all | solution.py:277
  53.6 11.8 %collective-permute-start.4 = (bf16[640,256]{1,0:T(8,128)(2,1)S(1)}, bf16[640,256]{1,0:T(8,128)(2,1)S(1)}, u32[]{:S(2)}, u32[]{:S(2)}) collective-permute-start(bf16[640,256]{1,0:T(8,128)(2,1)S(1)} %bitcast.50), channel_id=1, source_target_pairs={{0,1},{1,2},{2,3},{3,0},{4,5},{5,6},{6,7},{7,4},{8,9},{9,10},{10,1... | collective-permute-start | bytes 983048 | tf_op jit(solution)/shard_map/ppermute | solution.py:270
  53.8 15.3 %collective-permute-start.5 = (bf16[640,256]{1,0:T(8,128)(2,1)S(1)}, bf16[640,256]{1,0:T(8,128)(2,1)}, u32[]{:S(2)}, u32[]{:S(2)}) collective-permute-start(bf16[640,256]{1,0:T(8,128)(2,1)S(1)} %bitcast.51), channel_id=1, source_target_pairs={{0,2},{1,3},{2,0},{3,1},{4,6},{5,7},{6,4},{7,5},{8,10},{9,11},{10,... | collective-permute-start | bytes 983048 | tf_op jit(solution)/shard_map/ppermute | solution.py:270
  57.4 11.7 %collective-permute-start.6 = (bf16[640,256]{1,0:T(8,128)(2,1)S(1)}, bf16[640,256]{1,0:T(8,128)(2,1)}, u32[]{:S(2)}, u32[]{:S(2)}) collective-permute-start(bf16[640,256]{1,0:T(8,128)(2,1)S(1)} %bitcast.52), channel_id=1, source_target_pairs={{0,3},{1,0},{2,1},{3,2},{4,7},{5,4},{6,5},{7,6},{8,11},{9,8},{10,9... | collective-permute-start | bytes 983048 | tf_op jit(solution)/shard_map/ppermute | solution.py:270
  65.4 0.7 copy-start.4
  69.1 1.0 copy-start.5
  78.4 0.8 copy-start.3
  79.2 11.6 %collective-permute-start.9 = (bf16[640,256]{1,0:T(8,128)(2,1)}, bf16[640,256]{1,0:T(8,128)(2,1)}, u32[]{:S(2)}, u32[]{:S(2)}) collective-permute-start(bf16[640,256]{1,0:T(8,128)(2,1)} %get-tuple-element.55), channel_id=1, source_target_pairs={{0,1},{1,2},{2,3},{3,0},{4,5},{5,6},{6,7},{7,4},{8,9},{9,10},{10,1... | collective-permute-start | bytes 983048 | tf_op jit(solution)/shard_map/ppermute | solution.py:270
  79.2 17.6 %collective-permute-start.8 = (bf16[640,256]{1,0:T(8,128)(2,1)}, bf16[640,256]{1,0:T(8,128)(2,1)}, u32[]{:S(2)}, u32[]{:S(2)}) collective-permute-start(bf16[640,256]{1,0:T(8,128)(2,1)} %get-tuple-element.54), channel_id=1, source_target_pairs={{0,2},{1,3},{2,0},{3,1},{4,6},{5,7},{6,4},{7,5},{8,10},{9,11},{10,... | collective-permute-start | bytes 983048 | tf_op jit(solution)/shard_map/ppermute | solution.py:270
  83.0 13.8 %collective-permute-start.7 = (bf16[640,256]{1,0:T(8,128)(2,1)}, bf16[640,256]{1,0:T(8,128)(2,1)}, u32[]{:S(2)}, u32[]{:S(2)}) collective-permute-start(bf16[640,256]{1,0:T(8,128)(2,1)} %get-tuple-element.53), channel_id=1, source_target_pairs={{0,3},{1,0},{2,1},{3,2},{4,7},{5,4},{6,5},{7,6},{8,11},{9,8},{10,9... | collective-permute-start | bytes 983048 | tf_op jit(solution)/shard_map/ppermute | solution.py:270
  83.8 18.4 %all-to-all-start.2 = ((bf16[8,80,256]{2,1,0:T(8,128)(2,1)}), bf16[8,80,256]{2,1,0:T(8,128)(2,1)S(1)}, u32[]{:S(2)}, u32[]{:S(2)}) async-start(bf16[8,80,256]{2,1,0:T(8,128)(2,1)} %bitcast.58), calls=%async_computation.2 | async-start | bytes 655360 | tf_op jit(solution)/shard_map/all_to_all | solution.py:277
  90.7 40.0 %reduce-scatter.2.cloned.1.call-start = ((), (), s32[]{:S(2)}) async-start(), calls=%async_computation.8 | async-start | bytes 1310720 | tf_op jit(solution)/shard_map/reduce_scatter | solution.py:314
  102.2 1.7 copy-start.2
  107.1 15.9 %all-to-all-start.3 = ((bf16[8,80,256]{2,1,0:T(8,128)(2,1)}), bf16[8,80,256]{2,1,0:T(8,128)(2,1)S(1)}, u32[]{:S(2)}, u32[]{:S(2)}) async-start(bf16[8,80,256]{2,1,0:T(8,128)(2,1)} %bitcast.6), calls=%async_computation.3 | async-start | bytes 655360 | tf_op jit(solution)/shard_map/all_to_all | solution.py:277
  123.0 2.9 %copy-start.1 = (bf16[1024,3072]{1,0:T(8,128)(2,1)S(1)}, bf16[1024,3072]{1,0:T(8,128)(2,1)}, u32[]{:S(2)}) copy-start(bf16[1024,3072]{1,0:T(8,128)(2,1)} %weight_ref.1) | copy-start | bytes 18874372
  128.1 0.6 copy-start.6
  130.8 17.5 %all-to-all-start.4 = ((bf16[8,32,512]{2,1,0:T(8,128)(2,1)}), bf16[8,32,512]{2,1,0:T(8,128)(2,1)S(1)}, u32[]{:S(2)}, u32[]{:S(2)}) async-start(bf16[8,32,512]{2,1,0:T(8,128)(2,1)} %bitcast.59), calls=%async_computation.5 | async-start | bytes 524288 | tf_op jit(solution)/shard_map/all_to_all | solution.py:277
  137.8 5.2 %collective-permute-start.10 = (bf16[80,256]{1,0:T(8,128)(2,1)S(1)}, bf16[80,256]{1,0:T(8,128)(2,1)S(1)}, u32[]{:S(2)}, u32[]{:S(2)}) collective-permute-start(bf16[80,256]{1,0:T(8,128)(2,1)S(1)} %get-tuple-element.61), channel_id=1, source_target_pairs={{0,1},{1,2},{2,3},{3,0},{4,5},{5,6},{6,7},{7,4},{8,9},{9,10},{10,1... | collective-permute-start | bytes 122888 | tf_op jit(solution)/shard_map/ppermute | solution.py:270
  137.8 5.6 %collective-permute-start.11 = (bf16[80,256]{1,0:T(8,128)(2,1)S(1)}, bf16[80,256]{1,0:T(8,128)(2,1)S(1)}, u32[]{:S(2)}, u32[]{:S(2)}) collective-permute-start(bf16[80,256]{1,0:T(8,128)(2,1)S(1)} %get-tuple-element.62), channel_id=1, source_target_pairs={{0,2},{1,3},{2,0},{3,1},{4,6},{5,7},{6,4},{7,5},{8,10},{9,11},{10,... | collective-permute-start | bytes 122888 | tf_op jit(solution)/shard_map/ppermute | solution.py:270
  139.9 4.3 %collective-permute-start.12 = (bf16[80,256]{1,0:T(8,128)(2,1)S(1)}, bf16[80,256]{1,0:T(8,128)(2,1)S(1)}, u32[]{:S(2)}, u32[]{:S(2)}) collective-permute-start(bf16[80,256]{1,0:T(8,128)(2,1)S(1)} %get-tuple-element.63), channel_id=1, source_target_pairs={{0,3},{1,0},{2,1},{3,2},{4,7},{5,4},{6,5},{7,6},{8,11},{9,8},{10,9... | collective-permute-start | bytes 122888 | tf_op jit(solution)/shard_map/ppermute | solution.py:270
  142.7 20.6 %copy-start.10 = (bf16[320,256]{1,0:T(8,128)(2,1)S(1)}, bf16[320,256]{1,0:T(8,128)(2,1)}, u32[]{:S(2)}) copy-start(bf16[320,256]{1,0:T(8,128)(2,1)} %param.9) | copy-start | bytes 491524
  143.0 1.3 copy-start.11
  143.4 0.9 copy-start.12
  144.3 0.6 copy-start.13
  148.2 0.7 copy-start.9
  149.0 24.0 %all-to-all-start.5 = ((bf16[32,64,128]{2,1,0:T(8,128)(2,1)}), bf16[32,64,128]{2,1,0:T(8,128)(2,1)S(1)}, u32[]{:S(2)}, u32[]{:S(2)}) async-start(bf16[32,64,128]{2,1,0:T(8,128)(2,1)} %short_grads.1), calls=%async_computation.6 | async-start | bytes 1048576 | tf_op jit(solution)/shard_map/all_to_all | solution.py:323
  157.9 5.5 %collective-permute-start.13 = (bf16[3,256]{1,0:T(4,128)(2,1)S(1)}, bf16[3,256]{1,0:T(4,128)(2,1)S(1)}, u32[]{:S(2)}, u32[]{:S(2)}) collective-permute-start(bf16[3,256]{1,0:T(4,128)(2,1)S(1)} %slice.43), channel_id=1, source_target_pairs={{1,0},{2,1},{3,2},{4,3},{5,4},{6,5},{7,6},{8,7},{9,8},{10,9},{11,1... | collective-permute-start | bytes 4616 | tf_op jit(solution)/shard_map/ppermute | solution.py:330
  172.9 0.8 copy-start.7
Sparse Core Ops, SparseCore 0:
  46.9 43.6 all-gather.1
  107.2 23.5 reduce-scatter.1

commit v5 on v3

--- a/solution.py
+++ b/solution.py
@@ -330,8 +330,8 @@
     ).astype(jnp.bfloat16)
     first_back, d_kv = tie(first_back, d_kv)
     parts = head_grads(gathered, d_query, d_kv, attended, model_width, z_size, y_size)
-    parts, d_kv = tie(parts, d_kv)
     second_back = swap(d_kv.reshape(HEADS, short_rows, 2 * head_size))
+    second_back, parts = tie(second_back, parts)
     parts = lax.psum_scatter(parts, "y", scatter_dimension=0)
     d_hidden, *d_hidden_y = hidden_grad(y, first_back, second_back, w_attend, normed, hidden_scale, y_size)
     d_hidden_y = d_hidden_y[:1] + [turn_y(d_hidden_y[step], step) for step in range(1, y_size)]

time: 186 us -> 182 us (0.978)
  waiting for transfers between devices: 39.3 us -> 35.9 us
    all_to_all x4, waiting for transfers between devices: 14.3 us -> 8.61 us  [swap(): return lax.all_to_all(value, 'z', 0, 0)]
    ppermute x12, waiting for transfers between devices: 22.9 us -> 25.1 us  [turn_y(): lax.ppermute(value, 'y', [(i, (i + steps) % y_size) for i in range(y_size)])]
    ppermute x12, starting transfers between devices: 16 us -> 13.9 us  [turn_y(): lax.ppermute(value, 'y', [(i, (i + steps) % y_size) for i in range(y_size)])]
    all_to_all x4, starting transfers between devices: 30.5 us -> 32.6 us  [swap(): return lax.all_to_all(value, 'z', 0, 0)]
  transfers between devices with their start and end apart: 28 -> 28, of which waited for: 12 -> 12; matrix products, arithmetic and copies ran while one was open for 9% -> 9% of each run, Pallas kernels for 9% -> 11%
where the time goes in v5:
time: 182 us; the launch traced here: 181 us
  starting transfers between devices  76.2 us (42%)
  waiting for transfers between devices  35.9 us (20%)
  Pallas kernels  21.2 us (12%)
  local copies, waits for them, and re-layouts  15.6 us (9%)
  between operations  14.4 us (8%)
  matrix products  9.77 us (5%)
  other arithmetic  7.92 us (4%)
    all_to_all x4, starting transfers between devices, swap(): return lax.all_to_all(value, 'z', 0, 0)  32.6 us
    ppermute x12, waiting for transfers between devices, turn_y(): lax.ppermute(value, 'y', [(i, (i + steps) % y_size) for i in range(y_size)])  25.1 us
    ppermute x7, starting transfers between devices, local(): lax.ppermute(pieces[step], 'z', [(i, (i + step) % z_size) for i in range(...  20.2 us
    ppermute x12, starting transfers between devices, turn_y(): lax.ppermute(value, 'y', [(i, (i + steps) % y_size) for i in range(y_size)])  13.9 us
    dot_general x5, matrix products, mm(): lax.dot_general(left, right, dims, preferred_element_type=jnp.float32)  9.77 us
    unnamed x43, local copies, waits for them, and re-layouts  9.03 us
    all_to_all x4, waiting for transfers between devices, swap(): return lax.all_to_all(value, 'z', 0, 0)  8.61 us
    pallas_call x1, Pallas kernels, attention(): pl.pallas_call(functools.partial(attention_body, block, shards), out_shap...  8.31 us
  transfers between devices with their start and end apart: 28, of which 12 were waited for; matrix products, arithmetic and copies ran while one was open for 9% of the time, Pallas kernels for 11%

profile of v5, /device:TPU:6, one launch (start us, length us, event | category | flops | bytes accessed | tf_op | source)
XLA Modules:
  0.0 181.0 jit_solution(10892315356674088848)
XLA Ops:
  7.2 0.8 slice.34
  8.0 3.5 %collective-permute-start = (bf16[3,256]{1,0:T(4,128)(2,1)S(1)}, bf16[3,256]{1,0:T(4,128)(2,1)S(1)}, u32[]{:S(2)}, u32[]{:S(2)}) collective-permute-start(bf16[3,256]{1,0:T(4,128)(2,1)S(1)} %slice.34), channel_id=1, source_target_pairs={{0,1},{1,2},{2,3},{3,4},{4,5},{5,6},{6,7},{7,8},{8,9},{9,10},{10,1... | collective-permute-start | bytes 4616 | tf_op jit(solution)/shard_map/ppermute | solution.py:301
  11.5 1.0 reshape.85
  12.8 1.0 pad_maximum_fusion.3
  13.9 0.6 multiply_reduce_fusion
  14.6 4.0 %convolution_convert_fusion = bf16[80,3072]{1,0:T(8,128)(2,1)S(1)} fusion(bf16[80,1024]{1,0:T(8,128)(2,1)S(1)} %get-tuple-element.89, bf16[1024,3072]{1,0:T(8,128)(2,1)} %weight_ref.1), kind=kOutput, calls=%fused_computation | convolution fusion | flops 503562240 | bytes 6946816 | tf_op jit(solution)/shard_map/dot_general | solution.py:21
  19.1 0.9 reshape.83
  20.0 12.5 %all-to-all-start = ((bf16[8,80,256]{2,1,0:T(8,128)(2,1)}), bf16[8,80,256]{2,1,0:T(8,128)(2,1)S(1)}, u32[]{:S(2)}, u32[]{:S(2)}) async-start(bf16[8,80,256]{2,1,0:T(8,128)(2,1)} %reshape.83), calls=%async_computation | async-start | bytes 655360 | tf_op jit(solution)/shard_map/all_to_all | solution.py:298
  32.6 2.4 %fusion = bf16[10,8,8,128]{3,1,2,0:T(8,128)(2,1)S(1)} fusion(bf16[80,1024]{1,0:T(8,128)(2,1)S(1)} %reshape.85, bf16[1024,1024]{1,0:T(8,128)(2,1)} %param.8), kind=kOutput, calls=%fused_computation.3 | convolution fusion | flops 167854080 | bytes 2424832 | tf_op jit(solution)/shard_map/dot_general | solution.py:21
  35.0 1.1 collective-permute-start.2
  36.2 2.1 %collective-permute-start.3 = (bf16[80,1024]{1,0:T(8,128)(2,1)S(1)}, bf16[80,1024]{1,0:T(8,128)(2,1)}, u32[]{:S(2)}, u32[]{:S(2)}) collective-permute-start(bf16[80,1024]{1,0:T(8,128)(2,1)S(1)} %reshape.82.refs_0_), channel_id=1, source_target_pairs={{0,3},{1,0},{2,1},{3,2},{4,7},{5,4},{6,5},{7,6},{8,11},{9,8},{10,9... | collective-permute-start | bytes 491528 | tf_op jit(solution)/shard_map/ppermute | solution.py:291
  38.3 1.1 copy.14
  39.4 1.9 %reshape.86 = bf16[8,80,256]{2,1,0:T(8,128)(2,1)} reshape(bf16[8,80,2,128]{3,2,1,0:T(2,128)(2,1)} %copy.14) | data formatting | bytes 655360 | tf_op jit(solution)/shard_map/reshape | solution.py:295
  41.3 0.7 pad_maximum_fusion
  42.0 2.3 %collective-permute-done.1.refs_1_ = bf16[80,1024]{1,0:T(8,128)(2,1)} collective-permute-done((bf16[80,1024]{1,0:T(8,128)(2,1)S(1)}, bf16[80,1024]{1,0:T(8,128)(2,1)}, u32[]{:S(2)}, u32[]{:S(2)}) %collective-permute-start.1) | collective-permute-done | bytes 163872 | tf_op jit(solution)/shard_map/ppermute | solution.py:291
  44.4 0.6 collective-permute-done.3.refs_3_
  45.0 6.9 %all-to-all-start.1 = ((bf16[8,80,256]{2,1,0:T(8,128)(2,1)}), bf16[8,80,256]{2,1,0:T(8,128)(2,1)S(1)}, u32[]{:S(2)}, u32[]{:S(2)}) async-start(bf16[8,80,256]{2,1,0:T(8,128)(2,1)} %reshape.86), calls=%async_computation.1 | async-start | bytes 655360 | tf_op jit(solution)/shard_map/all_to_all | solution.py:298
  52.2 3.6 %collective-permute-start.5 = (bf16[640,256]{1,0:T(8,128)(2,1)S(1)}, bf16[640,256]{1,0:T(8,128)(2,1)}, u32[]{:S(2)}, u32[]{:S(2)}) collective-permute-start(bf16[640,256]{1,0:T(8,128)(2,1)S(1)} %bitcast.52), channel_id=1, source_target_pairs={{0,2},{1,3},{2,0},{3,1},{4,6},{5,7},{6,4},{7,5},{8,10},{9,11},{10,... | collective-permute-start | bytes 983048 | tf_op jit(solution)/shard_map/ppermute | solution.py:291
  55.9 7.9 %collective-permute-done.4.refs_1_ = bf16[640,256]{1,0:T(8,128)(2,1)S(1)} collective-permute-done((bf16[640,256]{1,0:T(8,128)(2,1)S(1)}, bf16[640,256]{1,0:T(8,128)(2,1)S(1)}, u32[]{:S(2)}, u32[]{:S(2)}) %collective-permute-start.4) | collective-permute-done | bytes 327712 | tf_op jit(solution)/shard_map/ppermute | solution.py:291
  63.8 0.7 copy-done.4
  64.5 2.9 %collective-permute-done.5.refs_2_ = bf16[640,256]{1,0:T(8,128)(2,1)} collective-permute-done((bf16[640,256]{1,0:T(8,128)(2,1)S(1)}, bf16[640,256]{1,0:T(8,128)(2,1)}, u32[]{:S(2)}, u32[]{:S(2)}) %collective-permute-start.5) | collective-permute-done | bytes 327712 | tf_op jit(solution)/shard_map/ppermute | solution.py:291
  67.4 1.0 copy-done.5
  68.4 8.3 %attention.1 = (bf16[640,128]{1,0:T(8,128)(2,1)S(1)}, bf16[640,128]{1,0:T(8,128)(2,1)S(1)}, f32[640,256]{1,0:T(8,128)S(1)}, bf16[640,256]{1,0:T(8,128)(2,1)}, bf...) custom-call(s32[1]{0:T(128)} %bitcast.3.y_ref, bf16[640,256]{1,0:T(8,128)(2,1)S(1)} %bitcast.58, ...), custom_call_target="tpu_custom_call" | custom-call | tf_op jit(solution)/shard_map/attention/pallas_call | solution.py:98
  76.7 0.8 copy-done.3
  77.6 2.4 %collective-permute-start.7 = (bf16[640,256]{1,0:T(8,128)(2,1)}, bf16[640,256]{1,0:T(8,128)(2,1)}, u32[]{:S(2)}, u32[]{:S(2)}) collective-permute-start(bf16[640,256]{1,0:T(8,128)(2,1)} %get-tuple-element.56), channel_id=1, source_target_pairs={{0,3},{1,0},{2,1},{3,2},{4,7},{5,4},{6,5},{7,6},{8,11},{9,8},{10,9... | collective-permute-start | bytes 983048 | tf_op jit(solution)/shard_map/ppermute | solution.py:291
  79.9 0.9 collective-permute-start.9
  80.8 0.8 pad_maximum_fusion.1
  81.6 6.9 %all-to-all-start.2 = ((bf16[8,80,256]{2,1,0:T(8,128)(2,1)}), bf16[8,80,256]{2,1,0:T(8,128)(2,1)S(1)}, u32[]{:S(2)}, u32[]{:S(2)}) async-start(bf16[8,80,256]{2,1,0:T(8,128)(2,1)} %bitcast.59), calls=%async_computation.2 | async-start | bytes 655360 | tf_op jit(solution)/shard_map/all_to_all | solution.py:298
  88.5 4.7 %collective-permute-done.7 = bf16[640,256]{1,0:T(8,128)(2,1)} collective-permute-done((bf16[640,256]{1,0:T(8,128)(2,1)}, bf16[640,256]{1,0:T(8,128)(2,1)}, u32[]{:S(2)}, u32[]{:S(2)}) %collective-permute-start.7) | collective-permute-done | bytes 327712 | tf_op jit(solution)/shard_map/ppermute | solution.py:291
  93.2 3.4 %collective-permute-done.9 = bf16[640,256]{1,0:T(8,128)(2,1)} collective-permute-done((bf16[640,256]{1,0:T(8,128)(2,1)}, bf16[640,256]{1,0:T(8,128)(2,1)}, u32[]{:S(2)}, u32[]{:S(2)}) %collective-permute-start.9) | collective-permute-done | bytes 327712 | tf_op jit(solution)/shard_map/ppermute | solution.py:291
  96.7 1.5 convert_add_fusion
  98.7 0.8 pad_maximum_fusion.2.dkv_ref
  99.5 0.4 all-to-all-done.2.first_ref
  99.9 6.2 %all-to-all-start.3 = ((bf16[8,80,256]{2,1,0:T(8,128)(2,1)}), bf16[8,80,256]{2,1,0:T(8,128)(2,1)S(1)}, u32[]{:S(2)}, u32[]{:S(2)}) async-start(bf16[8,80,256]{2,1,0:T(8,128)(2,1)} %bitcast.6), calls=%async_computation.3 | async-start | bytes 655360 | tf_op jit(solution)/shard_map/all_to_all | solution.py:298
  106.2 1.7 copy-done.2
  107.9 3.1 %head_grads.1 = bf16[4,8,32,512]{3,2,1,0:T(8,128)(2,1)} custom-call(bf16[640,2048]{1,0:T(8,128)(2,1)S(1)} %copy-done.2, bf16[640,128]{1,0:T(8,128)(2,1)S(1)} %get-tuple-element.54.dq_ref, bf16[640,256]{1,0:T(8,128)(2,1)} %pad_maximum_fusion.2.dkv_ref, bf16[640,128]{1,0:T(8,128)(2,1)S(1)} %get-tuple-element.53.attended_ref), custom_call_target="tpu_custom_call" | custom-call | tf_op jit(solution)/shard_map/head_grads/pallas_call | solution.py:168
  111.1 8.2 %all-to-all-done.3.second_ref = bf16[8,80,256]{2,1,0:T(8,128)(2,1)S(1)} async-done(((bf16[8,80,256]{2,1,0:T(8,128)(2,1)}), bf16[8,80,256]{2,1,0:T(8,128)(2,1)S(1)}, u32[]{:S(2)}, u32[]{:S(2)}) %all-to-all-start.3) | async-done | bytes 327712 | tf_op jit(solution)/shard_map/all_to_all | solution.py:298
  119.4 2.8 %copy-done.1 = bf16[1024,3072]{1,0:T(8,128)(2,1)S(1)} copy-done((bf16[1024,3072]{1,0:T(8,128)(2,1)S(1)}, bf16[1024,3072]{1,0:T(8,128)(2,1)}, u32[]{:S(2)}) %copy-start.1) | copy-done | bytes 6291480
  122.1 2.2 %hidden_grad.1 = (bf16[80,1024]{1,0:T(8,128)(2,1)S(1)}, bf16[80,256]{1,0:T(8,128)(2,1)S(1)}, bf16[80,256]{1,0:T(8,128)(2,1)S(1)}, bf16[80,256]{1,0:T(8,128)(2,1)S(1)}, bf16[80,256]{1,0:T(8,128)(2,1)S(1)}) custom-call(s32[1]{0:T(128)} %bitcast.3.y_ref, bf16[8,80,256]{2,1,0:T(8,128)(2,1)S(1)} %all-to-all-done.2.first_ref, ...), custom_call_target="tpu_custom_call" | custom-call | tf_op jit(solution)/shard_map/hidden_grad/pallas_call | solution.py:138
  124.4 0.6 copy-done.6
  125.0 1.0 collective-permute-start.11
  126.0 2.6 %collective-permute-start.12 = (bf16[80,256]{1,0:T(8,128)(2,1)S(1)}, bf16[80,256]{1,0:T(8,128)(2,1)S(1)}, u32[]{:S(2)}, u32[]{:S(2)}) collective-permute-start(bf16[80,256]{1,0:T(8,128)(2,1)S(1)} %get-tuple-element.66), channel_id=1, source_target_pairs={{0,3},{1,0},{2,1},{3,2},{4,7},{5,4},{6,5},{7,6},{8,11},{9,8},{10,9... | collective-permute-start | bytes 122888 | tf_op jit(solution)/shard_map/ppermute | solution.py:291
  128.5 0.8 convolution_convert_fusion.1
  129.4 2.0 %collective-permute-done.10.refs_5_ = bf16[80,256]{1,0:T(8,128)(2,1)S(1)} collective-permute-done((bf16[80,256]{1,0:T(8,128)(2,1)S(1)}, bf16[80,256]{1,0:T(8,128)(2,1)S(1)}, u32[]{:S(2)}, u32[]{:S(2)}) %collective-permute-start.10) | collective-permute-done | bytes 40992 | tf_op jit(solution)/shard_map/ppermute | solution.py:291
  131.5 1.1 collective-permute-done.12.refs_7_
  132.6 0.6 copy-done.11
  133.2 2.5 %short_grads.1 = bf16[32,64,128]{2,1,0:T(8,128)(2,1)} custom-call(bf16[80,1024]{1,0:T(8,128)(2,1)} %copy-done.7, bf16[80,1024]{1,0:T(8,128)(2,1)} %collective-permute-done.1.refs_1_, bf16[80,1024]{1,0:T(8,128)(2,1)} %collective-permute-done.2.refs_2_, bf16[80,1024]{1,0:T(8,128)(2,1)} %collective-permute-done.3.refs_3_, bf16[80,256]{1,0:T(8,128)(2,1)} %copy-done.6, ...), custom_call_target="tpu_custom_call" | custom-call | tf_op jit(solution)/shard_map/short_grads/pallas_call | solution.py:218
  135.7 4.8 %all-to-all-start.4 = ((bf16[32,64,128]{2,1,0:T(8,128)(2,1)}), bf16[32,64,128]{2,1,0:T(8,128)(2,1)}, u32[]{:S(2)}, u32[]{:S(2)}) async-start(bf16[32,64,128]{2,1,0:T(8,128)(2,1)} %short_grads.1), calls=%async_computation.4 | async-start | bytes 1048576 | tf_op jit(solution)/shard_map/all_to_all | solution.py:342
  140.5 2.1 %fusion.8 = f32[80,1024]{1,0:T(8,128)S(1)} fusion(bf16[1024,1024]{1,0:T(8,128)(2,1)} %param.8, bf16[8,80,256]{2,1,0:T(8,128)(2,1)S(1)} %all-to-all-done.2.first_ref), kind=kOutput, calls=%fused_computation.23 | convolution fusion | flops 167772160 | bytes 2588672 | tf_op jit(solution)/shard_map/dot_general | solution.py:21
  142.7 1.3 collective-permute-start.13
  144.0 1.7 split_parts.1
  145.7 4.9 %collective-permute-start.14 = (bf16[32,384]{1,0:T(8,128)(2,1)}, bf16[32,384]{1,0:T(8,128)(2,1)S(1)}, u32[]{:S(2)}, u32[]{:S(2)}) collective-permute-start(bf16[32,384]{1,0:T(8,128)(2,1)} %get-tuple-element.77), channel_id=1, source_target_pairs={{0,4},{4,8},{8,12},{12,16},{16,20},{20,24},{24,28},{28,0},{1,5},{5... | collective-permute-start | bytes 73736 | tf_op jit(solution)/shard_map/ppermute | solution.py:346
  150.6 2.4 %collective-permute-start.15 = (bf16[32,384]{1,0:T(8,128)(2,1)}, bf16[32,384]{1,0:T(8,128)(2,1)S(1)}, u32[]{:S(2)}, u32[]{:S(2)}) collective-permute-start(bf16[32,384]{1,0:T(8,128)(2,1)} %get-tuple-element.78), channel_id=1, source_target_pairs={{0,8},{4,12},{8,16},{12,20},{16,24},{20,28},{24,0},{28,4},{1,9},{5... | collective-permute-start | bytes 73736 | tf_op jit(solution)/shard_map/ppermute | solution.py:346
  153.0 0.7 add_convert_fusion
  153.7 3.7 %collective-permute-start.16 = (bf16[32,384]{1,0:T(8,128)(2,1)}, bf16[32,384]{1,0:T(8,128)(2,1)S(1)}, u32[]{:S(2)}, u32[]{:S(2)}) collective-permute-start(bf16[32,384]{1,0:T(8,128)(2,1)} %get-tuple-element.79), channel_id=1, source_target_pairs={{0,12},{4,16},{8,20},{12,24},{16,28},{20,0},{24,4},{28,8},{1,13},{... | collective-permute-start | bytes 73736 | tf_op jit(solution)/shard_map/ppermute | solution.py:346
  157.5 1.4 collective-permute-start.17
  158.8 3.7 %collective-permute-start.18 = (bf16[32,384]{1,0:T(8,128)(2,1)}, bf16[32,384]{1,0:T(8,128)(2,1)S(1)}, u32[]{:S(2)}, u32[]{:S(2)}) collective-permute-start(bf16[32,384]{1,0:T(8,128)(2,1)} %get-tuple-element.81), channel_id=1, source_target_pairs={{0,20},{4,24},{8,28},{12,0},{16,4},{20,8},{24,12},{28,16},{1,21},{... | collective-permute-start | bytes 73736 | tf_op jit(solution)/shard_map/ppermute | solution.py:346
  162.5 3.5 %collective-permute-start.19 = (bf16[32,384]{1,0:T(8,128)(2,1)}, bf16[32,384]{1,0:T(8,128)(2,1)S(1)}, u32[]{:S(2)}, u32[]{:S(2)}) collective-permute-start(bf16[32,384]{1,0:T(8,128)(2,1)} %get-tuple-element.82), channel_id=1, source_target_pairs={{0,24},{4,28},{8,0},{12,4},{16,8},{20,12},{24,16},{28,20},{1,25},{... | collective-permute-start | bytes 73736 | tf_op jit(solution)/shard_map/ppermute | solution.py:346
  166.1 0.5 collective-permute-start.20
  166.6 1.6 add_convert_fusion.1
  168.3 1.8 %collective-permute-done.20.refs_7_ = bf16[32,384]{1,0:T(8,128)(2,1)S(1)} collective-permute-done((bf16[32,384]{1,0:T(8,128)(2,1)}, bf16[32,384]{1,0:T(8,128)(2,1)S(1)}, u32[]{:S(2)}, u32[]{:S(2)}) %collective-permute-start.20) | collective-permute-done | bytes 24608 | tf_op jit(solution)/shard_map/ppermute | solution.py:346
  170.1 0.6 copy-done.18
  170.7 1.6 assemble_attend.1
  172.4 1.8 assemble_short.1
  (78 shorter events, 2.6 us)
Async XLA Ops:
  7.2 6.7 %copy-start = (bf16[1024,1024]{1,0:T(8,128)(2,1)S(1)}, bf16[1024,1024]{1,0:T(8,128)(2,1)}, u32[]{:S(2)}) copy-start(bf16[1024,1024]{1,0:T(8,128)(2,1)} %param.6) | copy-start | bytes 6291460
  8.0 4.8 %collective-permute-start = (bf16[3,256]{1,0:T(4,128)(2,1)S(1)}, bf16[3,256]{1,0:T(4,128)(2,1)S(1)}, u32[]{:S(2)}, u32[]{:S(2)}) collective-permute-start(bf16[3,256]{1,0:T(4,128)(2,1)S(1)} %slice.34), channel_id=1, source_target_pairs={{0,1},{1,2},{2,3},{3,4},{4,5},{5,6},{6,7},{7,8},{8,9},{9,10},{10,1... | collective-permute-start | bytes 4616 | tf_op jit(solution)/shard_map/ppermute | solution.py:301
  13.9 22.3 %copy-start.7 = (bf16[80,1024]{1,0:T(8,128)(2,1)}, bf16[80,1024]{1,0:T(8,128)(2,1)S(1)}, u32[]{:S(2)}) copy-start(bf16[80,1024]{1,0:T(8,128)(2,1)S(1)} %reshape.82.refs_0_) | copy-start | bytes 491524
  20.0 25.0 %all-to-all-start = ((bf16[8,80,256]{2,1,0:T(8,128)(2,1)}), bf16[8,80,256]{2,1,0:T(8,128)(2,1)S(1)}, u32[]{:S(2)}, u32[]{:S(2)}) async-start(bf16[8,80,256]{2,1,0:T(8,128)(2,1)} %reshape.83), calls=%async_computation | async-start | bytes 655360 | tf_op jit(solution)/shard_map/all_to_all | solution.py:298
  32.5 73.7 %all-gather.2.cloned.1.call-start = ((), (), s32[]{:S(2)}) async-start(), calls=%async_computation.6 | async-start | bytes 2949120 | tf_op jit(solution)/shard_map/all_gather | solution.py:314
  35.0 9.4 %collective-permute-start.1 = (bf16[80,1024]{1,0:T(8,128)(2,1)S(1)}, bf16[80,1024]{1,0:T(8,128)(2,1)}, u32[]{:S(2)}, u32[]{:S(2)}) collective-permute-start(bf16[80,1024]{1,0:T(8,128)(2,1)S(1)} %reshape.82.refs_0_), channel_id=1, source_target_pairs={{0,1},{1,2},{2,3},{3,0},{4,5},{5,6},{6,7},{7,4},{8,9},{9,10},{10,1... | collective-permute-start | bytes 491528 | tf_op jit(solution)/shard_map/ppermute | solution.py:291
  35.0 9.3 %collective-permute-start.2 = (bf16[80,1024]{1,0:T(8,128)(2,1)S(1)}, bf16[80,1024]{1,0:T(8,128)(2,1)}, u32[]{:S(2)}, u32[]{:S(2)}) collective-permute-start(bf16[80,1024]{1,0:T(8,128)(2,1)S(1)} %reshape.82.refs_0_), channel_id=1, source_target_pairs={{0,2},{1,3},{2,0},{3,1},{4,6},{5,7},{6,4},{7,5},{8,10},{9,11},{10,... | collective-permute-start | bytes 491528 | tf_op jit(solution)/shard_map/ppermute | solution.py:291
  36.2 8.8 %collective-permute-start.3 = (bf16[80,1024]{1,0:T(8,128)(2,1)S(1)}, bf16[80,1024]{1,0:T(8,128)(2,1)}, u32[]{:S(2)}, u32[]{:S(2)}) collective-permute-start(bf16[80,1024]{1,0:T(8,128)(2,1)S(1)} %reshape.82.refs_0_), channel_id=1, source_target_pairs={{0,3},{1,0},{2,1},{3,2},{4,7},{5,4},{6,5},{7,6},{8,11},{9,8},{10,9... | collective-permute-start | bytes 491528 | tf_op jit(solution)/shard_map/ppermute | solution.py:291
  45.0 22.4 %all-to-all-start.1 = ((bf16[8,80,256]{2,1,0:T(8,128)(2,1)}), bf16[8,80,256]{2,1,0:T(8,128)(2,1)S(1)}, u32[]{:S(2)}, u32[]{:S(2)}) async-start(bf16[8,80,256]{2,1,0:T(8,128)(2,1)} %reshape.86), calls=%async_computation.1 | async-start | bytes 655360 | tf_op jit(solution)/shard_map/all_to_all | solution.py:298
  52.0 11.8 %collective-permute-start.4 = (bf16[640,256]{1,0:T(8,128)(2,1)S(1)}, bf16[640,256]{1,0:T(8,128)(2,1)S(1)}, u32[]{:S(2)}, u32[]{:S(2)}) collective-permute-start(bf16[640,256]{1,0:T(8,128)(2,1)S(1)} %bitcast.51), channel_id=1, source_target_pairs={{0,1},{1,2},{2,3},{3,0},{4,5},{5,6},{6,7},{7,4},{8,9},{9,10},{10,1... | collective-permute-start | bytes 983048 | tf_op jit(solution)/shard_map/ppermute | solution.py:291
  52.2 15.3 %collective-permute-start.5 = (bf16[640,256]{1,0:T(8,128)(2,1)S(1)}, bf16[640,256]{1,0:T(8,128)(2,1)}, u32[]{:S(2)}, u32[]{:S(2)}) collective-permute-start(bf16[640,256]{1,0:T(8,128)(2,1)S(1)} %bitcast.52), channel_id=1, source_target_pairs={{0,2},{1,3},{2,0},{3,1},{4,6},{5,7},{6,4},{7,5},{8,10},{9,11},{10,... | collective-permute-start | bytes 983048 | tf_op jit(solution)/shard_map/ppermute | solution.py:291
  55.7 11.7 %collective-permute-start.6 = (bf16[640,256]{1,0:T(8,128)(2,1)S(1)}, bf16[640,256]{1,0:T(8,128)(2,1)}, u32[]{:S(2)}, u32[]{:S(2)}) collective-permute-start(bf16[640,256]{1,0:T(8,128)(2,1)S(1)} %bitcast.53), channel_id=1, source_target_pairs={{0,3},{1,0},{2,1},{3,2},{4,7},{5,4},{6,5},{7,6},{8,11},{9,8},{10,9... | collective-permute-start | bytes 983048 | tf_op jit(solution)/shard_map/ppermute | solution.py:291
  63.8 0.7 copy-start.4
  67.4 1.0 copy-start.5
  76.7 0.8 copy-start.3
  77.6 15.7 %collective-permute-start.7 = (bf16[640,256]{1,0:T(8,128)(2,1)}, bf16[640,256]{1,0:T(8,128)(2,1)}, u32[]{:S(2)}, u32[]{:S(2)}) collective-permute-start(bf16[640,256]{1,0:T(8,128)(2,1)} %get-tuple-element.56), channel_id=1, source_target_pairs={{0,3},{1,0},{2,1},{3,2},{4,7},{5,4},{6,5},{7,6},{8,11},{9,8},{10,9... | collective-permute-start | bytes 983048 | tf_op jit(solution)/shard_map/ppermute | solution.py:291
  79.9 13.3 %collective-permute-start.8 = (bf16[640,256]{1,0:T(8,128)(2,1)}, bf16[640,256]{1,0:T(8,128)(2,1)}, u32[]{:S(2)}, u32[]{:S(2)}) collective-permute-start(bf16[640,256]{1,0:T(8,128)(2,1)} %get-tuple-element.57), channel_id=1, source_target_pairs={{0,2},{1,3},{2,0},{3,1},{4,6},{5,7},{6,4},{7,5},{8,10},{9,11},{10,... | collective-permute-start | bytes 983048 | tf_op jit(solution)/shard_map/ppermute | solution.py:291
  79.9 16.7 %collective-permute-start.9 = (bf16[640,256]{1,0:T(8,128)(2,1)}, bf16[640,256]{1,0:T(8,128)(2,1)}, u32[]{:S(2)}, u32[]{:S(2)}) collective-permute-start(bf16[640,256]{1,0:T(8,128)(2,1)} %get-tuple-element.58), channel_id=1, source_target_pairs={{0,1},{1,2},{2,3},{3,0},{4,5},{5,6},{6,7},{7,4},{8,9},{9,10},{10,1... | collective-permute-start | bytes 983048 | tf_op jit(solution)/shard_map/ppermute | solution.py:291
  81.6 18.4 %all-to-all-start.2 = ((bf16[8,80,256]{2,1,0:T(8,128)(2,1)}), bf16[8,80,256]{2,1,0:T(8,128)(2,1)S(1)}, u32[]{:S(2)}, u32[]{:S(2)}) async-start(bf16[8,80,256]{2,1,0:T(8,128)(2,1)} %bitcast.59), calls=%async_computation.2 | async-start | bytes 655360 | tf_op jit(solution)/shard_map/all_to_all | solution.py:298
  99.9 19.3 %all-to-all-start.3 = ((bf16[8,80,256]{2,1,0:T(8,128)(2,1)}), bf16[8,80,256]{2,1,0:T(8,128)(2,1)S(1)}, u32[]{:S(2)}, u32[]{:S(2)}) async-start(bf16[8,80,256]{2,1,0:T(8,128)(2,1)} %bitcast.6), calls=%async_computation.3 | async-start | bytes 655360 | tf_op jit(solution)/shard_map/all_to_all | solution.py:298
  106.1 37.9 %reduce-scatter.2.cloned.1.call-start = ((), (), s32[]{:S(2)}) async-start(), calls=%async_computation.7 | async-start | bytes 1310720 | tf_op jit(solution)/shard_map/reduce_scatter | solution.py:335
  106.2 1.7 copy-start.2
  119.4 2.8 %copy-start.1 = (bf16[1024,3072]{1,0:T(8,128)(2,1)S(1)}, bf16[1024,3072]{1,0:T(8,128)(2,1)}, u32[]{:S(2)}) copy-start(bf16[1024,3072]{1,0:T(8,128)(2,1)} %weight_ref.1) | copy-start | bytes 18874372
  124.3 0.6 copy-start.6
  125.0 6.5 %collective-permute-start.10 = (bf16[80,256]{1,0:T(8,128)(2,1)S(1)}, bf16[80,256]{1,0:T(8,128)(2,1)S(1)}, u32[]{:S(2)}, u32[]{:S(2)}) collective-permute-start(bf16[80,256]{1,0:T(8,128)(2,1)S(1)} %get-tuple-element.64), channel_id=1, source_target_pairs={{0,1},{1,2},{2,3},{3,0},{4,5},{5,6},{6,7},{7,4},{8,9},{9,10},{10,1... | collective-permute-start | bytes 122888 | tf_op jit(solution)/shard_map/ppermute | solution.py:291
  125.0 6.5 %collective-permute-start.11 = (bf16[80,256]{1,0:T(8,128)(2,1)S(1)}, bf16[80,256]{1,0:T(8,128)(2,1)S(1)}, u32[]{:S(2)}, u32[]{:S(2)}) collective-permute-start(bf16[80,256]{1,0:T(8,128)(2,1)S(1)} %get-tuple-element.65), channel_id=1, source_target_pairs={{0,2},{1,3},{2,0},{3,1},{4,6},{5,7},{6,4},{7,5},{8,10},{9,11},{10,... | collective-permute-start | bytes 122888 | tf_op jit(solution)/shard_map/ppermute | solution.py:291
  126.0 6.6 %collective-permute-start.12 = (bf16[80,256]{1,0:T(8,128)(2,1)S(1)}, bf16[80,256]{1,0:T(8,128)(2,1)S(1)}, u32[]{:S(2)}, u32[]{:S(2)}) collective-permute-start(bf16[80,256]{1,0:T(8,128)(2,1)S(1)} %get-tuple-element.66), channel_id=1, source_target_pairs={{0,3},{1,0},{2,1},{3,2},{4,7},{5,4},{6,5},{7,6},{8,11},{9,8},{10,9... | collective-permute-start | bytes 122888 | tf_op jit(solution)/shard_map/ppermute | solution.py:291
  131.5 1.1 copy-start.9
  131.5 1.1 copy-start.10
  132.6 0.6 copy-start.11
  135.7 17.3 %copy-start.8 = (bf16[320,256]{1,0:T(8,128)(2,1)S(1)}, bf16[320,256]{1,0:T(8,128)(2,1)}, u32[]{:S(2)}) copy-start(bf16[320,256]{1,0:T(8,128)(2,1)} %param.5) | copy-start | bytes 491524
  135.7 36.7 %all-to-all-start.4 = ((bf16[32,64,128]{2,1,0:T(8,128)(2,1)}), bf16[32,64,128]{2,1,0:T(8,128)(2,1)}, u32[]{:S(2)}, u32[]{:S(2)}) async-start(bf16[32,64,128]{2,1,0:T(8,128)(2,1)} %short_grads.1), calls=%async_computation.4 | async-start | bytes 1048576 | tf_op jit(solution)/shard_map/all_to_all | solution.py:342
  142.7 16.2 %collective-permute-start.13 = (bf16[3,256]{1,0:T(4,128)(2,1)S(1)}, bf16[3,256]{1,0:T(4,128)(2,1)S(1)}, u32[]{:S(2)}, u32[]{:S(2)}) collective-permute-start(bf16[3,256]{1,0:T(4,128)(2,1)S(1)} %slice.43), channel_id=1, source_target_pairs={{1,0},{2,1},{3,2},{4,3},{5,4},{6,5},{7,6},{8,7},{9,8},{10,9},{11,1... | collective-permute-start | bytes 4616 | tf_op jit(solution)/shard_map/ppermute | solution.py:355
  145.7 16.9 %collective-permute-start.14 = (bf16[32,384]{1,0:T(8,128)(2,1)}, bf16[32,384]{1,0:T(8,128)(2,1)S(1)}, u32[]{:S(2)}, u32[]{:S(2)}) collective-permute-start(bf16[32,384]{1,0:T(8,128)(2,1)} %get-tuple-element.77), channel_id=1, source_target_pairs={{0,4},{4,8},{8,12},{12,16},{16,20},{20,24},{24,28},{28,0},{1,5},{5... | collective-permute-start | bytes 73736 | tf_op jit(solution)/shard_map/ppermute | solution.py:346
  150.6 15.5 %collective-permute-start.15 = (bf16[32,384]{1,0:T(8,128)(2,1)}, bf16[32,384]{1,0:T(8,128)(2,1)S(1)}, u32[]{:S(2)}, u32[]{:S(2)}) collective-permute-start(bf16[32,384]{1,0:T(8,128)(2,1)} %get-tuple-element.78), channel_id=1, source_target_pairs={{0,8},{4,12},{8,16},{12,20},{16,24},{20,28},{24,0},{28,4},{1,9},{5... | collective-permute-start | bytes 73736 | tf_op jit(solution)/shard_map/ppermute | solution.py:346
  153.7 14.5 %collective-permute-start.16 = (bf16[32,384]{1,0:T(8,128)(2,1)}, bf16[32,384]{1,0:T(8,128)(2,1)S(1)}, u32[]{:S(2)}, u32[]{:S(2)}) collective-permute-start(bf16[32,384]{1,0:T(8,128)(2,1)} %get-tuple-element.79), channel_id=1, source_target_pairs={{0,12},{4,16},{8,20},{12,24},{16,28},{20,0},{24,4},{28,8},{1,13},{... | collective-permute-start | bytes 73736 | tf_op jit(solution)/shard_map/ppermute | solution.py:346
  157.5 10.8 %collective-permute-start.17 = (bf16[32,384]{1,0:T(8,128)(2,1)}, bf16[32,384]{1,0:T(8,128)(2,1)S(1)}, u32[]{:S(2)}, u32[]{:S(2)}) collective-permute-start(bf16[32,384]{1,0:T(8,128)(2,1)} %get-tuple-element.80), channel_id=1, source_target_pairs={{0,16},{4,20},{8,24},{12,28},{16,0},{20,4},{24,8},{28,12},{1,17},{... | collective-permute-start | bytes 73736 | tf_op jit(solution)/shard_map/ppermute | solution.py:346
  158.8 9.4 %collective-permute-start.18 = (bf16[32,384]{1,0:T(8,128)(2,1)}, bf16[32,384]{1,0:T(8,128)(2,1)S(1)}, u32[]{:S(2)}, u32[]{:S(2)}) collective-permute-start(bf16[32,384]{1,0:T(8,128)(2,1)} %get-tuple-element.81), channel_id=1, source_target_pairs={{0,20},{4,24},{8,28},{12,0},{16,4},{20,8},{24,12},{28,16},{1,21},{... | collective-permute-start | bytes 73736 | tf_op jit(solution)/shard_map/ppermute | solution.py:346
  162.5 7.6 %copy-start.12 = (bf16[32,384]{1,0:T(8,128)(2,1)}, bf16[32,384]{1,0:T(8,128)(2,1)S(1)}, u32[]{:S(2)}) copy-start(bf16[32,384]{1,0:T(8,128)(2,1)S(1)} %collective-permute-done.14.refs_1_) | copy-start | bytes 73732
  162.5 5.7 %collective-permute-start.19 = (bf16[32,384]{1,0:T(8,128)(2,1)}, bf16[32,384]{1,0:T(8,128)(2,1)S(1)}, u32[]{:S(2)}, u32[]{:S(2)}) collective-permute-start(bf16[32,384]{1,0:T(8,128)(2,1)} %get-tuple-element.82), channel_id=1, source_target_pairs={{0,24},{4,28},{8,0},{12,4},{16,8},{20,12},{24,16},{28,20},{1,25},{... | collective-permute-start | bytes 73736 | tf_op jit(solution)/shard_map/ppermute | solution.py:346
  166.1 4.0 %copy-start.13 = (bf16[32,384]{1,0:T(8,128)(2,1)}, bf16[32,384]{1,0:T(8,128)(2,1)S(1)}, u32[]{:S(2)}) copy-start(bf16[32,384]{1,0:T(8,128)(2,1)S(1)} %collective-permute-done.15.refs_2_) | copy-start | bytes 73732
  166.1 4.0 %collective-permute-start.20 = (bf16[32,384]{1,0:T(8,128)(2,1)}, bf16[32,384]{1,0:T(8,128)(2,1)S(1)}, u32[]{:S(2)}, u32[]{:S(2)}) collective-permute-start(bf16[32,384]{1,0:T(8,128)(2,1)} %get-tuple-element.83), channel_id=1, source_target_pairs={{0,28},{4,0},{8,4},{12,8},{16,12},{20,16},{24,20},{28,24},{1,29},{... | collective-permute-start | bytes 73736 | tf_op jit(solution)/shard_map/ppermute | solution.py:346
  168.2 1.9 %copy-start.14 = (bf16[32,384]{1,0:T(8,128)(2,1)}, bf16[32,384]{1,0:T(8,128)(2,1)S(1)}, u32[]{:S(2)}) copy-start(bf16[32,384]{1,0:T(8,128)(2,1)S(1)} %collective-permute-done.16.refs_3_) | copy-start | bytes 73732
  168.2 1.9 %copy-start.15 = (bf16[32,384]{1,0:T(8,128)(2,1)}, bf16[32,384]{1,0:T(8,128)(2,1)S(1)}, u32[]{:S(2)}) copy-start(bf16[32,384]{1,0:T(8,128)(2,1)S(1)} %collective-permute-done.17.refs_4_) | copy-start | bytes 73732
  168.3 1.9 %copy-start.16 = (bf16[32,384]{1,0:T(8,128)(2,1)}, bf16[32,384]{1,0:T(8,128)(2,1)S(1)}, u32[]{:S(2)}) copy-start(bf16[32,384]{1,0:T(8,128)(2,1)S(1)} %collective-permute-done.18.refs_5_) | copy-start | bytes 73732
  168.3 1.9 %copy-start.17 = (bf16[32,384]{1,0:T(8,128)(2,1)}, bf16[32,384]{1,0:T(8,128)(2,1)S(1)}, u32[]{:S(2)}) copy-start(bf16[32,384]{1,0:T(8,128)(2,1)S(1)} %collective-permute-done.19.refs_6_) | copy-start | bytes 73732
  170.1 0.6 copy-start.18
Sparse Core Ops, SparseCore 0:
  45.1 43.6 all-gather.1
  119.4 20.8 reduce-scatter.1
